TPU v7x, 256 devices: a whole 4x4x8 slice. The times are simulated.
256 devices in a mesh: grp: 4 (over x), gx: 16 (over y_hi, z), gy: 4 (over y_lo, core).
Axes of the slice: x: 4, y: 4 (y_hi: 2, y_lo: 2; y = y_hi * 2 + y_lo), z: 8, core: 2. Of those that a mesh axis runs over, the one named last changes fastest.
Arguments:
- coarse_modes: float32 [4, 2, 8, 64, 4096], P('grp', None, None, 'gy', 'gx'), may hold values from -6 to 6
- salinity: float32 [32, 256, 16384], P('grp', 'gy', 'gx'), may hold values from -6 to 6
- viscosity: float32 [4], P('grp'), may hold values from 0.1 to 1
- forcing_gain: float32 [4], P('grp'), may hold values from 0.5 to 2
- diffusivity: float32 [32], P('grp'), may hold values from 0.3 to 1.5
Outputs:
- salinity_next: float32 [32, 256, 16384], P('grp', 'gy', 'gx')
- coarse_next: float32 [4, 2, 8, 64, 4096], P('grp', None, None, 'gy', 'gx')
All inputs are finite; a program needn't handle non-finite values.
Results may differ from a plain program's by a relative error of at most 0.0003.
Values sent between devices are 32-bit elements; how exact they have to be, the bound alone decides.
No kernel may reach another device: no remote copies, remote signals or barrier semaphores. Data moves between devices by JAX's collectives and lax.ppermute only.
A program may use at most 128 MiB of HBM per device.

v0:
```python
import math

import jax
import jax.numpy as jnp
from jax import lax
from jax.sharding import Mesh
from jax.sharding import PartitionSpec as P

RATIO = 4
GX = ("gx_0", "gx_1")
GRP_GX = ("grp", "gx_0", "gx_1")


fine_step = 0.1


def cut_along(array, dim, length):
    before, after = (array.shape[:dim], array.shape[dim + 1 :])
    return jnp.moveaxis(array.reshape(*before, length, -1, *after), dim, 0)


def joined_along(parts, dim):
    parts = jnp.moveaxis(parts, 0, dim)
    lengths = parts.shape
    return parts.reshape(*lengths[:dim], lengths[dim] * lengths[dim + 1], *lengths[dim + 2 :])


def joined_exchange(array, axis, axes, splits, concats):
    sizes = [lax.axis_size(a) for a in axes]
    parts = cut_along(array, splits[0], sizes[0])
    parts = jnp.moveaxis(cut_along(parts, splits[1] + 1, sizes[1]), 0, 1)
    inside = parts.shape[2:]
    parts = parts.reshape(-1, *inside)
    parts = lax.all_to_all(parts, axis, split_axis=0, concat_axis=0, tiled=True)
    parts = joined_along(parts.reshape(*sizes, *inside), concats[0] + 1)
    return joined_along(parts, concats[1])


def extended(cells, sides, width):
    for axis, dim in sides:
        count = lax.axis_size(axis)
        head = lax.slice_in_dim(cells, 0, width, axis=dim)
        tail = lax.slice_in_dim(cells, cells.shape[dim] - width, cells.shape[dim], axis=dim)
        cells = jnp.concatenate(
            [
                lax.ppermute(tail, axis, [(i, (i + 1) % count) for i in range(count)]),
                cells,
                lax.ppermute(head, axis, [((i + 1) % count, i) for i in range(count)]),
            ],
            axis=dim,
        )
    return cells


def with_halo(array, sides, width):
    edges = {}
    for axis, dim in sides:
        size, length = (lax.axis_size(axis), array.shape[dim])
        up = [(i, (i + 1) % size) for i in range(size)]
        last = lax.slice_in_dim(array, length - width, length, axis=dim)
        first = lax.slice_in_dim(array, 0, width, axis=dim)
        edges[dim] = (
            lax.ppermute(last, axis, up),
            lax.ppermute(first, axis, [(b, a) for a, b in up]),
        )
    done = []
    for _, dim in sides:
        low, high = edges[dim]
        around = [(width, width) if d in done else (0, 0) for d in range(array.ndim)]
        array = jnp.concatenate([jnp.pad(low, around), array, jnp.pad(high, around)], axis=dim)
        done.append(dim)
    return array


def exchange_in_order(parts, axes, sequence):
    inside = parts.shape[1:]
    filled = parts.reshape(*(lax.axis_size(a) for a in axes), *inside)
    for k in sequence:
        filled = lax.all_to_all(filled, axes[k], k, k, tiled=True)
    return filled.reshape(-1, *inside)


def stepwise_exchange(array, axes, sequence, split_dim, concat_dim):
    parts = cut_along(array, split_dim, lax.axis_size(axes))
    return joined_along(exchange_in_order(parts, axes, sequence), concat_dim)


def sent_to_all(array, axis):
    length = lax.axis_size(axis)
    return lax.all_to_all(
        jnp.broadcast_to(array[None], (length, *array.shape)), axis, 0, 0, tiled=True
    )


def gather_directly(array, axis, dim):
    parts = sent_to_all(array, axis)
    return joined_along(parts, dim)


def circle_table(row_count, col_count, period, orient):
    product = (
        lax.broadcasted_iota(jnp.int32, (row_count, col_count), 0)
        * lax.broadcasted_iota(jnp.int32, (row_count, col_count), 1)
        % period
    )
    angle = 2.0 * math.pi / period * product.astype(jnp.float32)
    return (jnp.cos(angle), orient * jnp.sin(angle))


def contract(data, table, form):
    return jnp.einsum(form, data, table, precision=lax.Precision.HIGHEST)


def fourier_lines(real_part, imag_part, orient, want_imag):
    length = real_part.shape[-1]
    exponent = length.bit_length() - 1
    inner_count = 2 ** ((exponent + 2) // 2)
    outer_count = length // inner_count
    leading = real_part.shape[:-1]
    cos_outer, sin_outer = circle_table(outer_count, outer_count, outer_count, orient)
    cos_twist, sin_twist = circle_table(outer_count, inner_count, length, orient)
    cos_inner, sin_inner = circle_table(inner_count, inner_count, inner_count, orient)
    first_form = "...ba,bk->...ka"
    second_form = "...ka,aj->...jk"
    split_real = real_part.reshape(leading + (outer_count, inner_count))
    section_real = contract(split_real, cos_outer, first_form)
    section_imag = contract(split_real, sin_outer, first_form)
    if imag_part is not None:
        split_imag = imag_part.reshape(leading + (outer_count, inner_count))
        section_real = section_real - contract(split_imag, sin_outer, first_form)
        section_imag = section_imag + contract(split_imag, cos_outer, first_form)
    twist_real = section_real * cos_twist - section_imag * sin_twist
    twist_imag = section_real * sin_twist + section_imag * cos_twist
    norm_factor = length ** (-0.5)
    final_real = (
        contract(twist_real, cos_inner, second_form) - contract(twist_imag, sin_inner, second_form)
    ) * norm_factor
    if not want_imag:
        return final_real.reshape(leading + (length,))
    final_imag = (
        contract(twist_real, sin_inner, second_form) + contract(twist_imag, cos_inner, second_form)
    ) * norm_factor
    return (final_real.reshape(leading + (length,)), final_imag.reshape(leading + (length,)))


def refine_rows(padded, dimension):
    extent = padded.shape[dimension] - 2
    middle = lax.slice_in_dim(padded, 1, extent + 1, axis=dimension)
    previous = lax.slice_in_dim(padded, 0, extent, axis=dimension)
    following = lax.slice_in_dim(padded, 2, extent + 2, axis=dimension)
    pieces = []
    for sub_cell in range(RATIO):
        offset = (sub_cell + 0.5) / RATIO - 0.5
        beside = following if offset > 0 else previous
        pieces.append((1.0 - abs(offset)) * middle + abs(offset) * beside)
    stacked = jnp.stack(pieces, axis=dimension + 1)
    target = list(middle.shape)
    target[dimension] = extent * RATIO
    return stacked.reshape(target)


def spread_table(cell_count):
    fine_count = cell_count * RATIO
    source = lax.broadcasted_iota(jnp.int32, (cell_count + 2, fine_count), 0)
    fine_cell = lax.broadcasted_iota(jnp.int32, (cell_count + 2, fine_count), 1)
    parent = fine_cell // RATIO
    sub_cell = (fine_cell % RATIO).astype(jnp.float32)
    offset = (sub_cell + 0.5) / RATIO - 0.5
    magnitude = jnp.abs(offset)
    own_weight = jnp.where(source == parent + 1, 1.0 - magnitude, 0.0)
    after_weight = jnp.where((source == parent + 2) & (offset > 0), magnitude, 0.0)
    before_weight = jnp.where((source == parent) & (offset < 0), magnitude, 0.0)
    return own_weight + after_weight + before_weight


def average_table(fine_count):
    fine_cell = lax.broadcasted_iota(jnp.int32, (fine_count, fine_count // RATIO), 0)
    coarse_cell = lax.broadcasted_iota(jnp.int32, (fine_count, fine_count // RATIO), 1)
    return jnp.where(fine_cell // RATIO == coarse_cell, 1.0 / RATIO, 0.0).astype(jnp.float32)


def per_device(coarse_modes, salinity, viscosity, forcing_gain, diffusivity):
    planes = coarse_modes.shape[2]
    row_count = coarse_modes.shape[3]
    width = coarse_modes.shape[4]
    groups = lax.axis_size("grp")
    quarter = planes // groups
    pencil = lax.all_to_all(coarse_modes[0], GX, split_axis=2, concat_axis=3, tiled=True)
    physical = fourier_lines(pencil[0], pencil[1], 1.0, False)
    sliced = physical.reshape((groups, quarter) + physical.shape[1:])
    received = joined_exchange(sliced, GRP_GX, ("grp", GX), (0, 3), (0, 2))
    rimmed = extended(received, ((GX, 3), ("gy", 2)), 1)
    along_y = refine_rows(rimmed, 2)
    velocity = jnp.einsum(
        "fqyj,jx->fqyx", along_y, spread_table(width), precision=lax.Precision.HIGHEST
    )[:, :, None]
    padded = with_halo(salinity, (("grp", 0), (GX, 2), ("gy", 1)), 1)

    def levels(piece):
        return piece.reshape((quarter, RATIO) + piece.shape[1:])

    centre = levels(padded[1:-1, 1:-1, 1:-1])
    east_cells = levels(padded[1:-1, 1:-1, 2:])
    west_cells = levels(padded[1:-1, 1:-1, :-2])
    north_cells = levels(padded[1:-1, 2:, 1:-1])
    south_cells = levels(padded[1:-1, :-2, 1:-1])
    upper_cells = levels(padded[2:, 1:-1, 1:-1])
    lower_cells = levels(padded[:-2, 1:-1, 1:-1])
    diffuse_rate = diffusivity.reshape(quarter, RATIO, 1, 1)
    spread = diffuse_rate * (
        east_cells
        + west_cells
        + north_cells
        + south_cells
        + upper_cells
        + lower_cells
        - 6.0 * centre
    )
    advection = (
        velocity[0] * (east_cells - west_cells) * 0.5
        + velocity[1] * (north_cells - south_cells) * 0.5
        + velocity[2] * (upper_cells - lower_cells) * 0.5
    )
    updated = centre + fine_step * (spread - advection)
    buoyancy = velocity[3] - updated
    partial_mean = buoyancy.reshape(quarter, RATIO, row_count, RATIO, width * RATIO).mean(
        axis=(1, 3)
    )
    restricted = jnp.einsum(
        "qyx,xc->qyc", partial_mean, average_table(width * RATIO), precision=lax.Precision.HIGHEST
    )
    salinity_next = updated.reshape(salinity.shape)
    columns = lax.all_to_all(restricted, GX, split_axis=1, concat_axis=2, tiled=True)
    spec_real, spec_imag = fourier_lines(columns, None, -1.0, True)
    own_spectra = stepwise_exchange(jnp.stack([spec_real, spec_imag]), GX, (0, 1), 3, 2)
    spectrum = gather_directly(own_spectra, "grp", 1)
    total_modes = width * lax.axis_size(GX)
    mode_index = lax.axis_index(GX) * width + lax.broadcasted_iota(jnp.int32, (width,), 0)
    wavenumber = jnp.where(mode_index < total_modes // 2, mode_index, mode_index - total_modes)
    scaled_wave = 2.0 * math.pi / total_modes * wavenumber.astype(jnp.float32)
    damping = jnp.exp(-viscosity[0] * scaled_wave * scaled_wave)
    coarse_next = damping * coarse_modes + forcing_gain[0] * spectrum[None]
    return (salinity_next, coarse_next)


def solution(mesh):
    finer = Mesh(
        mesh.devices.reshape(mesh.shape["grp"], 2, 8, mesh.shape["gy"]),
        ("grp", "gx_0", "gx_1", "gy"),
    )
    in_specs = (P("grp", None, None, "gy", GX), P("grp", "gy", GX), P("grp"), P("grp"), P("grp"))
    out_specs = (P("grp", "gy", GX), P("grp", None, None, "gy", GX))
    return jax.shard_map(
        per_device, mesh=finer, in_specs=in_specs, out_specs=out_specs, check_vma=False
    )
```

profile of v0, /device:TPU:32, one launch (start us, length us, event | category | flops | bytes accessed | tf_op | source)
XLA Modules:
  0.0 168.3 jit_solution(12407453693399749987)
XLA Ops:
  0.6 2.0 %copy.49 = f32[1,2,8,16,256]{4,2,1,3,0:T(8,128)} copy(f32[1,2,8,16,256]{4,3,2,1,0:T(8,128)} %param.5) | data formatting | bytes 524288 | tf_op args[0]
  2.6 11.2 %all-to-all-start = ((f32[2,8,16,256]{3,1,0,2:T(8,128)}), f32[2,8,16,256]{3,1,0,2:T(8,128)S(1)}, u32[]{:S(2)}, u32[]{:S(2)}) async-start(f32[2,8,16,256]{3,1,0,2:T(8,128)} %bitcast.177), calls=%async_computation | async-start | bytes 524288 | tf_op jit(solution)/shard_map/all_to_all | solution.py:188
  15.7 2.8 %collective-permute-start.1 = (f32[1,64,1024]{2,1,0:T(8,128)}, f32[1,64,1024]{2,1,0:T(8,128)S(1)}, u32[]{:S(2)}, u32[]{:S(2)}) collective-permute-start(f32[1,64,1024]{2,1,0:T(8,128)} %get-tuple-element.22), channel_id=1, source_target_pairs={{64,0},{128,64},{192,128},{0,192},{65,1},{129,65},{193,129},{1,193... | collective-permute-start | bytes 786440 | tf_op jit(solution)/shard_map/ppermute | solution.py:64
  19.4 1.9 %collective-permute-start.3 = (f32[8,64,1]{2,1,0:T(8,128)}, f32[8,64,1]{2,1,0:T(8,128)}, u32[]{:S(2)}, u32[]{:S(2)}) collective-permute-start(f32[8,64,1]{2,1,0:T(8,128)} %get-tuple-element.20), channel_id=1, source_target_pairs={{0,4},{4,8},{8,12},{12,16},{16,20},{20,24},{24,28},{28,32},{32,36}... | collective-permute-start | bytes 6152 | tf_op jit(solution)/shard_map/ppermute | solution.py:63
  22.7 2.7 %all-to-all-done = f32[2,8,16,256]{3,1,0,2:T(8,128)S(1)} async-done(((f32[2,8,16,256]{3,1,0,2:T(8,128)}), f32[2,8,16,256]{3,1,0,2:T(8,128)S(1)}, u32[]{:S(2)}, u32[]{:S(2)}) %all-to-all-start) | async-done | bytes 262176 | tf_op jit(solution)/shard_map/all_to_all | solution.py:188
  29.2 11.1 %all-to-all-start.1 = ((f32[64,1,2,1,256]{4,2,3,1,0:T(2,128)}), f32[64,1,2,1,256]{4,2,3,1,0:T(2,128)S(1)}, u32[]{:S(2)}, u32[]{:S(2)}) async-start(f32[64,1,2,1,256]{4,2,3,1,0:T(2,128)} %copy.34), calls=%async_computation.1 | async-start | bytes 262144 | tf_op jit(solution)/shard_map/all_to_all | solution.py:34
  46.5 6.4 %all-to-all-done.1 = f32[64,1,2,1,256]{4,2,3,1,0:T(2,128)S(1)} async-done(((f32[64,1,2,1,256]{4,2,3,1,0:T(2,128)}), f32[64,1,2,1,256]{4,2,3,1,0:T(2,128)S(1)}, u32[]{:S(2)}, u32[]{:S(2)}) %all-to-all-start.1) | async-done | bytes 131104 | tf_op jit(solution)/shard_map/all_to_all | solution.py:34
  55.1 2.7 %pad_maximum_fusion.1 = (f32[8,64,1024]{2,1,0:T(8,128)}, f32[10,64,1024]{2,1,0:T(8,128)}) fusion(f32[1,64,1024]{2,1,0:T(8,128)S(1)} %collective-permute-done.1, f32[8,64,1024]{2,1,0:T(8,128)S(1)} %copy-done, f32[10,64,1024]{2,1,0:T(8,128)} %constant_dynamic-update-slice_fusion.2), kind=kLoop, calls=%fused_computation.4 | loop fusion | flops 524288 | bytes 6553600 | tf_op jit(solution)/shard_map/concatenate | solution.py:70
  59.1 2.9 %reshape.237 = f32[2,4,16,4,1024]{4,3,2,1,0:T(4,128)} reshape(f32[8,64,1024]{2,1,0:T(8,128)} %get-tuple-element.15) | data formatting | bytes 4194304 | tf_op jit(solution)/shard_map/reshape | solution.py:200
  62.0 4.5 %concatenate.39 = f32[10,64,1026]{2,1,0:T(8,128)} concatenate(f32[10,64,1]{2,1,0:T(8,128)S(1)} %pad.15, f32[10,64,1024]{2,1,0:T(8,128)} %constant_dynamic-update-slice_fusion, f32[10,64,1]{2,1,0:T(8,128)S(1)} %pad.14), dimensions={2} | concatenate | bytes 5253120 | tf_op jit(solution)/shard_map/concatenate | solution.py:70
  72.5 5.0 %fusion.16 = f32[4,2,64,1024]{3,2,1,0:T(8,128)S(1)} fusion(f32[4,2,64,258]{3,2,1,0:T(8,128)} %reshape.233, s32[1024]{0:T(1024)} %get-tuple-element.36, s32[1024]{0:T(1024)} %get-tuple-element.37, s32[1024]{0:T(1024)} %get-tuple-element.35, s32[1024]{0:T(1024)} %get-tuple-element.38, pred[1024]{0:T(1024)(128)(4,1)} %get-tuple-element.39, ...), kind=kOutput, calls=%fused_computation.42 | convolution fusion | flops 1629007872 | bytes 2643968 | tf_op jit(solution)/shard_map/fqyj,jx->fqyx/dot_general | solution.py:194
  81.0 7.6 %fusion.4 = (f32[8,64,1024]{2,1,0:T(8,128)}, f32[8,64,1024]{2,1,0:T(8,128)}, f32[8,64,1024]{2,1,0:T(8,128)}, f32[8,64,1024]{2,1,0:T(8,128)}, f32[8,64,1024]{2,1,0:T(8,128)}, /*index=5*/f32[8,64,1024]{2,1,0:T(8,128)}) fusion(f32[8,64,1024]{2,1,0:T(8,128)S(1)} %copy-done, f32[2,64,1024]{2,1,0:T(8,128)S(1)} %get-tuple-element.11, ...), kind=kLoop, calls=%fused_computation.18 | loop fusion | flops 16777216 | bytes 22095904 | tf_op jit(solution)/shard_map/add | solution.py:224
  88.6 2.9 %add.252 = f32[2,4,16,4,1024]{4,3,2,1,0:T(4,128)} reshape(f32[8,64,1024]{2,1,0:T(8,128)} %get-tuple-element.3) | data formatting | bytes 4194304 | tf_op jit(solution)/shard_map/add | solution.py:211
  91.5 3.0 %reshape.235 = f32[2,4,16,4,1024]{4,3,2,1,0:T(4,128)} reshape(f32[8,64,1024]{2,1,0:T(8,128)} %get-tuple-element.5) | data formatting | bytes 4194304 | tf_op jit(solution)/shard_map/reshape | solution.py:200
  96.1 3.1 %reshape.238 = f32[2,4,16,4,1024]{4,3,2,1,0:T(4,128)} reshape(f32[8,64,1024]{2,1,0:T(8,128)} %get-tuple-element.7) | data formatting | bytes 4194304 | tf_op jit(solution)/shard_map/reshape | solution.py:200
  102.3 2.0 %mul.497 = f32[2,16,4,1024]{3,2,1,0:T(4,128)} reshape(f32[1,2,64,1024]{3,2,1,0:T(8,128)} %get-tuple-element.12) | data formatting | bytes 1048576 | tf_op jit(solution)/shard_map/mul | solution.py:222
  104.3 2.0 %sub.121 = f32[2,16,4,1024]{3,2,1,0:T(4,128)} reshape(f32[1,2,64,1024]{3,2,1,0:T(8,128)} %get-tuple-element.8) | data formatting | bytes 1048576 | tf_op jit(solution)/shard_map/sub | solution.py:225
  106.3 7.6 %subtract_reduce_fusion = f32[2,16,1024]{2,1,0:T(8,128)S(1)} fusion(f32[2,4,16,4,1024]{4,3,2,1,0:T(4,128)S(1)} %copy-done.3, f32[2,4,16,4,1024]{4,3,2,1,0:T(4,128)} %reshape.237, f32[2,4,16,4,1024]{4,3,2,1,0:T(4,128)} %reshape.238, f32[2,4,16,4,1024]{4,3,2,1,0:T(4,128)} %reshape.235, f32[2,4,16,4,1024]{4,3,2,1,0:T(4,128)} %reshape.236, ...), kind=kLoop, calls=%fused_computation.22 | loop fusion | flops 10452992 | bytes 16908320 | tf_op jit(solution)/shard_map/reduce_sum | solution.py:226
  115.5 11.1 %all-to-all-start.2 = ((f32[2,16,256]{2,0,1:T(2,128)}), f32[2,16,256]{2,0,1:T(2,128)S(1)}, u32[]{:S(2)}, u32[]{:S(2)}) async-start(f32[2,16,256]{2,0,1:T(2,128)} %copy.37), calls=%async_computation.2 | async-start | bytes 65536 | tf_op jit(solution)/shard_map/all_to_all | solution.py:233
  126.6 8.7 %all-to-all-done.2 = f32[2,16,256]{2,0,1:T(2,128)S(1)} async-done(((f32[2,16,256]{2,0,1:T(2,128)}), f32[2,16,256]{2,0,1:T(2,128)S(1)}, u32[]{:S(2)}, u32[]{:S(2)}) %all-to-all-start.2) | async-done | bytes 32800 | tf_op jit(solution)/shard_map/all_to_all | solution.py:233
  138.0 8.0 %all_to_all.38 = f32[2,8,2,2,1,256]{5,1,3,2,4,0:T(8,128)S(1)} all-to-all(f32[2,8,2,2,1,256]{5,1,3,2,4,0:T(8,128)S(1)} %copy.41), channel_id=1, replica_groups=mesh['grp'=4,'gx_0'=2,'gx_1'=8,'gy'=4] {'gx_0'}, dimensions={0} | all-to-all | bytes 131072 | tf_op jit(solution)/shard_map/all_to_all | solution.py:79
  146.1 10.6 %all_to_all.39 = f32[2,8,2,2,1,256]{5,0,3,2,4,1:T(2,128)S(1)} all-to-all(f32[2,8,2,2,1,256]{5,0,3,2,4,1:T(2,128)S(1)} %copy.42), channel_id=1, replica_groups=mesh['grp'=4,'gx_0'=2,'gx_1'=8,'gy'=4] {'gx_1'}, dimensions={1} | all-to-all | bytes 131072 | tf_op jit(solution)/shard_map/all_to_all | solution.py:79
  157.5 3.4 %all-to-all-start.5 = ((f32[4,2,2,16,256]{4,3,2,1,0:T(8,128)}), f32[4,2,2,16,256]{4,3,2,1,0:T(8,128)S(1)}, u32[]{:S(2)}, u32[]{:S(2)}) async-start(f32[4,2,2,16,256]{4,3,2,1,0:T(8,128)} %broadcast_in_dim.35), calls=%async_computation.5 | async-start | bytes 524288 | tf_op jit(solution)/shard_map/all_to_all | solution.py:90
  162.2 5.3 %all-to-all-done.5 = f32[4,2,2,16,256]{4,3,2,1,0:T(8,128)S(1)} async-done(((f32[4,2,2,16,256]{4,3,2,1,0:T(8,128)}), f32[4,2,2,16,256]{4,3,2,1,0:T(8,128)S(1)}, u32[]{:S(2)}, u32[]{:S(2)}) %all-to-all-start.5) | async-done | bytes 262176 | tf_op jit(solution)/shard_map/all_to_all | solution.py:90
  (117 shorter events, 37.5 us)
Async XLA Ops:
  0.6 17.8 %copy-start = (f32[8,64,1024]{2,1,0:T(8,128)S(1)}, f32[8,64,1024]{2,1,0:T(8,128)}, u32[]{:S(2)}) copy-start(f32[8,64,1024]{2,1,0:T(8,128)} %param.6) | copy-start | bytes 6291460
  2.6 22.8 %all-to-all-start = ((f32[2,8,16,256]{3,1,0,2:T(8,128)}), f32[2,8,16,256]{3,1,0,2:T(8,128)S(1)}, u32[]{:S(2)}, u32[]{:S(2)}) async-start(f32[2,8,16,256]{3,1,0,2:T(8,128)} %bitcast.177), calls=%async_computation | async-start | bytes 524288 | tf_op jit(solution)/shard_map/all_to_all | solution.py:188
  15.7 39.4 %collective-permute-start.1 = (f32[1,64,1024]{2,1,0:T(8,128)}, f32[1,64,1024]{2,1,0:T(8,128)S(1)}, u32[]{:S(2)}, u32[]{:S(2)}) collective-permute-start(f32[1,64,1024]{2,1,0:T(8,128)} %get-tuple-element.22), channel_id=1, source_target_pairs={{64,0},{128,64},{192,128},{0,192},{65,1},{129,65},{193,129},{1,193... | collective-permute-start | bytes 786440 | tf_op jit(solution)/shard_map/ppermute | solution.py:64
  18.4 26.4 %collective-permute-start = (f32[1,64,1024]{2,1,0:T(8,128)}, f32[1,64,1024]{2,1,0:T(8,128)}, u32[]{:S(2)}, u32[]{:S(2)}) collective-permute-start(f32[1,64,1024]{2,1,0:T(8,128)} %get-tuple-element.21), channel_id=1, source_target_pairs={{0,64},{64,128},{128,192},{192,0},{1,65},{65,129},{129,193},{193,1... | collective-permute-start | bytes 786440 | tf_op jit(solution)/shard_map/ppermute | solution.py:63
  19.3 24.5 %collective-permute-start.2 = (f32[8,64,1]{2,1,0:T(8,128)}, f32[8,64,1]{2,1,0:T(8,128)S(1)}, u32[]{:S(2)}, u32[]{:S(2)}) collective-permute-start(f32[8,64,1]{2,1,0:T(8,128)} %get-tuple-element.19), channel_id=1, source_target_pairs={{4,0},{8,4},{12,8},{16,12},{20,16},{24,20},{28,24},{32,28},{36,32}... | collective-permute-start | bytes 6152 | tf_op jit(solution)/shard_map/ppermute | solution.py:64
  19.4 24.4 %collective-permute-start.3 = (f32[8,64,1]{2,1,0:T(8,128)}, f32[8,64,1]{2,1,0:T(8,128)}, u32[]{:S(2)}, u32[]{:S(2)}) collective-permute-start(f32[8,64,1]{2,1,0:T(8,128)} %get-tuple-element.20), channel_id=1, source_target_pairs={{0,4},{4,8},{8,12},{12,16},{16,20},{20,24},{24,28},{28,32},{32,36}... | collective-permute-start | bytes 6152 | tf_op jit(solution)/shard_map/ppermute | solution.py:63
  22.0 57.2 %collective-permute-start.4 = (f32[8,1,1024]{2,1,0:T(1,128)}, f32[8,1,1024]{2,1,0:T(1,128)}, u32[]{:S(2)}, u32[]{:S(2)}) collective-permute-start(f32[8,1,1024]{2,1,0:T(1,128)} %get-tuple-element.17), channel_id=1, source_target_pairs={{1,0},{2,1},{3,2},{0,3},{5,4},{6,5},{7,6},{4,7},{9,8},{10,9},{11,1... | collective-permute-start | bytes 98312 | tf_op jit(solution)/shard_map/ppermute | solution.py:64
  29.2 23.7 %all-to-all-start.1 = ((f32[64,1,2,1,256]{4,2,3,1,0:T(2,128)}), f32[64,1,2,1,256]{4,2,3,1,0:T(2,128)S(1)}, u32[]{:S(2)}, u32[]{:S(2)}) async-start(f32[64,1,2,1,256]{4,2,3,1,0:T(2,128)} %copy.34), calls=%async_computation.1 | async-start | bytes 262144 | tf_op jit(solution)/shard_map/all_to_all | solution.py:34
  43.8 35.4 %collective-permute-start.5 = (f32[8,1,1024]{2,1,0:T(1,128)}, f32[8,1,1024]{2,1,0:T(1,128)}, u32[]{:S(2)}, u32[]{:S(2)}) collective-permute-start(f32[8,1,1024]{2,1,0:T(1,128)} %get-tuple-element.18), channel_id=1, source_target_pairs={{0,1},{1,2},{2,3},{3,0},{4,5},{5,6},{6,7},{7,4},{8,9},{9,10},{10,1... | collective-permute-start | bytes 98312 | tf_op jit(solution)/shard_map/ppermute | solution.py:63
  53.0 4.8 %collective-permute-start.6 = (f32[4,2,16,1]{3,2,0,1:T(8,128)S(1)}, f32[4,2,16,1]{3,2,0,1:T(8,128)S(1)}, u32[]{:S(2)}, u32[]{:S(2)}) collective-permute-start(f32[4,2,16,1]{3,2,0,1:T(8,128)S(1)} %get-tuple-element.31), channel_id=1, source_target_pairs={{0,4},{4,8},{8,12},{12,16},{16,20},{20,24},{24,28},{28,32},{32,36}... | collective-permute-start | bytes 1544 | tf_op jit(solution)/shard_map/ppermute | solution.py:46
  53.7 4.3 %collective-permute-start.7 = (f32[4,2,16,1]{3,2,0,1:T(8,128)S(1)}, f32[4,2,16,1]{3,2,0,1:T(8,128)S(1)}, u32[]{:S(2)}, u32[]{:S(2)}) collective-permute-start(f32[4,2,16,1]{3,2,0,1:T(8,128)S(1)} %get-tuple-element.32), channel_id=1, source_target_pairs={{4,0},{8,4},{12,8},{16,12},{20,16},{24,20},{28,24},{32,28},{36,32}... | collective-permute-start | bytes 1544 | tf_op jit(solution)/shard_map/ppermute | solution.py:48
  57.9 10.3 %copy-start.10 = (f32[4,2,16,1]{3,2,0,1:T(8,128)}, f32[4,2,16,1]{3,2,0,1:T(8,128)S(1)}, u32[]{:S(2)}) copy-start(f32[4,2,16,1]{3,2,0,1:T(8,128)S(1)} %collective-permute-done.7) | copy-start | bytes 1540
  58.1 10.1 %collective-permute-start.8 = (f32[4,2,1,258]{3,2,0,1:T(1,128)S(1)}, f32[4,2,1,258]{3,2,0,1:T(1,128)S(1)}, u32[]{:S(2)}, u32[]{:S(2)}) collective-permute-start(f32[4,2,1,258]{3,2,0,1:T(1,128)S(1)} %get-tuple-element.29), channel_id=1, source_target_pairs={{0,1},{1,2},{2,3},{3,0},{4,5},{5,6},{6,7},{7,4},{8,9},{9,10},{10,1... | collective-permute-start | bytes 24776 | tf_op jit(solution)/shard_map/ppermute | solution.py:46
  66.5 3.1 %collective-permute-start.9 = (f32[4,2,1,258]{3,2,0,1:T(1,128)S(1)}, f32[4,2,1,258]{3,2,0,1:T(1,128)S(1)}, u32[]{:S(2)}, u32[]{:S(2)}) collective-permute-start(f32[4,2,1,258]{3,2,0,1:T(1,128)S(1)} %get-tuple-element.30), channel_id=1, source_target_pairs={{1,0},{2,1},{3,2},{0,3},{5,4},{6,5},{7,6},{4,7},{9,8},{10,9},{11,1... | collective-permute-start | bytes 24776 | tf_op jit(solution)/shard_map/ppermute | solution.py:48
  72.5 6.7 %copy-start.7 = (f32[1,64,1024]{2,1,0:T(8,128)S(1)}, f32[1,64,1024]{2,1,0:T(8,128)}, u32[]{:S(2)}) copy-start(f32[1,64,1024]{2,1,0:T(8,128)} %copy-done.6) | copy-start | bytes 786436
  77.6 3.4 %copy-start.2 = (f32[10,64,1024]{2,1,0:T(8,128)S(1)}, f32[10,64,1024]{2,1,0:T(8,128)}, u32[]{:S(2)}) copy-start(f32[10,64,1024]{2,1,0:T(8,128)} %constant_dynamic-update-slice_fusion) | copy-start | bytes 7864324
  100.8 5.4 %copy-start.3 = (f32[2,4,16,4,1024]{4,3,2,1,0:T(4,128)S(1)}, f32[2,4,16,4,1024]{4,3,2,1,0:T(4,128)}, u32[]{:S(2)}) copy-start(f32[2,4,16,4,1024]{4,3,2,1,0:T(4,128)} %reshape.234) | copy-start | bytes 6291460
  100.8 5.4 %copy-start.13 = (f32[2,4]{1,0:T(2,128)S(1)}, f32[2,4]{1,0:T(2,128)}, u32[]{:S(2)}) copy-start(f32[2,4]{1,0:T(2,128)} %mul.485) | copy-start | bytes 100
  106.3 7.6 %copy-start.11 = (s32[1024]{0:T(1024)S(1)}, s32[1024]{0:T(1024)}, u32[]{:S(2)}) copy-start(s32[1024]{0:T(1024)} %get-tuple-element.35) | copy-start | bytes 12292
  106.3 7.6 %copy-start.12 = (s32[1024]{0:T(1024)S(1)}, s32[1024]{0:T(1024)}, u32[]{:S(2)}) copy-start(s32[1024]{0:T(1024)} %get-tuple-element.38) | copy-start | bytes 12292
  106.3 7.6 %copy-start.14 = (pred[1024]{0:T(1024)(128)(4,1)S(1)}, pred[1024]{0:T(1024)(128)(4,1)}, u32[]{:S(2)}) copy-start(pred[1024]{0:T(1024)(128)(4,1)} %get-tuple-element.40) | copy-start | bytes 3076
  115.5 19.8 %all-to-all-start.2 = ((f32[2,16,256]{2,0,1:T(2,128)}), f32[2,16,256]{2,0,1:T(2,128)S(1)}, u32[]{:S(2)}, u32[]{:S(2)}) async-start(f32[2,16,256]{2,0,1:T(2,128)} %copy.37), calls=%async_computation.2 | async-start | bytes 65536 | tf_op jit(solution)/shard_map/all_to_all | solution.py:233
  135.3 32.3 %copy-start.9 = (f32[1,2,8,16,256]{4,3,2,1,0:T(8,128)S(1)}, f32[1,2,8,16,256]{4,3,2,1,0:T(8,128)}, u32[]{:S(2)}) copy-start(f32[1,2,8,16,256]{4,3,2,1,0:T(8,128)} %param.5) | copy-start | bytes 786436
  157.5 10.1 %all-to-all-start.5 = ((f32[4,2,2,16,256]{4,3,2,1,0:T(8,128)}), f32[4,2,2,16,256]{4,3,2,1,0:T(8,128)S(1)}, u32[]{:S(2)}, u32[]{:S(2)}) async-start(f32[4,2,2,16,256]{4,3,2,1,0:T(8,128)} %broadcast_in_dim.35), calls=%async_computation.5 | async-start | bytes 524288 | tf_op jit(solution)/shard_map/all_to_all | solution.py:90
  (7 other events, 18.6 us)
where the time goes:
time: 170 us; the launch traced here: 168 us
  starting transfers between devices  45.7 us (27%)
  local copies, waits for them, and re-layouts  44.4 us (26%)
  waiting for transfers between devices  24.4 us (14%)
  other arithmetic  22.1 us (13%)
  blocking collectives  18.6 us (11%)
  matrix products  10.7 us (6%)
  between operations  2.36 us (1%)
    all_to_all x2, blocking collectives, exchange_in_order(): filled = lax.all_to_all(filled, axes[k], k, k, tiled=True)  18.6 us
    reshape x5, local copies, waits for them, and re-layouts, levels(): return piece.reshape((quarter, RATIO) + piece.shape[1:])  12.2 us
    all_to_all x1, starting transfers between devices, per_device(): lax.all_to_all(coarse_modes[0], GX, split_axis=2, concat_axis=3, tiled=True)  11.2 us
    all_to_all x1, starting transfers between devices, joined_exchange(): parts = lax.all_to_all(parts, axis, split_axis=0, concat_axis=0, tiled=True)  11.1 us
    all_to_all x1, starting transfers between devices, per_device(): lax.all_to_all(restricted, GX, split_axis=1, concat_axis=2, tiled=True)  11.1 us
    all_to_all x1, waiting for transfers between devices, per_device(): lax.all_to_all(restricted, GX, split_axis=1, concat_axis=2, tiled=True)  8.67 us
    add x1, other arithmetic, per_device(): updated = centre + fine_step * (spread - advection)  7.62 us
    reduce_sum x1, other arithmetic, per_device(): buoyancy.reshape(quarter, RATIO, row_count, RATIO, width * RATIO)  7.56 us
  transfers between devices with their start and end apart: 14, of which 6 were waited for; matrix products, arithmetic and copies ran while one was open for 21% of the time, Pallas kernels for 0%

commit v1 on v0

v1 whole, which is shorter than its diff:
```python
import functools
import math

import jax
import jax.numpy as jnp
import numpy as np
from jax import lax
from jax.experimental import pallas as pl
from jax.experimental.pallas import tpu as pltpu
from jax.sharding import Mesh
from jax.sharding import PartitionSpec as P

GX = ("gx_0", "gx_1")
GRP_GX = ("grp", "gx_0", "gx_1")
F32 = jnp.float32
BF16 = jnp.bfloat16
G = 16
NV = 4096
W = 256
FINE = 1024
VMEM_LIMIT = 48 << 20


def split_table(table):
    table = np.asarray(table, np.float64)
    high = table.astype(np.float32).astype(jnp.bfloat16)
    low = (table - high.astype(np.float64)).astype(np.float32).astype(jnp.bfloat16)
    return high, low


@functools.cache
def tables():
    out = {}
    k = np.arange(W)
    angle = 2 * np.pi * (np.outer(k, k) % W) / W
    norm = NV ** -0.5
    out["inv"] = split_table(np.concatenate([np.cos(angle), -np.sin(angle)], 0) * norm)
    r = np.arange(G)
    angle = 2 * np.pi * np.outer(r, k) / NV
    twc = np.zeros((G, 8, 128), np.float32)
    tws = np.zeros((G, 8, 128), np.float32)
    twc[:, :2] = np.cos(angle).reshape(G, 2, 128)
    tws[:, :2] = np.sin(angle).reshape(G, 2, 128)
    out["tw"] = (twc, tws)
    lanes = 16 * (k % 16) + k // 16
    order = np.argsort(lanes)
    assert np.array_equal(order, 16 * (k % 16) + k // 16)
    full = np.zeros((W + 2, FINE))
    for n in range(FINE):
        c, s = divmod(n, 4)
        o = (s + 0.5) / 4 - 0.5
        full[c + 1, n] += 1 - abs(o)
        full[c + 1 + (1 if o > 0 else -1), n] += abs(o)
    out["ref"] = full[1:-1][order].astype(jnp.bfloat16)
    edge = np.zeros((2, 128, 256))
    filt = np.zeros((W + 2, W))
    for b in range(W):
        filt[b : b + 3, b] = (0.125, 0.75, 0.125)
    out["filt"] = filt[1:-1][order].astype(jnp.bfloat16)
    fedge = np.zeros((2, 128, 256))
    for q in range(2):
        edge[q, 2 * q, :128] = full[0, :128]
        edge[q, 2 * q + 1, 128:] = full[-1, -128:]
        fedge[q, 2 * q] = filt[0]
        fedge[q, 2 * q + 1] = filt[-1]
    out["edge"] = edge.astype(jnp.bfloat16)
    out["fedge"] = fedge.astype(jnp.bfloat16)
    ym = np.zeros((64, 32))
    yt = np.zeros((16, 32))
    place = lambda c: 16 if c < 0 else 17 if c > 15 else c
    for n in range(64):
        c, s = divmod(n, 4)
        o = (s + 0.5) / 4 - 0.5
        ym[n, c] += 1 - abs(o)
        ym[n, place(c + (1 if o > 0 else -1))] += abs(o)
    for c in range(16):
        yt[c, c] += 0.75
        yt[c, place(c - 1)] += 0.125
        yt[c, place(c + 1)] += 0.125
    out["ym"] = np.concatenate([ym, ym], 1).astype(jnp.bfloat16)
    out["yt"] = np.concatenate([yt, yt], 1).astype(jnp.bfloat16)
    cm = np.zeros((FINE, W))
    cm[np.arange(FINE), np.arange(FINE) // 4] = 1.0 / 4
    out["cm"] = cm.astype(jnp.bfloat16)
    rm = np.zeros((32, 128))
    rm[np.arange(128) // 4, np.arange(128)] = 1.0 / 16
    out["rm"] = np.concatenate([rm, rm], 1).astype(jnp.bfloat16)
    g = np.arange(G)
    angle = 2 * np.pi * np.outer(k, k) / NV
    out["fwd"] = (np.concatenate([np.cos(angle), -np.sin(angle)], 1) * norm).astype(np.float32)
    angle = 2 * np.pi * (np.outer(g, k) % G) / G
    out["comb"] = (np.cos(angle).astype(np.float32), np.sin(angle).astype(np.float32))
    return out


def halves(x):
    high = x.astype(BF16)
    low = (x - high.astype(F32)).astype(BF16)
    return high, low


def mm(a, b):
    return jnp.dot(a, b, preferred_element_type=F32)


def call(kernel, out_shape, **kw):
    return pl.pallas_call(
        kernel,
        out_shape=out_shape,
        compiler_params=pltpu.CompilerParams(vmem_limit_bytes=VMEM_LIMIT),
        **kw,
    )


def sds(*shape, dtype=F32):
    return jax.ShapeDtypeStruct(shape, dtype)


def iota(shape, dim):
    return lax.broadcasted_iota(jnp.int32, shape, dim)


def roll(x, shift, axis):
    return pltpu.roll(x, shift % x.shape[axis], axis)


def edges_kernel(me, modes_a, modes_b, south, north, west, east, low, high, chunk, up, down, zlow, zhigh):
    zlow[...] = low[0]
    zhigh[...] = high[0]
    for dst, rows, row, line in ((up, north, 7, 15), (down, south, 0, 0)):
        dst[0:16, :128] = modes_a[pl.ds(line, 16, stride=16), :]
        dst[0:16, 128:] = modes_b[pl.ds(line, 16, stride=16), :]
        face = rows[:, row, :]
        for j in range(4):
            dst[16 + 8 * j : 24 + 8 * j, :] = face[:, 256 * j : 256 * j + 256]
    zero = jnp.zeros((8, 128), F32)
    for r in range(G):
        chunk[r, 0:16, :] = modes_a[pl.ds(r, 16, stride=16), :]
        chunk[r, 16:32, :] = modes_b[pl.ds(r, 16, stride=16), :]
        chunk[r, 32:40, :] = zero
    row_id = iota((8, 128), 0)

    def column(block, lane):
        tile = zero
        for i in range(4):
            both = jnp.concatenate([block[2 * i], block[2 * i + 1]], 0).T
            line = jnp.broadcast_to(both[lane : lane + 1, :], (8, 128))
            tile = jnp.where(row_id == 4 + i, line, tile)
        return tile

    chunk[(me[0] + 1) % G, 32:40, :] = column(east, 127)
    chunk[(me[0] + G - 1) % G, 32:40, :] = column(west, 0)


def edges(me, modes, salinity):
    block = lambda shape, *index: pl.BlockSpec(shape, lambda i, m, index=index: index)
    return call(
        edges_kernel,
        (sds(G, 40, 128), sds(48, 256), sds(48, 256), sds(64, FINE), sds(64, FINE)),
        grid_spec=pltpu.PrefetchScalarGridSpec(
            num_scalar_prefetch=1,
            grid=(1,),
            in_specs=[
                block((256, 128), 0, 0),
                block((256, 128), 0, 1),
                block((8, 8, FINE), 0, 0, 0),
                block((8, 8, FINE), 0, 7, 0),
                block((8, 64, 128), 0, 0, 0),
                block((8, 64, 128), 0, 0, 7),
                block((1, 64, FINE), 0, 0, 0),
                block((1, 64, FINE), 7, 0, 0),
            ],
            out_specs=[
                block((G, 40, 128), 0, 0, 0),
                block((48, 256), 0, 0),
                block((48, 256), 0, 0),
                block((64, FINE), 0, 0),
                block((64, FINE), 0, 0),
            ],
        ),
        name="edges",
    )(me, modes, modes, *[salinity] * 6)


def tails_kernel(chunk, from_south, from_north, out):
    row_id = iota((8, 128), 0)
    for r in range(G):
        rows = from_south if r < 8 else from_north
        p = r % 8
        tile = chunk[r]
        parts = (rows[p : p + 1, :128], rows[p : p + 1, 128:], rows[8 + p : 9 + p, :128], rows[8 + p : 9 + p, 128:])
        for i, part in enumerate(parts):
            tile = jnp.where(row_id == i, jnp.broadcast_to(part, (8, 128)), tile)
        out[r] = tile


def tails(chunk, from_south, from_north):
    tail = pl.BlockSpec((G, 8, 128), lambda i: (0, 4, 0))
    lines = pl.BlockSpec((16, 256), lambda i: (0, 0))
    return call(
        tails_kernel,
        sds(G, 40, 128),
        grid=(1,),
        in_specs=[tail, lines, lines],
        out_specs=tail,
        input_output_aliases={0: 0},
        name="tails",
    )(chunk, from_south, from_north)


def cmul(a, b, c, s):
    return a * c - b * s, a * s + b * c


def four(z):
    (ar, ai), (br, bi), (cr, ci), (dr, di) = z
    t0r, t0i, t1r, t1i = ar + cr, ai + ci, ar - cr, ai - ci
    t2r, t2i, t3r, t3i = br + dr, bi + di, br - dr, bi - di
    return (
        (t0r + t2r, t0i + t2i),
        (t1r - t3i, t1i + t3r),
        (t0r - t2r, t0i - t2i),
        (t1r + t3i, t1i - t3r),
    )


def sixteen(z):
    inner = [four([z[4 * g1 + g0] for g1 in range(4)]) for g0 in range(4)]
    out = [None] * 16
    for r0 in range(4):
        column = []
        for g0 in range(4):
            angle = 2 * math.pi * g0 * r0 / 16
            a, b = inner[g0][r0]
            column.append((a, b) if g0 * r0 == 0 else cmul(a, b, math.cos(angle), math.sin(angle)))
        for r1, value in enumerate(four(column)):
            out[4 * r1 + r0] = value
    return out


def inverse_kernel(recv, twc, tws, inv_high, inv_low, send, left_high, left_low, mid):
    row_id = iota((8, 128), 0)
    lane_id = iota((8, 128), 1)

    def put(r, top, part, value):
        high, low = halves(value)
        left_high[16 * r + 8 * top : 16 * r + 8 * top + 8, 128 * part : 128 * part + 128] = high
        left_low[16 * r + 8 * top : 16 * r + 8 * top + 8, 128 * part : 128 * part + 128] = low

    for h in range(2):
        z = [(recv[g, 16 * h : 16 * h + 8, :], recv[g, 16 * h + 8 : 16 * h + 16, :]) for g in range(G)]
        for r, (a, b) in enumerate(sixteen(z)):
            a, b = cmul(a, b, twc[r, h : h + 1, :], tws[r, h : h + 1, :])
            put(r, 0, h, a)
            put(r, 0, 2 + h, b)
    z = []
    for g in range(G):
        tile = jnp.where(row_id < 4, recv[g, 32:40, :], 0.0)
        z.append((tile, roll(tile, -2, 0)))
    for r, (a, b) in enumerate(sixteen(z)):
        a, b = cmul(a, b, twc[r], tws[r])
        for part, value in ((0, a), (2, b)):
            put(r, 1, part, jnp.where(row_id == 0, value, 0.0))
            put(r, 1, part + 1, jnp.where(row_id == 0, roll(value, -1, 0), 0.0))

    mid[...] = (
        mm(left_high[...], inv_high[...]) + mm(left_low[...], inv_high[...]) + mm(left_high[...], inv_low[...])
    )

    first, second, single = [], [], []
    for r in range(G):
        first.append(mid[16 * r : 16 * r + 8, 0:128])
        second.append(mid[16 * r : 16 * r + 8, 128:256])
        low = mid[16 * r + 8 : 16 * r + 16, 0:128]
        high = mid[16 * r + 8 : 16 * r + 16, 128:256]
        single.append(jnp.where(row_id == 0, low, roll(high, 1, 0)))
    for i in range(8):
        a, b = first[i], second[i]
        c, d = first[i + 8], second[i + 8]
        first[i], second[i], first[i + 8], second[i + 8] = a, c, b, d
        a, c = single[i], single[i + 8]
        single[i] = jnp.where(row_id == 0, a, roll(c, 1, 0))
        single[i + 8] = jnp.where(row_id == 0, roll(a, -1, 0), c)
    for bit in (4, 2, 1):
        upper = (lane_id // (16 * bit)) % 2 == 1
        for tiles in (first, second, single):
            for i in range(G):
                if i & bit:
                    continue
                a, b = tiles[i], tiles[i | bit]
                tiles[i] = jnp.where(upper, roll(b, 16 * bit, 1), a)
                tiles[i | bit] = jnp.where(upper, b, roll(a, -16 * bit, 1))

    left = [roll(second[d], 1, 1) for d in range(G)]
    right = [roll(first[d], 1, 1) for d in range(G)]
    side = [roll(single[d], 5, 1) for d in range(G)]
    for d in range(G):
        before, after = (d - 1) % G, (d + 1) % G
        own = jnp.where(lane_id == 0, left[before], jnp.where(lane_id == 1, right[after], 0.0))
        rim = own + roll(roll(own, -1, 0), 2, 1)
        base = jnp.where(row_id == 2, roll(single[d], 2, 0), 0.0)
        base = jnp.where(row_id == 6, roll(single[d], 5, 0), base)
        base = jnp.where((row_id == 3) & (lane_id == 4), roll(side[before], 2, 0), base)
        base = jnp.where((row_id == 3) & (lane_id == 5), roll(side[after], 3, 0), base)
        for g in range(4):
            tile = jnp.where(row_id < 2, roll(first[d], -2 * g, 0), base)
            tile = jnp.where((row_id == 4) | (row_id == 5), roll(second[d], 4 - 2 * g, 0), tile)
            tile = jnp.where((row_id == 3) & (lane_id < 4), roll(rim, 3 - 2 * g, 0), tile)
            send[16 * g + d] = tile


def inverse(recv):
    t = tables()
    twc, tws = map(jnp.asarray, t["tw"])
    high, low = map(jnp.asarray, t["inv"])
    return call(
        inverse_kernel,
        sds(64, 8, 128),
        scratch_shapes=[
            pltpu.VMEM((256, 512), BF16),
            pltpu.VMEM((256, 512), BF16),
            pltpu.VMEM((256, 256), F32),
        ],
        name="inverse",
    )(recv, twc, tws, high, low)


def fine_kernel(
    pos,
    recv,
    salinity,
    zlow,
    zhigh,
    from_south,
    from_north,
    west,
    east,
    rate,
    ym,
    yt,
    ref,
    edge,
    filt,
    fedge,
    cm,
    rm,
    out,
    spread,
    y_high,
    y_low,
    side,
    vel,
    total,
    warm,
):
    grp = pos[0]
    row_id = iota((8, 128), 0)
    lane_id = iota((8, 128), 1)

    def lines(f, q):
        main = [recv[pl.ds(f * 128 + i, 16, stride=8), :] for i in (q, 4 + q, 3)]
        south = recv[pl.ds(pl.multiple_of((f * 16 + 2 * grp + q) * 8, 8), 8), :]
        north = recv[pl.ds(pl.multiple_of((f * 16 + 8 + 2 * grp + q) * 8, 8), 8), :]
        parts = []
        for x, row in zip(main, (2, 6, 3)):
            s, n = roll(south, -row, 0), roll(north, 1 - row, 0)
            if row == 3:
                s, n = roll(s, 2 * q - 4, 1), roll(n, 2 * q - 4, 1)
            tile = jnp.where(row_id == 0, s, jnp.where(row_id == 1, n, 0.0))
            parts.append(jnp.concatenate([x, tile, jnp.zeros((8, 128), F32)], 0))
        return jnp.concatenate(parts, 1)

    def along_y(table, f, q):
        high, low = halves(lines(f, q))
        return mm(table[...], jnp.concatenate([high, low], 0))

    for f in range(3):
        for q in range(2):
            at = slice(64 * (2 * f + q), 64 * (2 * f + q) + 64)
            high, low = halves(along_y(ym, f, q) * 0.05)
            y_high[at, :] = high[:, :256]
            y_low[at, :] = low[:, :256]
            side[at, :] = mm(high[:, 256:], edge[q]) + mm(low[:, 256:], edge[q])
    for q in range(2):
        high, low = halves(along_y(yt, 3, q))
        warm[16 * q : 16 * q + 16, :] = (
            mm(high[:, :256], filt[...])
            + mm(low[:, :256], filt[...])
            + mm(high[:, 256:], fedge[q])
            + mm(low[:, 256:], fedge[q])
        )
    vel[...] = mm(y_high[...], ref[...]) + mm(y_low[...], ref[...])
    vel[:, :128] += side[:, :128]
    vel[:, FINE - 128 :] += side[:, 128:]

    west_t = west[0].T
    east_t = east[0].T
    last_row = iota((8, FINE), 0) == 7
    first_row = iota((8, FINE), 0) == 0
    last_lane = lane_id == 127
    first_lane = lane_id == 0

    def outer(rows, l):
        line = jnp.concatenate([rows[16 + 8 * j + l : 17 + 8 * j + l, :] for j in range(4)], 1)
        return jnp.broadcast_to(line, (8, FINE))

    for yb in range(8):
        ys = slice(8 * yb, 8 * yb + 8)
        for q in range(2):
            vx, vy, vz = (vel[64 * (2 * f + q) + 8 * yb : 64 * (2 * f + q) + 8 * yb + 8, :] for f in range(3))
            acc = None
            for l in range(4 * q, 4 * q + 4):
                c = salinity[l, ys, :]
                upper = salinity[l + 1, ys, :] if l < 7 else zhigh[ys, :]
                lower = salinity[l - 1, ys, :] if l > 0 else zlow[ys, :]
                if yb < 7:
                    north = salinity[l, 8 * yb + 1 : 8 * yb + 9, :]
                else:
                    north = jnp.where(last_row, outer(from_north, l), roll(c, -1, 0))
                if yb > 0:
                    south = salinity[l, 8 * yb - 1 : 8 * yb + 7, :]
                else:
                    south = jnp.where(first_row, outer(from_south, l), roll(c, 1, 0))
                at = (l % 2) * 64 + 8 * yb
                ecol = jnp.broadcast_to(east_t[at : at + 8, 4 + l // 2 : 5 + l // 2], (8, 128))
                wcol = jnp.broadcast_to(west_t[at : at + 8, 4 + l // 2 : 5 + l // 2], (8, 128))
                e = roll(c, -1, 1)
                w = roll(c, 1, 1)
                e = jnp.concatenate([e[:, :-128], jnp.where(last_lane, ecol, e[:, -128:])], 1)
                w = jnp.concatenate([jnp.where(first_lane, wcol, w[:, :128]), w[:, 128:]], 1)
                k = rate[l] * 0.1
                new = (
                    c
                    + k * (((e + w) + (north + south)) + (upper + lower) - 6.0 * c)
                    - (vx * (e - w) + vy * (north - south) + vz * (upper - lower))
                )
                out[l, ys, :] = new
                acc = new if acc is None else acc + new
            total[64 * q + 8 * yb : 64 * q + 8 * yb + 8, :] = acc
    high, low = halves(total[...])
    high, low = halves(mm(high, cm[...]) + mm(low, cm[...]))
    mean = warm[...] - mm(rm[...], jnp.concatenate([high, low], 0))
    for a in range(G):
        spread[a] = mean


def fine(pos, recv1, recv2, salinity, zlow, zhigh, from_south, from_north, rate):
    t = tables()
    whole = lambda x: pl.BlockSpec(x.shape, lambda i, m, n=x.ndim: (0,) * n)
    consts = [jnp.asarray(t[name]) for name in ("ym", "yt", "ref", "edge", "filt", "fedge", "cm", "rm")]
    recv2 = recv2.reshape(512, 128)
    arrays = [recv2, salinity, zlow, zhigh, from_south, from_north]
    near = lambda step: pl.BlockSpec((1, 8, 128), lambda i, m: ((m[1] + step) % G, 4, 0))
    return call(
        fine_kernel,
        (sds(8, 64, FINE), sds(G, 32, 256)),
        grid_spec=pltpu.PrefetchScalarGridSpec(
            num_scalar_prefetch=1,
            grid=(1,),
            in_specs=[whole(x) for x in arrays]
            + [near(G - 1), near(1), pl.BlockSpec(memory_space=pltpu.SMEM)]
            + [whole(x) for x in consts],
            out_specs=[
                pl.BlockSpec((8, 64, FINE), lambda i, m: (0, 0, 0)),
                pl.BlockSpec((G, 32, 256), lambda i, m: (0, 0, 0)),
            ],
            scratch_shapes=[
                pltpu.VMEM((384, 256), BF16),
                pltpu.VMEM((384, 256), BF16),
                pltpu.VMEM((384, 256), F32),
                pltpu.VMEM((384, FINE), F32),
                pltpu.VMEM((128, FINE), F32),
                pltpu.VMEM((32, 256), F32),
            ],
        ),
        name="fine",
    )(pos, *arrays, recv1, recv1, rate, *consts)


def table_kernel(pos, base, high, low):
    turns = (iota((16, 128), 0) * pos[1]) % G
    angle = turns.astype(F32) * (2.0 * math.pi / G)
    cos = jnp.concatenate([jnp.cos(angle)] * 2, 1)
    sin = -jnp.concatenate([jnp.sin(angle)] * 2, 1)
    for t in range(G):
        rows = slice(16 * t, 16 * t + 16)
        real, imag = base[rows, :256], base[rows, 256:]
        for at, value in ((0, real * cos - imag * sin), (256, real * sin + imag * cos)):
            high[rows, at : at + 256], low[rows, at : at + 256] = halves(value)


def table(pos):
    whole = pl.BlockSpec((256, 512), lambda i, m: (0, 0))
    return call(
        table_kernel,
        (sds(256, 512, dtype=BF16), sds(256, 512, dtype=BF16)),
        grid_spec=pltpu.PrefetchScalarGridSpec(
            num_scalar_prefetch=1, grid=(1,), in_specs=[whole], out_specs=[whole, whole]
        ),
        name="table",
    )(pos, jnp.asarray(tables()["fwd"]))


def forward_kernel(recv, table_high, table_low, comb_cos, comb_sin, out, left_high, left_low, mid):
    for a in range(G):
        high, low = halves(recv[a])
        left_high[32 * a : 32 * a + 32, :] = high
        left_low[32 * a : 32 * a + 32, :] = low
    mid[...] = (
        mm(left_high[...], table_high[...]) + mm(left_low[...], table_high[...]) + mm(left_high[...], table_low[...])
    )
    real = imag = jnp.zeros((32, 256), F32)
    for a in range(G):
        c, s = comb_cos[a : a + 1, :], comb_sin[a : a + 1, :]
        x, y = mid[32 * a : 32 * a + 32, :256], mid[32 * a : 32 * a + 32, 256:]
        real = real + (x * c + y * s)
        imag = imag + (y * c - x * s)
    for g in range(4):
        out[g, 0:32, :] = real
        out[g, 32:64, :] = imag


def forward(recv, high, low):
    cos, sin = map(jnp.asarray, tables()["comb"])
    return call(
        forward_kernel,
        sds(4, 64, 256),
        scratch_shapes=[
            pltpu.VMEM((512, 256), BF16),
            pltpu.VMEM((512, 256), BF16),
            pltpu.VMEM((512, 512), F32),
        ],
        name="forward",
    )(recv, high, low, cos, sin)


def shifted(array, axis, step):
    count = lax.axis_size(axis)
    return lax.ppermute(array, axis, [(i, (i + step) % count) for i in range(count)])


def per_device(coarse_modes, salinity, viscosity, forcing_gain, diffusivity):
    me = lax.axis_index(GX).astype(jnp.int32)
    pos = jnp.stack([lax.axis_index("grp").astype(jnp.int32), me])
    modes = coarse_modes.reshape(256, 256)
    chunk, up, down, low_face, high_face = edges(pos[1:], modes, salinity)
    from_south = shifted(up, "gy", 1)
    from_north = shifted(down, "gy", -1)
    zlow = shifted(high_face, "grp", 1)
    zhigh = shifted(low_face, "grp", -1)
    chunk = tails(chunk, from_south, from_north)
    recv1 = lax.all_to_all(chunk, GX, 0, 0, tiled=True)
    recv2 = lax.all_to_all(inverse(recv1), GRP_GX, 0, 0, tiled=True)
    salinity_next, spread = fine(
        pos, recv1, recv2, salinity, zlow, zhigh, from_south, from_north, diffusivity
    )
    recv3 = lax.all_to_all(spread, GX, 0, 0, tiled=True)
    recv4 = lax.all_to_all(forward(recv3, *table(pos)), "grp", 0, 0, tiled=True)
    spectrum = recv4.reshape(4, 2, 2, 16, W).transpose(1, 0, 2, 3, 4).reshape(2, 8, 16, W)
    mode_index = me * W + lax.broadcasted_iota(jnp.int32, (W,), 0)
    wavenumber = jnp.where(mode_index < NV // 2, mode_index, mode_index - NV)
    scaled_wave = 2.0 * math.pi / NV * wavenumber.astype(F32)
    damping = jnp.exp(-viscosity[0] * scaled_wave * scaled_wave)
    coarse_next = damping * coarse_modes + forcing_gain[0] * spectrum[None]
    return (salinity_next, coarse_next)


def solution(mesh):
    finer = Mesh(
        mesh.devices.reshape(mesh.shape["grp"], 2, 8, mesh.shape["gy"]),
        ("grp", "gx_0", "gx_1", "gy"),
    )
    in_specs = (P("grp", None, None, "gy", GX), P("grp", "gy", GX), P("grp"), P("grp"), P("grp"))
    out_specs = (P("grp", "gy", GX), P("grp", None, None, "gy", GX))
    return jax.shard_map(
        per_device, mesh=finer, in_specs=in_specs, out_specs=out_specs, check_vma=False
    )
```

time: 170 us -> 107 us (0.63)
  local copies, waits for them, and re-layouts: 44.4 us -> 12.9 us
  starting transfers between devices: 45.7 us -> 24.3 us
  other arithmetic: 22.1 us -> 1.36 us
  matrix products: 10.7 us -> 0 us
  Pallas kernels: 0 us -> 9.97 us
  waiting for transfers between devices: 24.4 us -> 31.8 us
  blocking collectives: 18.6 us -> 24 us
    all_to_all x4 -> x3, starting transfers between devices: 36.8 us -> 19.2 us  [the longest x1 8.98 us: per_device(): recv2 = lax.all_to_all(inverse(recv1), GRP_GX, 0, 0, tiled=True)]
    reshape x8 -> x0, local copies, waits for them, and re-layouts: 14.1 us -> none  [the longest x5 12.2 us: levels(): return piece.reshape((quarter, RATIO) + piece.shape[1:])]
    dot_general x14 -> x0, matrix products: 10.7 us -> none  [the longest x1 5.04 us: per_device(): jnp.einsum('fqyj,jx->fqyx', along_y, spread_table(width), precision=lax.P...]
    pallas_call x0 -> x6, Pallas kernels: none -> 9.97 us  [the longest x1 6.12 us: fine(): call(fine_kernel, (sds(8, 64, FINE), sds(G, 32, 256)), grid_spec=pltpu.Pr...]
    ppermute x10 -> x4, waiting for transfers between devices: 1.38 us -> 9.69 us  [shifted(): lax.ppermute(array, axis, [(i, (i + step) % count) for i in range(count)])]
    add x2 -> x0, other arithmetic: 8.22 us -> none  [the longest x1 7.62 us: per_device(): updated = centre + fine_step * (spread - advection)]
    reduce_sum x1 -> x0, other arithmetic: 7.56 us -> none  [per_device(): buoyancy.reshape(quarter, RATIO, row_count, RATIO, width * RATIO)]
    unnamed x36 -> x54, local copies, waits for them, and re-layouts: 5.43 us -> 12.9 us
  transfers between devices with their start and end apart: 14 -> 7, of which waited for: 6 -> 5; matrix products, arithmetic and copies ran while one was open for 21% -> 1% of each run, Pallas kernels for 0% -> 1%
where the time goes in v1:
time: 107 us; the launch traced here: 106 us
  waiting for transfers between devices  31.8 us (30%)
  starting transfers between devices  24.3 us (23%)
  blocking collectives  24 us (22%)
  local copies, waits for them, and re-layouts  12.9 us (12%)
  Pallas kernels  9.97 us (9%)
  between operations  2.11 us (2%)
  other arithmetic  1.36 us (1%)
    all_to_all x1, blocking collectives, per_device(): recv1 = lax.all_to_all(chunk, GX, 0, 0, tiled=True)  24 us
    all_to_all x1, waiting for transfers between devices, per_device(): recv3 = lax.all_to_all(spread, GX, 0, 0, tiled=True)  13.8 us
    unnamed x54, local copies, waits for them, and re-layouts  12.9 us
    ppermute x4, waiting for transfers between devices, shifted(): lax.ppermute(array, axis, [(i, (i + step) % count) for i in range(count)])  9.69 us
    all_to_all x1, starting transfers between devices, per_device(): recv2 = lax.all_to_all(inverse(recv1), GRP_GX, 0, 0, tiled=True)  8.98 us
    all_to_all x1, starting transfers between devices, per_device(): recv3 = lax.all_to_all(spread, GX, 0, 0, tiled=True)  6.79 us
    pallas_call x1, Pallas kernels, fine(): call(fine_kernel, (sds(8, 64, FINE), sds(G, 32, 256)), grid_spec=pltpu.Pr...  6.12 us
    all_to_all x1, waiting for transfers between devices, per_device(): recv4 = lax.all_to_all(forward(recv3, *table(pos)), 'grp', 0, 0, tiled=True)  5.33 us
  transfers between devices with their start and end apart: 7, of which 5 were waited for; matrix products, arithmetic and copies ran while one was open for 1% of the time, Pallas kernels for 1%

profile of v1, /device:TPU:32, one launch (start us, length us, event | category | flops | bytes accessed | tf_op | source)
XLA Modules:
  0.0 106.5 jit_solution(8425879177592507417)
XLA Ops:
  0.6 1.6 %copy-done = f32[8,64,1024]{2,1,0:T(8,128)S(1)} copy-done((f32[8,64,1024]{2,1,0:T(8,128)S(1)}, f32[8,64,1024]{2,1,0:T(8,128)}, u32[]{:S(2)}) %copy-start) | copy-done | bytes 2097176
  2.2 0.9 copy-done.2
  3.6 1.7 %collective-permute-start.1 = (f32[48,256]{1,0:T(8,128)S(1)}, f32[48,256]{1,0:T(8,128)S(1)}, u32[]{:S(2)}, u32[]{:S(2)}) collective-permute-start(f32[48,256]{1,0:T(8,128)S(1)} %get-tuple-element.13), channel_id=1, source_target_pairs={{0,3},{1,0},{2,1},{3,2},{4,7},{5,4},{6,5},{7,6},{8,11},{9,8},{10,9... | collective-permute-start | bytes 147464 | tf_op jit(solution)/shard_map/ppermute | solution.py:539
  5.3 1.8 %collective-permute-done.from_south = f32[48,256]{1,0:T(8,128)S(1)} collective-permute-done((f32[48,256]{1,0:T(8,128)S(1)}, f32[48,256]{1,0:T(8,128)S(1)}, u32[]{:S(2)}, u32[]{:S(2)}) %collective-permute-start) | collective-permute-done | bytes 49184 | tf_op jit(solution)/shard_map/ppermute | solution.py:539
  7.1 24.0 %all_to_all.20.recv.west.east = f32[16,40,128]{2,1,0:T(8,128)S(1)} all-to-all(f32[16,40,128]{2,1,0:T(8,128)S(1)} %tails.1), channel_id=1, replica_groups=mesh['grp'=4,'gx_0'=2,'gx_1'=8,'gy'=4] {'gx_0','gx_1'}, dimensions={0} | all-to-all | bytes 655360 | tf_op jit(solution)/shard_map/all_to_all | solution.py:552
  31.1 1.6 %inverse.1 = f32[64,8,128]{2,1,0:T(8,128)} custom-call(f32[16,40,128]{2,1,0:T(8,128)S(1)} %all_to_all.20.recv.west.east, f32[16,8,128]{2,1,0:T(8,128)S(1)} %copy-done.15, f32[16,8,128]{2,1,0:T(8,128)S(1)} %copy-done.16, bf16[512,256]{1,0:T(8,128)(2,1)S(1)} %copy-done.8, bf16[512,256]{1,0:T(8,128)(2,1)S(1)} %copy-done.9), custom_call_target="tpu_custom_call" | custom-call | tf_op jit(solution)/shard_map/inverse/pallas_call | solution.py:316
  32.7 9.0 %all-to-all-start.1 = ((f32[64,8,128]{2,1,0:T(8,128)}), f32[64,8,128]{2,1,0:T(8,128)S(1)}, u32[]{:S(2)}, u32[]{:S(2)}) async-start(f32[64,8,128]{2,1,0:T(8,128)} %inverse.1), calls=%async_computation.1 | async-start | bytes 524288 | tf_op jit(solution)/shard_map/all_to_all | solution.py:553
  41.7 1.5 %collective-permute-start.2 = (f32[64,1024]{1,0:T(8,128)}, f32[64,1024]{1,0:T(8,128)S(1)}, u32[]{:S(2)}, u32[]{:S(2)}) collective-permute-start(f32[64,1024]{1,0:T(8,128)} %copy-done.26), channel_id=1, source_target_pairs={{0,64},{64,128},{128,192},{192,0},{1,65},{65,129},{129,193},{193,1... | collective-permute-start | bytes 786440 | tf_op jit(solution)/shard_map/ppermute | solution.py:539
  43.2 1.8 %collective-permute-start.3 = (f32[64,1024]{1,0:T(8,128)}, f32[64,1024]{1,0:T(8,128)}, u32[]{:S(2)}, u32[]{:S(2)}) collective-permute-start(f32[64,1024]{1,0:T(8,128)} %copy-done.25), channel_id=1, source_target_pairs={{0,192},{64,0},{128,64},{192,128},{1,193},{65,1},{129,65},{193,129... | collective-permute-start | bytes 786440 | tf_op jit(solution)/shard_map/ppermute | solution.py:539
  45.6 7.9 %collective-permute-done.2.zlow = f32[64,1024]{1,0:T(8,128)S(1)} collective-permute-done((f32[64,1024]{1,0:T(8,128)}, f32[64,1024]{1,0:T(8,128)S(1)}, u32[]{:S(2)}, u32[]{:S(2)}) %collective-permute-start.2) | collective-permute-done | bytes 262176 | tf_op jit(solution)/shard_map/ppermute | solution.py:539
  53.5 3.0 %all-to-all-done.1 = f32[64,8,128]{2,1,0:T(8,128)S(1)} async-done(((f32[64,8,128]{2,1,0:T(8,128)}), f32[64,8,128]{2,1,0:T(8,128)S(1)}, u32[]{:S(2)}, u32[]{:S(2)}) %all-to-all-start.1) | async-done | bytes 262176 | tf_op jit(solution)/shard_map/all_to_all | solution.py:553
  56.5 1.0 copy-done.5
  57.5 0.8 copy-done.11
  58.3 0.9 copy-done.12
  59.2 0.9 copy-done.13
  60.1 0.9 copy-done.14
  64.4 6.1 %fine.1 = (f32[8,64,1024]{2,1,0:T(8,128)}, f32[16,32,256]{2,1,0:T(8,128)S(1)}) custom-call(s32[2]{0:T(128)S(1)} %copy-done.22, f32[512,128]{1,0:T(8,128)S(1)} %bitcast.13, f32[8,64,1024]{2,1,0:T(8,128)S(1)} %copy-done.1, f32[64,1024]{1,0:T(8,128)S(1)} %collective-permute-done.2.zlow, f32[64,1024]{1,0:T(8,128)} %collective-permute-done.3.zhigh, ...), custom_call_target="tpu_custom_call" | custom-call | tf_op jit(solution)/shard_map/fine/pallas_call | solution.py:454
  70.6 0.8 copy-done.7
  71.3 6.8 %all-to-all-start.2 = ((f32[16,32,256]{2,1,0:T(8,128)}), f32[16,32,256]{2,1,0:T(8,128)S(1)}, u32[]{:S(2)}, u32[]{:S(2)}) async-start(f32[16,32,256]{2,1,0:T(8,128)} %copy-done.7), calls=%async_computation.2 | async-start | bytes 1048576 | tf_op jit(solution)/shard_map/all_to_all | solution.py:557
  78.1 1.0 copy-done.6
  80.5 13.8 %all-to-all-done.2.recv = f32[16,32,256]{2,1,0:T(8,128)S(1)} async-done(((f32[16,32,256]{2,1,0:T(8,128)}), f32[16,32,256]{2,1,0:T(8,128)S(1)}, u32[]{:S(2)}, u32[]{:S(2)}) %all-to-all-start.2) | async-done | bytes 524320 | tf_op jit(solution)/shard_map/all_to_all | solution.py:557
  94.3 1.3 %forward.1 = f32[4,64,256]{2,1,0:T(8,128)} custom-call(f32[16,32,256]{2,1,0:T(8,128)S(1)} %all-to-all-done.2.recv, bf16[256,512]{1,0:T(8,128)(2,1)S(1)} %get-tuple-element.18.table_high, bf16[256,512]{1,0:T(8,128)(2,1)S(1)} %get-tuple-element.19.table_low, f32[16,256]{1,0:T(8,128)S(1)} %copy-done.17, f32[16,256]{1,0:T(8,128)S(1)} %copy-done.18), custom_call_target="tpu_custom_call" | custom-call | tf_op jit(solution)/shard_map/forward/pallas_call | solution.py:525
  95.6 3.4 %all-to-all-start.3 = ((f32[4,64,256]{2,1,0:T(8,128)}), f32[4,64,256]{2,1,0:T(8,128)S(1)}, u32[]{:S(2)}, u32[]{:S(2)}) async-start(f32[4,64,256]{2,1,0:T(8,128)} %forward.1), calls=%async_computation.3 | async-start | bytes 524288 | tf_op jit(solution)/shard_map/all_to_all | solution.py:558
  100.3 5.3 %all-to-all-done.3 = f32[4,64,256]{2,1,0:T(8,128)S(1)} async-done(((f32[4,64,256]{2,1,0:T(8,128)}), f32[4,64,256]{2,1,0:T(8,128)S(1)}, u32[]{:S(2)}, u32[]{:S(2)}) %all-to-all-start.3) | async-done | bytes 262176 | tf_op jit(solution)/shard_map/all_to_all | solution.py:558
  (56 shorter events, 6.5 us)
Async XLA Ops:
  0.6 1.6 %copy-start = (f32[8,64,1024]{2,1,0:T(8,128)S(1)}, f32[8,64,1024]{2,1,0:T(8,128)}, u32[]{:S(2)}) copy-start(f32[8,64,1024]{2,1,0:T(8,128)} %salinity.1) | copy-start | bytes 6291460
  2.2 0.9 copy-start.2
  3.2 27.9 %copy-start.8 = (bf16[512,256]{1,0:T(8,128)(2,1)S(1)}, bf16[512,256]{1,0:T(8,128)(2,1)}, u32[]{:S(2)}) copy-start(bf16[512,256]{1,0:T(8,128)(2,1)} %constant.62.clone.inv_high) | copy-start | bytes 786436
  3.2 27.9 %copy-start.9 = (bf16[512,256]{1,0:T(8,128)(2,1)S(1)}, bf16[512,256]{1,0:T(8,128)(2,1)}, u32[]{:S(2)}) copy-start(bf16[512,256]{1,0:T(8,128)(2,1)} %constant.63.clone.inv_low) | copy-start | bytes 786436
  3.2 27.9 %copy-start.15 = (f32[16,8,128]{2,1,0:T(8,128)S(1)}, f32[16,8,128]{2,1,0:T(8,128)}, u32[]{:S(2)}) copy-start(f32[16,8,128]{2,1,0:T(8,128)} %constant.60.clone.twc) | copy-start | bytes 196612
  3.2 27.9 %copy-start.16 = (f32[16,8,128]{2,1,0:T(8,128)S(1)}, f32[16,8,128]{2,1,0:T(8,128)}, u32[]{:S(2)}) copy-start(f32[16,8,128]{2,1,0:T(8,128)} %constant.61.clone.tws) | copy-start | bytes 196612
  3.4 27.7 %copy-start.25 = (f32[64,1024]{1,0:T(8,128)}, f32[64,1024]{1,0:T(8,128)S(1)}, u32[]{:S(2)}) copy-start(f32[64,1024]{1,0:T(8,128)S(1)} %get-tuple-element.15) | copy-start | bytes 786436
  3.4 27.6 %copy-start.26 = (f32[64,1024]{1,0:T(8,128)}, f32[64,1024]{1,0:T(8,128)S(1)}, u32[]{:S(2)}) copy-start(f32[64,1024]{1,0:T(8,128)S(1)} %get-tuple-element.14) | copy-start | bytes 786436
  3.4 53.0 %copy-start.1 = (f32[8,64,1024]{2,1,0:T(8,128)S(1)}, f32[8,64,1024]{2,1,0:T(8,128)}, u32[]{:S(2)}) copy-start(f32[8,64,1024]{2,1,0:T(8,128)} %salinity.1) | copy-start | bytes 6291460
  3.5 53.0 %copy-start.4 = (bf16[256,1024]{1,0:T(8,128)(2,1)S(1)}, bf16[256,1024]{1,0:T(8,128)(2,1)}, u32[]{:S(2)}) copy-start(bf16[256,1024]{1,0:T(8,128)(2,1)} %constant.66.clone.ref) | copy-start | bytes 1572868
  3.5 3.6 %collective-permute-start = (f32[48,256]{1,0:T(8,128)S(1)}, f32[48,256]{1,0:T(8,128)S(1)}, u32[]{:S(2)}, u32[]{:S(2)}) collective-permute-start(f32[48,256]{1,0:T(8,128)S(1)} %get-tuple-element.12), channel_id=1, source_target_pairs={{0,1},{1,2},{2,3},{3,0},{4,5},{5,6},{6,7},{7,4},{8,9},{9,10},{10,1... | collective-permute-start | bytes 147464 | tf_op jit(solution)/shard_map/ppermute | solution.py:539
  3.6 3.5 %collective-permute-start.1 = (f32[48,256]{1,0:T(8,128)S(1)}, f32[48,256]{1,0:T(8,128)S(1)}, u32[]{:S(2)}, u32[]{:S(2)}) collective-permute-start(f32[48,256]{1,0:T(8,128)S(1)} %get-tuple-element.13), channel_id=1, source_target_pairs={{0,3},{1,0},{2,1},{3,2},{4,7},{5,4},{6,5},{7,6},{8,11},{9,8},{10,9... | collective-permute-start | bytes 147464 | tf_op jit(solution)/shard_map/ppermute | solution.py:539
  7.1 24.0 %copy-start.10 = (f32[48,256]{1,0:T(8,128)}, f32[48,256]{1,0:T(8,128)S(1)}, u32[]{:S(2)}) copy-start(f32[48,256]{1,0:T(8,128)S(1)} %collective-permute-done.1.from_north) | copy-start | bytes 147460
  32.7 23.8 %all-to-all-start.1 = ((f32[64,8,128]{2,1,0:T(8,128)}), f32[64,8,128]{2,1,0:T(8,128)S(1)}, u32[]{:S(2)}, u32[]{:S(2)}) async-start(f32[64,8,128]{2,1,0:T(8,128)} %inverse.1), calls=%async_computation.1 | async-start | bytes 524288 | tf_op jit(solution)/shard_map/all_to_all | solution.py:553
  41.7 11.8 %collective-permute-start.2 = (f32[64,1024]{1,0:T(8,128)}, f32[64,1024]{1,0:T(8,128)S(1)}, u32[]{:S(2)}, u32[]{:S(2)}) collective-permute-start(f32[64,1024]{1,0:T(8,128)} %copy-done.26), channel_id=1, source_target_pairs={{0,64},{64,128},{128,192},{192,0},{1,65},{65,129},{129,193},{193,1... | collective-permute-start | bytes 786440 | tf_op jit(solution)/shard_map/ppermute | solution.py:539
  43.2 10.3 %collective-permute-start.3 = (f32[64,1024]{1,0:T(8,128)}, f32[64,1024]{1,0:T(8,128)}, u32[]{:S(2)}, u32[]{:S(2)}) collective-permute-start(f32[64,1024]{1,0:T(8,128)} %copy-done.25), channel_id=1, source_target_pairs={{0,192},{64,0},{128,64},{192,128},{1,193},{65,1},{129,65},{193,129... | collective-permute-start | bytes 786440 | tf_op jit(solution)/shard_map/ppermute | solution.py:539
  56.5 1.0 copy-start.5
  59.2 0.9 copy-start.13
  64.4 29.9 %copy-start.17 = (f32[16,256]{1,0:T(8,128)S(1)}, f32[16,256]{1,0:T(8,128)}, u32[]{:S(2)}) copy-start(f32[16,256]{1,0:T(8,128)} %constant.73.clone.comb_cos) | copy-start | bytes 49156
  64.4 29.9 %copy-start.18 = (f32[16,256]{1,0:T(8,128)S(1)}, f32[16,256]{1,0:T(8,128)}, u32[]{:S(2)}) copy-start(f32[16,256]{1,0:T(8,128)} %constant.74.clone.comb_sin) | copy-start | bytes 49156
  71.3 34.4 %copy-start.3 = (f32[1,2,8,16,256]{4,3,2,1,0:T(8,128)S(1)}, f32[1,2,8,16,256]{4,3,2,1,0:T(8,128)}, u32[]{:S(2)}) copy-start(f32[1,2,8,16,256]{4,3,2,1,0:T(8,128)} %param.20) | copy-start | bytes 786436
  71.3 23.0 %all-to-all-start.2 = ((f32[16,32,256]{2,1,0:T(8,128)}), f32[16,32,256]{2,1,0:T(8,128)S(1)}, u32[]{:S(2)}, u32[]{:S(2)}) async-start(f32[16,32,256]{2,1,0:T(8,128)} %copy-done.7), calls=%async_computation.2 | async-start | bytes 1048576 | tf_op jit(solution)/shard_map/all_to_all | solution.py:557
  78.1 1.0 copy-start.6
  95.6 10.1 %all-to-all-start.3 = ((f32[4,64,256]{2,1,0:T(8,128)}), f32[4,64,256]{2,1,0:T(8,128)S(1)}, u32[]{:S(2)}, u32[]{:S(2)}) async-start(f32[4,64,256]{2,1,0:T(8,128)} %forward.1), calls=%async_computation.3 | async-start | bytes 524288 | tf_op jit(solution)/shard_map/all_to_all | solution.py:558
  (10 other events, 7.4 us)

commit v2 on v1

--- a/solution.py
+++ b/solution.py
@@ -18,7 +18,6 @@
 NV = 4096
 W = 256
 FINE = 1024
-VMEM_LIMIT = 48 << 20
 
 
 def split_table(table):
@@ -103,13 +102,34 @@
     return jnp.dot(a, b, preferred_element_type=F32)
 
 
-def call(kernel, out_shape, **kw):
-    return pl.pallas_call(
+VM = pl.BlockSpec(memory_space=pltpu.VMEM)
+SM = pl.BlockSpec(memory_space=pltpu.SMEM)
+HB = pl.BlockSpec(memory_space=pltpu.HBM)
+
+
+def call(kernel, out_shape, in_specs, out_specs, limit=12, **kw):
+    inner = pl.pallas_call(
         kernel,
         out_shape=out_shape,
-        compiler_params=pltpu.CompilerParams(vmem_limit_bytes=VMEM_LIMIT),
+        in_specs=in_specs,
+        out_specs=out_specs,
+        compiler_params=pltpu.CompilerParams(vmem_limit_bytes=limit << 20),
         **kw,
     )
+
+    def placed(*args):
+        return inner(
+            *[x if spec is not HB else pltpu.with_memory_space_constraint(x, pltpu.HBM) for x, spec in zip(args, in_specs)]
+        )
+
+    return placed
+
+
+def fetch(pairs, sems, first=0):
+    copies = [pltpu.make_async_copy(src, dst, sems.at[first + i]) for i, (src, dst) in enumerate(pairs)]
+    for copy in copies:
+        copy.start()
+    return copies
 
 
 def sds(*shape, dtype=F32):
@@ -124,9 +144,22 @@
     return pltpu.roll(x, shift % x.shape[axis], axis)
 
 
-def edges_kernel(me, modes_a, modes_b, south, north, west, east, low, high, chunk, up, down, zlow, zhigh):
-    zlow[...] = low[0]
-    zhigh[...] = high[0]
+def edges_kernel(me, modes, sal, chunk, up, down, zlow, zhigh, modes_a, modes_b, south, north, west, east, sems):
+    copies = fetch(
+        (
+            (modes.at[:, 0:128], modes_a),
+            (modes.at[:, 128:256], modes_b),
+            (sal.at[:, 0:8, :], south),
+            (sal.at[:, 56:64, :], north),
+            (sal.at[:, :, 0:128], west),
+            (sal.at[:, :, FINE - 128 :], east),
+            (sal.at[0], zlow),
+            (sal.at[7], zhigh),
+        ),
+        sems,
+    )
+    for copy in copies[:4]:
+        copy.wait()
     for dst, rows, row, line in ((up, north, 7, 15), (down, south, 0, 0)):
         dst[0:16, :128] = modes_a[pl.ds(line, 16, stride=16), :]
         dst[0:16, 128:] = modes_b[pl.ds(line, 16, stride=16), :]
@@ -148,38 +181,31 @@
             tile = jnp.where(row_id == 4 + i, line, tile)
         return tile
 
+    for copy in copies[4:6]:
+        copy.wait()
     chunk[(me[0] + 1) % G, 32:40, :] = column(east, 127)
     chunk[(me[0] + G - 1) % G, 32:40, :] = column(west, 0)
+    for copy in copies[6:]:
+        copy.wait()
 
 
 def edges(me, modes, salinity):
-    block = lambda shape, *index: pl.BlockSpec(shape, lambda i, m, index=index: index)
     return call(
         edges_kernel,
         (sds(G, 40, 128), sds(48, 256), sds(48, 256), sds(64, FINE), sds(64, FINE)),
-        grid_spec=pltpu.PrefetchScalarGridSpec(
-            num_scalar_prefetch=1,
-            grid=(1,),
-            in_specs=[
-                block((256, 128), 0, 0),
-                block((256, 128), 0, 1),
-                block((8, 8, FINE), 0, 0, 0),
-                block((8, 8, FINE), 0, 7, 0),
-                block((8, 64, 128), 0, 0, 0),
-                block((8, 64, 128), 0, 0, 7),
-                block((1, 64, FINE), 0, 0, 0),
-                block((1, 64, FINE), 7, 0, 0),
-            ],
-            out_specs=[
-                block((G, 40, 128), 0, 0, 0),
-                block((48, 256), 0, 0),
-                block((48, 256), 0, 0),
-                block((64, FINE), 0, 0),
-                block((64, FINE), 0, 0),
-            ],
-        ),
+        [SM, HB, HB],
+        [VM, VM, VM, HB, HB],
+        scratch_shapes=[
+            pltpu.VMEM((256, 128), F32),
+            pltpu.VMEM((256, 128), F32),
+            pltpu.VMEM((8, 8, FINE), F32),
+            pltpu.VMEM((8, 8, FINE), F32),
+            pltpu.VMEM((8, 64, 128), F32),
+            pltpu.VMEM((8, 64, 128), F32),
+            pltpu.SemaphoreType.DMA((8,)),
+        ],
         name="edges",
-    )(me, modes, modes, *[salinity] * 6)
+    )(me, modes, salinity)
 
 
 def tails_kernel(chunk, from_south, from_north, out):
@@ -187,25 +213,16 @@
     for r in range(G):
         rows = from_south if r < 8 else from_north
         p = r % 8
-        tile = chunk[r]
+        tile = chunk[r, 32:40, :]
         parts = (rows[p : p + 1, :128], rows[p : p + 1, 128:], rows[8 + p : 9 + p, :128], rows[8 + p : 9 + p, 128:])
         for i, part in enumerate(parts):
             tile = jnp.where(row_id == i, jnp.broadcast_to(part, (8, 128)), tile)
-        out[r] = tile
+        out[r, 0:32, :] = chunk[r, 0:32, :]
+        out[r, 32:40, :] = tile
 
 
 def tails(chunk, from_south, from_north):
-    tail = pl.BlockSpec((G, 8, 128), lambda i: (0, 4, 0))
-    lines = pl.BlockSpec((16, 256), lambda i: (0, 0))
-    return call(
-        tails_kernel,
-        sds(G, 40, 128),
-        grid=(1,),
-        in_specs=[tail, lines, lines],
-        out_specs=tail,
-        input_output_aliases={0: 0},
-        name="tails",
-    )(chunk, from_south, from_north)
+    return call(tails_kernel, sds(G, 40, 128), [VM] * 3, VM, name="tails")(chunk, from_south, from_north)
 
 
 def cmul(a, b, c, s):
@@ -238,7 +255,11 @@
     return out
 
 
-def inverse_kernel(recv, twc, tws, inv_high, inv_low, send, left_high, left_low, mid):
+def inverse_kernel(recv, twc_hbm, tws_hbm, high_hbm, low_hbm, send, left_high, left_low, mid, twc, tws, inv_high, inv_low, sems):
+    copies = fetch(((twc_hbm, twc), (tws_hbm, tws), (high_hbm, inv_high), (low_hbm, inv_low)), sems)
+    for copy in copies[:2]:
+        copy.wait()
+
     row_id = iota((8, 128), 0)
     lane_id = iota((8, 128), 1)
 
@@ -263,6 +284,8 @@
             put(r, 1, part, jnp.where(row_id == 0, value, 0.0))
             put(r, 1, part + 1, jnp.where(row_id == 0, roll(value, -1, 0), 0.0))
 
+    for copy in copies[2:]:
+        copy.wait()
     mid[...] = (
         mm(left_high[...], inv_high[...]) + mm(left_low[...], inv_high[...]) + mm(left_high[...], inv_low[...])
     )
@@ -316,44 +339,34 @@
     return call(
         inverse_kernel,
         sds(64, 8, 128),
+        [VM, HB, HB, HB, HB],
+        VM,
         scratch_shapes=[
             pltpu.VMEM((256, 512), BF16),
             pltpu.VMEM((256, 512), BF16),
             pltpu.VMEM((256, 256), F32),
+            pltpu.VMEM((G, 8, 128), F32),
+            pltpu.VMEM((G, 8, 128), F32),
+            pltpu.VMEM((512, 256), BF16),
+            pltpu.VMEM((512, 256), BF16),
+            pltpu.SemaphoreType.DMA((4,)),
         ],
         name="inverse",
     )(recv, twc, tws, high, low)
 
 
-def fine_kernel(
-    pos,
-    recv,
-    salinity,
-    zlow,
-    zhigh,
-    from_south,
-    from_north,
-    west,
-    east,
-    rate,
-    ym,
-    yt,
-    ref,
-    edge,
-    filt,
-    fedge,
-    cm,
-    rm,
-    out,
-    spread,
-    y_high,
-    y_low,
-    side,
-    vel,
-    total,
-    warm,
-):
-    grp = pos[0]
+CONSTS = ("ym", "edge", "yt", "filt", "fedge", "ref", "cm", "rm")
+
+
+def fine_kernel(me, grp_ref, rate_hbm, recv, edge_cols, salinity, zlow, zhigh, from_south, from_north, *rest):
+    hbm, (out, spread), rest = rest[:8], rest[8:10], rest[10:]
+    (y_high, y_low, side, vel, total, warm, new_sal), consts, (rate, sems, out_sems) = rest[:7], rest[7:15], rest[15:]
+    *copies, rates = fetch(tuple(zip(hbm, consts)) + ((rate_hbm, rate),), sems)
+    copies = dict(zip(CONSTS, copies))
+    ym, edge, yt, filt, fedge, ref, cm, rm = consts
+    grp = grp_ref[0]
+    copies["ym"].wait()
+    copies["edge"].wait()
     row_id = iota((8, 128), 0)
     lane_id = iota((8, 128), 1)
 
@@ -381,6 +394,8 @@
             y_high[at, :] = high[:, :256]
             y_low[at, :] = low[:, :256]
             side[at, :] = mm(high[:, 256:], edge[q]) + mm(low[:, 256:], edge[q])
+    for name in ("yt", "filt", "fedge"):
+        copies[name].wait()
     for q in range(2):
         high, low = halves(along_y(yt, 3, q))
         warm[16 * q : 16 * q + 16, :] = (
@@ -389,12 +404,13 @@
             + mm(high[:, 256:], fedge[q])
             + mm(low[:, 256:], fedge[q])
         )
+    copies["ref"].wait()
     vel[...] = mm(y_high[...], ref[...]) + mm(y_low[...], ref[...])
     vel[:, :128] += side[:, :128]
     vel[:, FINE - 128 :] += side[:, 128:]
 
-    west_t = west[0].T
-    east_t = east[0].T
+    west_t = edge_cols[(me[0] + G - 1) % G, 32:40, :].T
+    east_t = edge_cols[(me[0] + 1) % G, 32:40, :].T
     last_row = iota((8, FINE), 0) == 7
     first_row = iota((8, FINE), 0) == 0
     last_lane = lane_id == 127
@@ -404,6 +420,8 @@
         line = jnp.concatenate([rows[16 + 8 * j + l : 17 + 8 * j + l, :] for j in range(4)], 1)
         return jnp.broadcast_to(line, (8, FINE))
 
+    rates.wait()
+    stores = []
     for yb in range(8):
         ys = slice(8 * yb, 8 * yb + 8)
         for q in range(2):
@@ -434,51 +452,48 @@
                     + k * (((e + w) + (north + south)) + (upper + lower) - 6.0 * c)
                     - (vx * (e - w) + vy * (north - south) + vz * (upper - lower))
                 )
-                out[l, ys, :] = new
+                new_sal[l, ys, :] = new
                 acc = new if acc is None else acc + new
             total[64 * q + 8 * yb : 64 * q + 8 * yb + 8, :] = acc
+        stores.append(pltpu.make_async_copy(new_sal.at[:, ys, :], out.at[:, ys, :], out_sems.at[yb]))
+        stores[-1].start()
+    copies["cm"].wait()
+    copies["rm"].wait()
     high, low = halves(total[...])
     high, low = halves(mm(high, cm[...]) + mm(low, cm[...]))
     mean = warm[...] - mm(rm[...], jnp.concatenate([high, low], 0))
     for a in range(G):
         spread[a] = mean
-
-
-def fine(pos, recv1, recv2, salinity, zlow, zhigh, from_south, from_north, rate):
-    t = tables()
-    whole = lambda x: pl.BlockSpec(x.shape, lambda i, m, n=x.ndim: (0,) * n)
-    consts = [jnp.asarray(t[name]) for name in ("ym", "yt", "ref", "edge", "filt", "fedge", "cm", "rm")]
-    recv2 = recv2.reshape(512, 128)
-    arrays = [recv2, salinity, zlow, zhigh, from_south, from_north]
-    near = lambda step: pl.BlockSpec((1, 8, 128), lambda i, m: ((m[1] + step) % G, 4, 0))
+    for store in stores:
+        store.wait()
+
+
+def fine(me, grp, recv1, recv2, salinity, zlow, zhigh, from_south, from_north, rate):
+    consts = [jnp.asarray(tables()[name]) for name in CONSTS]
+    arrays = [recv2.reshape(512, 128), recv1, salinity, zlow, zhigh, from_south, from_north]
     return call(
         fine_kernel,
         (sds(8, 64, FINE), sds(G, 32, 256)),
-        grid_spec=pltpu.PrefetchScalarGridSpec(
-            num_scalar_prefetch=1,
-            grid=(1,),
-            in_specs=[whole(x) for x in arrays]
-            + [near(G - 1), near(1), pl.BlockSpec(memory_space=pltpu.SMEM)]
-            + [whole(x) for x in consts],
-            out_specs=[
-                pl.BlockSpec((8, 64, FINE), lambda i, m: (0, 0, 0)),
-                pl.BlockSpec((G, 32, 256), lambda i, m: (0, 0, 0)),
-            ],
-            scratch_shapes=[
-                pltpu.VMEM((384, 256), BF16),
-                pltpu.VMEM((384, 256), BF16),
-                pltpu.VMEM((384, 256), F32),
-                pltpu.VMEM((384, FINE), F32),
-                pltpu.VMEM((128, FINE), F32),
-                pltpu.VMEM((32, 256), F32),
-            ],
-        ),
+        [SM, SM, HB] + [VM] * len(arrays) + [HB] * len(consts),
+        [HB, VM],
+        scratch_shapes=[
+            pltpu.VMEM((384, 256), BF16),
+            pltpu.VMEM((384, 256), BF16),
+            pltpu.VMEM((384, 256), F32),
+            pltpu.VMEM((384, FINE), F32),
+            pltpu.VMEM((128, FINE), F32),
+            pltpu.VMEM((32, 256), F32),
+            pltpu.VMEM((8, 64, FINE), F32),
+        ]
+        + [pltpu.VMEM(x.shape, x.dtype) for x in consts]
+        + [pltpu.SMEM((8,), F32), pltpu.SemaphoreType.DMA((len(consts) + 1,)), pltpu.SemaphoreType.DMA((8,))],
+        limit=24,
         name="fine",
-    )(pos, *arrays, recv1, recv1, rate, *consts)
-
-
-def table_kernel(pos, base, high, low):
-    turns = (iota((16, 128), 0) * pos[1]) % G
+    )(me, grp, rate, *arrays, *consts)
+
+
+def table_kernel(me, base, high, low):
+    turns = (iota((16, 128), 0) * me[0]) % G
     angle = turns.astype(F32) * (2.0 * math.pi / G)
     cos = jnp.concatenate([jnp.cos(angle)] * 2, 1)
     sin = -jnp.concatenate([jnp.sin(angle)] * 2, 1)
@@ -489,19 +504,18 @@
             high[rows, at : at + 256], low[rows, at : at + 256] = halves(value)
 
 
-def table(pos):
-    whole = pl.BlockSpec((256, 512), lambda i, m: (0, 0))
+def table(me):
     return call(
         table_kernel,
         (sds(256, 512, dtype=BF16), sds(256, 512, dtype=BF16)),
-        grid_spec=pltpu.PrefetchScalarGridSpec(
-            num_scalar_prefetch=1, grid=(1,), in_specs=[whole], out_specs=[whole, whole]
-        ),
+        [SM, VM],
+        [VM, VM],
         name="table",
-    )(pos, jnp.asarray(tables()["fwd"]))
-
-
-def forward_kernel(recv, table_high, table_low, comb_cos, comb_sin, out, left_high, left_low, mid):
+    )(me, jnp.asarray(tables()["fwd"]))
+
+
+def forward_kernel(recv, table_high, table_low, cos_hbm, sin_hbm, out, left_high, left_low, mid, comb_cos, comb_sin, sems):
+    copies = fetch(((cos_hbm, comb_cos), (sin_hbm, comb_sin)), sems)
     for a in range(G):
         high, low = halves(recv[a])
         left_high[32 * a : 32 * a + 32, :] = high
@@ -509,6 +523,8 @@
     mid[...] = (
         mm(left_high[...], table_high[...]) + mm(left_low[...], table_high[...]) + mm(left_high[...], table_low[...])
     )
+    for copy in copies:
+        copy.wait()
     real = imag = jnp.zeros((32, 256), F32)
     for a in range(G):
         c, s = comb_cos[a : a + 1, :], comb_sin[a : a + 1, :]
@@ -525,44 +541,65 @@
     return call(
         forward_kernel,
         sds(4, 64, 256),
+        [VM, VM, VM, HB, HB],
+        VM,
         scratch_shapes=[
             pltpu.VMEM((512, 256), BF16),
             pltpu.VMEM((512, 256), BF16),
             pltpu.VMEM((512, 512), F32),
+            pltpu.VMEM((G, 256), F32),
+            pltpu.VMEM((G, 256), F32),
+            pltpu.SemaphoreType.DMA((2,)),
         ],
         name="forward",
     )(recv, high, low, cos, sin)
 
 
+def finish_kernel(me, viscosity, gain, recv, modes, out):
+    index = me[0] * W + iota((8, W), 1)
+    number = jnp.where(index < NV // 2, index, index - NV).astype(F32)
+    wave = (2.0 * math.pi / NV) * number
+    damping = jnp.exp(-viscosity[0] * wave * wave)[0:1, :]
+    for c in range(2):
+        for g in range(4):
+            at = slice(128 * c + 32 * g, 128 * c + 32 * g + 32)
+            out[at, :] = damping * modes[at, :] + gain[0] * recv[g, 32 * c : 32 * c + 32, :]
+
+
+def finish(me, viscosity, gain, recv, modes):
+    return call(finish_kernel, sds(256, W), [SM, SM, SM, VM, VM], VM, name="finish")(
+        me, viscosity, gain, recv, modes
+    )
+
+
 def shifted(array, axis, step):
     count = lax.axis_size(axis)
     return lax.ppermute(array, axis, [(i, (i + step) % count) for i in range(count)])
 
 
 def per_device(coarse_modes, salinity, viscosity, forcing_gain, diffusivity):
-    me = lax.axis_index(GX).astype(jnp.int32)
-    pos = jnp.stack([lax.axis_index("grp").astype(jnp.int32), me])
+    me = lax.axis_index(GX).astype(jnp.int32).reshape(1)
+    grp = lax.axis_index("grp").astype(jnp.int32).reshape(1)
     modes = coarse_modes.reshape(256, 256)
-    chunk, up, down, low_face, high_face = edges(pos[1:], modes, salinity)
+    chunk, up, down, low_face, high_face = edges(me, modes, salinity)
+    zlow = shifted(high_face, "grp", 1)
+    zhigh = shifted(low_face, "grp", -1)
     from_south = shifted(up, "gy", 1)
     from_north = shifted(down, "gy", -1)
-    zlow = shifted(high_face, "grp", 1)
-    zhigh = shifted(low_face, "grp", -1)
+    weights = table(me)
+    from_south, from_north, zlow, zhigh, weights = lax.optimization_barrier(
+        (from_south, from_north, zlow, zhigh, weights)
+    )
     chunk = tails(chunk, from_south, from_north)
     recv1 = lax.all_to_all(chunk, GX, 0, 0, tiled=True)
     recv2 = lax.all_to_all(inverse(recv1), GRP_GX, 0, 0, tiled=True)
     salinity_next, spread = fine(
-        pos, recv1, recv2, salinity, zlow, zhigh, from_south, from_north, diffusivity
+        me, grp, recv1, recv2, salinity, zlow, zhigh, from_south, from_north, diffusivity
     )
     recv3 = lax.all_to_all(spread, GX, 0, 0, tiled=True)
-    recv4 = lax.all_to_all(forward(recv3, *table(pos)), "grp", 0, 0, tiled=True)
-    spectrum = recv4.reshape(4, 2, 2, 16, W).transpose(1, 0, 2, 3, 4).reshape(2, 8, 16, W)
-    mode_index = me * W + lax.broadcasted_iota(jnp.int32, (W,), 0)
-    wavenumber = jnp.where(mode_index < NV // 2, mode_index, mode_index - NV)
-    scaled_wave = 2.0 * math.pi / NV * wavenumber.astype(F32)
-    damping = jnp.exp(-viscosity[0] * scaled_wave * scaled_wave)
-    coarse_next = damping * coarse_modes + forcing_gain[0] * spectrum[None]
-    return (salinity_next, coarse_next)
+    recv4 = lax.all_to_all(forward(recv3, *weights), "grp", 0, 0, tiled=True)
+    coarse_next = finish(me, viscosity, forcing_gain, recv4, modes)
+    return (salinity_next, coarse_next.reshape(coarse_modes.shape))
 
 
 def solution(mesh):

time: 107 us -> 96.4 us (0.901)
  blocking collectives: 24 us -> 41.2 us
  local copies, waits for them, and re-layouts: 12.9 us -> 0.83 us
  waiting for transfers between devices: 31.8 us -> 22.9 us
  starting transfers between devices: 24.3 us -> 15.7 us
  Pallas kernels: 9.97 us -> 13.1 us
  other arithmetic: 1.36 us -> 0 us
    all_to_all x0 -> x1, blocking collectives: none -> 18.2 us  [per_device(): recv3 = lax.all_to_all(spread, GX, 0, 0, tiled=True)]
    all_to_all x2 -> x1, waiting for transfers between devices: 19.2 us -> 5.35 us  [per_device(): recv4 = lax.all_to_all(forward(recv3, *weights), 'grp', 0, 0, tiled=True)]
    unnamed x54 -> x14, local copies, waits for them, and re-layouts: 12.9 us -> 0.83 us
    all_to_all x1, waiting for transfers between devices: 2.97 us -> 13.5 us  [per_device(): recv2 = lax.all_to_all(inverse(recv1), GRP_GX, 0, 0, tiled=True)]
    all_to_all x2 -> x1, starting transfers between devices: 10.2 us -> 3.42 us  [per_device(): recv4 = lax.all_to_all(forward(recv3, *weights), 'grp', 0, 0, tiled=True)]
    ppermute x4, waiting for transfers between devices: 9.69 us -> 4.08 us  [shifted(): lax.ppermute(array, axis, [(i, (i + step) % count) for i in range(count)])]
    pallas_call x6 -> x7, Pallas kernels: 9.97 us -> 13.1 us  [placed(): inner(*[x if spec is not HB else pltpu.with_memory_space_constraint(x, pl...]
    all_to_all x1, starting transfers between devices: 8.98 us -> 7.26 us  [per_device(): recv2 = lax.all_to_all(inverse(recv1), GRP_GX, 0, 0, tiled=True)]
  transfers between devices with their start and end apart: 7 -> 6, of which waited for: 5 -> 4; matrix products, arithmetic and copies ran while one was open for 1% -> 0% of each run, Pallas kernels for 1% -> 0%
where the time goes in v2:
time: 96.4 us; the launch traced here: 95.9 us
  blocking collectives  41.2 us (43%)
  waiting for transfers between devices  22.9 us (24%)
  starting transfers between devices  15.7 us (16%)
  Pallas kernels  13.1 us (14%)
  between operations  2.04 us (2%)
    all_to_all x1, blocking collectives, per_device(): recv1 = lax.all_to_all(chunk, GX, 0, 0, tiled=True)  23 us
    all_to_all x1, blocking collectives, per_device(): recv3 = lax.all_to_all(spread, GX, 0, 0, tiled=True)  18.2 us
    all_to_all x1, waiting for transfers between devices, per_device(): recv2 = lax.all_to_all(inverse(recv1), GRP_GX, 0, 0, tiled=True)  13.5 us
    pallas_call x7, Pallas kernels, placed(): inner(*[x if spec is not HB else pltpu.with_memory_space_constraint(x, pl...  13.1 us
    all_to_all x1, starting transfers between devices, per_device(): recv2 = lax.all_to_all(inverse(recv1), GRP_GX, 0, 0, tiled=True)  7.26 us
    all_to_all x1, waiting for transfers between devices, per_device(): recv4 = lax.all_to_all(forward(recv3, *weights), 'grp', 0, 0, tiled=True)  5.35 us
    ppermute x4, starting transfers between devices, shifted(): lax.ppermute(array, axis, [(i, (i + step) % count) for i in range(count)])  5.06 us
    ppermute x4, waiting for transfers between devices, shifted(): lax.ppermute(array, axis, [(i, (i + step) % count) for i in range(count)])  4.08 us
  transfers between devices with their start and end apart: 6, of which 4 were waited for; matrix products, arithmetic and copies ran while one was open for 0% of the time, Pallas kernels for 0%

profile of v2, /device:TPU:32, one launch (start us, length us, event | category | flops | bytes accessed | tf_op | source)
XLA Modules:
  0.0 95.9 jit_solution(6396394930080011025)
XLA Ops:
  0.6 0.0 copy-start.2
  0.6 1.6 %edges.1 = (f32[16,40,128]{2,1,0:T(8,128)S(1)}, f32[48,256]{1,0:T(8,128)S(1)}, f32[48,256]{1,0:T(8,128)S(1)}, f32[64,1024]{1,0:T(8,128)S(1)}, f32[64,1024]{1,0:T(8,128)S(1)}) custom-call(s32[1]{0:T(128)} %bitcast.me, f32[256,256]{1,0:T(8,128)} %bitcast.5, f32[8,64,1024]{2,1,0:T(8,128)} %salinity.1), custom_call_target="tpu_custom_call" | custom-call | tf_op jit(solution)/shard_map/edges/pallas_call | solution.py:121
  2.3 0.0 copy-start
  2.3 1.6 %collective-permute-start.2 = (f32[64,1024]{1,0:T(8,128)S(1)}, f32[64,1024]{1,0:T(8,128)S(1)}, u32[]{:S(2)}, u32[]{:S(2)}) collective-permute-start(f32[64,1024]{1,0:T(8,128)S(1)} %get-tuple-element.20), channel_id=1, source_target_pairs={{0,64},{64,128},{128,192},{192,0},{1,65},{65,129},{129,193},{193,1... | collective-permute-start | bytes 786440 | tf_op jit(solution)/shard_map/ppermute | solution.py:577
  3.9 1.7 %collective-permute-start.3 = (f32[64,1024]{1,0:T(8,128)S(1)}, f32[64,1024]{1,0:T(8,128)S(1)}, u32[]{:S(2)}, u32[]{:S(2)}) collective-permute-start(f32[64,1024]{1,0:T(8,128)S(1)} %get-tuple-element.21), channel_id=1, source_target_pairs={{0,192},{64,0},{128,64},{192,128},{1,193},{65,1},{129,65},{193,129... | collective-permute-start | bytes 786440 | tf_op jit(solution)/shard_map/ppermute | solution.py:577
  5.6 0.0 collective-permute-start
  5.6 1.7 %collective-permute-start.1 = (f32[48,256]{1,0:T(8,128)S(1)}, f32[48,256]{1,0:T(8,128)S(1)}, u32[]{:S(2)}, u32[]{:S(2)}) collective-permute-start(f32[48,256]{1,0:T(8,128)S(1)} %get-tuple-element.19), channel_id=1, source_target_pairs={{0,3},{1,0},{2,1},{3,2},{4,7},{5,4},{6,5},{7,6},{8,11},{9,8},{10,9... | collective-permute-start | bytes 147464 | tf_op jit(solution)/shard_map/ppermute | solution.py:577
  7.4 0.2 table.1
  7.5 1.6 %collective-permute-done.from_south = f32[48,256]{1,0:T(8,128)S(1)} collective-permute-done((f32[48,256]{1,0:T(8,128)S(1)}, f32[48,256]{1,0:T(8,128)S(1)}, u32[]{:S(2)}, u32[]{:S(2)}) %collective-permute-start) | collective-permute-done | bytes 49184 | tf_op jit(solution)/shard_map/ppermute | solution.py:577
  9.1 0.0 collective-permute-done.1.from_north
  9.1 2.5 %collective-permute-done.2.zlow = f32[64,1024]{1,0:T(8,128)S(1)} collective-permute-done((f32[64,1024]{1,0:T(8,128)S(1)}, f32[64,1024]{1,0:T(8,128)S(1)}, u32[]{:S(2)}, u32[]{:S(2)}) %collective-permute-start.2) | collective-permute-done | bytes 262176 | tf_op jit(solution)/shard_map/ppermute | solution.py:577
  11.6 0.0 collective-permute-done.3.zhigh
  11.7 23.0 %all_to_all.20.recv.edge_cols = f32[16,40,128]{2,1,0:T(8,128)S(1)} all-to-all(f32[16,40,128]{2,1,0:T(8,128)S(1)} %tails.1), channel_id=1, replica_groups=mesh['grp'=4,'gx_0'=2,'gx_1'=8,'gy'=4] {'gx_0','gx_1'}, dimensions={0} | all-to-all | bytes 655360 | tf_op jit(solution)/shard_map/all_to_all | solution.py:594
  34.7 2.6 %inverse.1 = f32[64,8,128]{2,1,0:T(8,128)} custom-call(f32[16,40,128]{2,1,0:T(8,128)S(1)} %all_to_all.20.recv.edge_cols, f32[16,8,128]{2,1,0:T(8,128)} %constant.50.clone.twc_hbm, f32[16,8,128]{2,1,0:T(8,128)} %constant.51.clone.tws_hbm, bf16[512,256]{1,0:T(8,128)(2,1)} %constant.52.clone.high_hbm, bf16[512,256]{1,0:T(8,128)(2,1)} %constant.53.clone.low_hbm), custom_call_target="tpu_custom_call" | custom-call | tf_op jit(solution)/shard_map/inverse/pallas_call | solution.py:121
  37.3 7.3 %all-to-all-start.1 = ((f32[64,8,128]{2,1,0:T(8,128)}), f32[64,8,128]{2,1,0:T(8,128)S(1)}, u32[]{:S(2)}, u32[]{:S(2)}) async-start(f32[64,8,128]{2,1,0:T(8,128)} %inverse.1), calls=%async_computation.1 | async-start | bytes 524288 | tf_op jit(solution)/shard_map/all_to_all | solution.py:595
  44.6 13.5 %all-to-all-done.1 = f32[64,8,128]{2,1,0:T(8,128)S(1)} async-done(((f32[64,8,128]{2,1,0:T(8,128)}), f32[64,8,128]{2,1,0:T(8,128)S(1)}, u32[]{:S(2)}, u32[]{:S(2)}) %all-to-all-start.1) | async-done | bytes 262176 | tf_op jit(solution)/shard_map/all_to_all | solution.py:595
  58.1 0.8 copy-done.6
  58.9 6.1 %fine.1 = (f32[8,64,1024]{2,1,0:T(8,128)}, f32[16,32,256]{2,1,0:T(8,128)S(1)}) custom-call(s32[1]{0:T(128)} %bitcast.me, s32[1]{0:T(128)} %bitcast.1.grp_ref, f32[8]{0:T(128)} %rate_hbm.1, f32[512,128]{1,0:T(8,128)S(1)} %bitcast.7, f32[16,40,128]{2,1,0:T(8,128)S(1)} %all_to_all.20.recv.edge_cols, f32[8,64,1024]{2,1,0:T(8,128)S(1)} %copy-done, ...), custom_call_target="tpu_custom_call" | custom-call | tf_op jit(solution)/shard_map/fine/pallas_call | solution.py:121
  65.0 0.0 copy-start.1
  65.0 18.2 %all_to_all.21.recv = f32[16,32,256]{2,1,0:T(8,128)S(1)} all-to-all(f32[16,32,256]{2,1,0:T(8,128)S(1)} %get-tuple-element.29), channel_id=1, replica_groups=mesh['grp'=4,'gx_0'=2,'gx_1'=8,'gy'=4] {'gx_0','gx_1'}, dimensions={0} | all-to-all | bytes 1048576 | tf_op jit(solution)/shard_map/all_to_all | solution.py:599
  83.2 1.9 %forward.1 = f32[4,64,256]{2,1,0:T(8,128)} custom-call(f32[16,32,256]{2,1,0:T(8,128)S(1)} %all_to_all.21.recv, bf16[256,512]{1,0:T(8,128)(2,1)S(1)} %get-tuple-element.30.table_high, bf16[256,512]{1,0:T(8,128)(2,1)S(1)} %copy-done.4, f32[16,256]{1,0:T(8,128)} %constant.62.clone.cos_hbm, f32[16,256]{1,0:T(8,128)} %constant.63.clone.sin_hbm), custom_call_target="tpu_custom_call" | custom-call | tf_op jit(solution)/shard_map/forward/pallas_call | solution.py:121
  85.0 3.4 %all-to-all-start.3 = ((f32[4,64,256]{2,1,0:T(8,128)}), f32[4,64,256]{2,1,0:T(8,128)S(1)}, u32[]{:S(2)}, u32[]{:S(2)}) async-start(f32[4,64,256]{2,1,0:T(8,128)} %forward.1), calls=%async_computation.3 | async-start | bytes 524288 | tf_op jit(solution)/shard_map/all_to_all | solution.py:600
  89.8 5.3 %all-to-all-done.3.recv = f32[4,64,256]{2,1,0:T(8,128)S(1)} async-done(((f32[4,64,256]{2,1,0:T(8,128)}), f32[4,64,256]{2,1,0:T(8,128)S(1)}, u32[]{:S(2)}, u32[]{:S(2)}) %all-to-all-start.3) | async-done | bytes 262176 | tf_op jit(solution)/shard_map/all_to_all | solution.py:600
  95.1 0.7 finish.1
  (11 shorter events, 0.1 us)
Async XLA Ops:
  0.6 6.7 %copy-start.2 = (f32[256,512]{1,0:T(8,128)S(1)}, f32[256,512]{1,0:T(8,128)}, u32[]{:S(2)}) copy-start(f32[256,512]{1,0:T(8,128)} %constant.49.clone.base) | copy-start | bytes 1572868
  2.3 55.8 %copy-start = (f32[8,64,1024]{2,1,0:T(8,128)S(1)}, f32[8,64,1024]{2,1,0:T(8,128)}, u32[]{:S(2)}) copy-start(f32[8,64,1024]{2,1,0:T(8,128)} %salinity.1) | copy-start | bytes 6291460
  2.3 9.3 %collective-permute-start.2 = (f32[64,1024]{1,0:T(8,128)S(1)}, f32[64,1024]{1,0:T(8,128)S(1)}, u32[]{:S(2)}, u32[]{:S(2)}) collective-permute-start(f32[64,1024]{1,0:T(8,128)S(1)} %get-tuple-element.20), channel_id=1, source_target_pairs={{0,64},{64,128},{128,192},{192,0},{1,65},{65,129},{129,193},{193,1... | collective-permute-start | bytes 786440 | tf_op jit(solution)/shard_map/ppermute | solution.py:577
  3.9 7.8 %collective-permute-start.3 = (f32[64,1024]{1,0:T(8,128)S(1)}, f32[64,1024]{1,0:T(8,128)S(1)}, u32[]{:S(2)}, u32[]{:S(2)}) collective-permute-start(f32[64,1024]{1,0:T(8,128)S(1)} %get-tuple-element.21), channel_id=1, source_target_pairs={{0,192},{64,0},{128,64},{192,128},{1,193},{65,1},{129,65},{193,129... | collective-permute-start | bytes 786440 | tf_op jit(solution)/shard_map/ppermute | solution.py:577
  5.6 3.5 %collective-permute-start = (f32[48,256]{1,0:T(8,128)S(1)}, f32[48,256]{1,0:T(8,128)S(1)}, u32[]{:S(2)}, u32[]{:S(2)}) collective-permute-start(f32[48,256]{1,0:T(8,128)S(1)} %get-tuple-element.18), channel_id=1, source_target_pairs={{0,1},{1,2},{2,3},{3,0},{4,5},{5,6},{6,7},{7,4},{8,9},{9,10},{10,1... | collective-permute-start | bytes 147464 | tf_op jit(solution)/shard_map/ppermute | solution.py:577
  5.6 3.5 %collective-permute-start.1 = (f32[48,256]{1,0:T(8,128)S(1)}, f32[48,256]{1,0:T(8,128)S(1)}, u32[]{:S(2)}, u32[]{:S(2)}) collective-permute-start(f32[48,256]{1,0:T(8,128)S(1)} %get-tuple-element.19), channel_id=1, source_target_pairs={{0,3},{1,0},{2,1},{3,2},{4,7},{5,4},{6,5},{7,6},{8,11},{9,8},{10,9... | collective-permute-start | bytes 147464 | tf_op jit(solution)/shard_map/ppermute | solution.py:577
  7.5 27.2 %copy-start.3 = (bf16[256,512]{1,0:T(8,128)(2,1)}, bf16[256,512]{1,0:T(8,128)(2,1)S(1)}, u32[]{:S(2)}) copy-start(bf16[256,512]{1,0:T(8,128)(2,1)S(1)} %get-tuple-element.31.table_low) | copy-start | bytes 786436
  9.1 28.2 %copy-start.5 = (f32[48,256]{1,0:T(8,128)}, f32[48,256]{1,0:T(8,128)S(1)}, u32[]{:S(2)}) copy-start(f32[48,256]{1,0:T(8,128)S(1)} %collective-permute-done.1.from_north) | copy-start | bytes 147460
  37.3 20.8 %all-to-all-start.1 = ((f32[64,8,128]{2,1,0:T(8,128)}), f32[64,8,128]{2,1,0:T(8,128)S(1)}, u32[]{:S(2)}, u32[]{:S(2)}) async-start(f32[64,8,128]{2,1,0:T(8,128)} %inverse.1), calls=%async_computation.1 | async-start | bytes 524288 | tf_op jit(solution)/shard_map/all_to_all | solution.py:595
  58.1 0.8 copy-start.6
  58.9 24.3 %copy-start.4 = (bf16[256,512]{1,0:T(8,128)(2,1)S(1)}, bf16[256,512]{1,0:T(8,128)(2,1)}, u32[]{:S(2)}) copy-start(bf16[256,512]{1,0:T(8,128)(2,1)} %copy-done.3) | copy-start | bytes 786436
  65.0 30.1 %copy-start.1 = (f32[1,2,8,16,256]{4,3,2,1,0:T(8,128)S(1)}, f32[1,2,8,16,256]{4,3,2,1,0:T(8,128)}, u32[]{:S(2)}) copy-start(f32[1,2,8,16,256]{4,3,2,1,0:T(8,128)} %param.20) | copy-start | bytes 786436
  85.0 10.1 %all-to-all-start.3 = ((f32[4,64,256]{2,1,0:T(8,128)}), f32[4,64,256]{2,1,0:T(8,128)S(1)}, u32[]{:S(2)}, u32[]{:S(2)}) async-start(f32[4,64,256]{2,1,0:T(8,128)} %forward.1), calls=%async_computation.3 | async-start | bytes 524288 | tf_op jit(solution)/shard_map/all_to_all | solution.py:600

commit v3 on v2

--- a/solution.py
+++ b/solution.py
@@ -78,15 +78,22 @@
         yt[c, place(c + 1)] += 0.125
     out["ym"] = np.concatenate([ym, ym], 1).astype(jnp.bfloat16)
     out["yt"] = np.concatenate([yt, yt], 1).astype(jnp.bfloat16)
-    cm = np.zeros((FINE, W))
-    cm[np.arange(FINE), np.arange(FINE) // 4] = 1.0 / 4
+    cm = np.zeros((512, 128))
+    cm[np.arange(512), np.arange(512) // 4] = 1.0 / 4
     out["cm"] = cm.astype(jnp.bfloat16)
     rm = np.zeros((32, 128))
     rm[np.arange(128) // 4, np.arange(128)] = 1.0 / 16
     out["rm"] = np.concatenate([rm, rm], 1).astype(jnp.bfloat16)
     g = np.arange(G)
-    angle = 2 * np.pi * np.outer(k, k) / NV
-    out["fwd"] = (np.concatenate([np.cos(angle), -np.sin(angle)], 1) * norm).astype(np.float32)
+    fine_angle = 2 * np.pi * np.outer(g, k) / NV
+    coarse_angle = 2 * np.pi * (np.outer(g, k) % W) / W
+    out["fwd"] = tuple(
+        x.astype(np.float32)
+        for x in (
+            np.concatenate([np.cos(fine_angle), -np.sin(fine_angle)], 1) * norm,
+            np.concatenate([np.cos(coarse_angle), -np.sin(coarse_angle)], 1),
+        )
+    )
     angle = 2 * np.pi * (np.outer(g, k) % G) / G
     out["comb"] = (np.cos(angle).astype(np.float32), np.sin(angle).astype(np.float32))
     return out
@@ -136,6 +143,14 @@
     return jax.ShapeDtypeStruct(shape, dtype)
 
 
+def vds(*shape, dtype=F32):
+    return pltpu.VMEM(shape, dtype)
+
+
+def hds(*shape, dtype=F32):
+    return pltpu.HBM(shape, dtype)
+
+
 def iota(shape, dim):
     return lax.broadcasted_iota(jnp.int32, shape, dim)
 
@@ -144,28 +159,55 @@
     return pltpu.roll(x, shift % x.shape[axis], axis)
 
 
-def edges_kernel(me, modes, sal, chunk, up, down, zlow, zhigh, modes_a, modes_b, south, north, west, east, sems):
+def lines_kernel(modes, sal, up, down, ends, south, north, sems):
+    copies = fetch(
+        (
+            (modes.at[:, 0:8, :], ends.at[0]),
+            (modes.at[:, 8:16, :], ends.at[1]),
+            (sal.at[:, 0:8, :], south),
+            (sal.at[:, 56:64, :], north),
+        ),
+        sems,
+    )
+    for copy in copies:
+        copy.wait()
+    for dst, rows, end, row in ((up, north, 1, 7), (down, south, 0, 0)):
+        dst[0:16, :] = ends[end, :, row, :]
+        face = rows[:, row, :]
+        for j in range(4):
+            dst[16 + 8 * j : 24 + 8 * j, :] = face[:, 256 * j : 256 * j + 256]
+
+
+def outer_lines(modes, salinity):
+    return call(
+        lines_kernel,
+        (vds(48, 256), vds(48, 256)),
+        [HB, HB],
+        [VM, VM],
+        scratch_shapes=[
+            pltpu.VMEM((2, 16, 8, 256), F32),
+            pltpu.VMEM((8, 8, FINE), F32),
+            pltpu.VMEM((8, 8, FINE), F32),
+            pltpu.SemaphoreType.DMA((4,)),
+        ],
+        name="outer_lines",
+    )(modes.reshape(16, 16, 256), salinity)
+
+
+def pack_kernel(me, modes, sal, chunk, low_face, high_face, modes_a, modes_b, west, east, sems):
     copies = fetch(
         (
             (modes.at[:, 0:128], modes_a),
             (modes.at[:, 128:256], modes_b),
-            (sal.at[:, 0:8, :], south),
-            (sal.at[:, 56:64, :], north),
             (sal.at[:, :, 0:128], west),
             (sal.at[:, :, FINE - 128 :], east),
-            (sal.at[0], zlow),
-            (sal.at[7], zhigh),
+            (sal.at[0], low_face),
+            (sal.at[7], high_face),
         ),
         sems,
     )
-    for copy in copies[:4]:
+    for copy in copies[:2]:
         copy.wait()
-    for dst, rows, row, line in ((up, north, 7, 15), (down, south, 0, 0)):
-        dst[0:16, :128] = modes_a[pl.ds(line, 16, stride=16), :]
-        dst[0:16, 128:] = modes_b[pl.ds(line, 16, stride=16), :]
-        face = rows[:, row, :]
-        for j in range(4):
-            dst[16 + 8 * j : 24 + 8 * j, :] = face[:, 256 * j : 256 * j + 256]
     zero = jnp.zeros((8, 128), F32)
     for r in range(G):
         chunk[r, 0:16, :] = modes_a[pl.ds(r, 16, stride=16), :]
@@ -181,30 +223,28 @@
             tile = jnp.where(row_id == 4 + i, line, tile)
         return tile
 
-    for copy in copies[4:6]:
+    for copy in copies[2:4]:
         copy.wait()
     chunk[(me[0] + 1) % G, 32:40, :] = column(east, 127)
     chunk[(me[0] + G - 1) % G, 32:40, :] = column(west, 0)
-    for copy in copies[6:]:
+    for copy in copies[4:]:
         copy.wait()
 
 
-def edges(me, modes, salinity):
+def pack(me, modes, salinity):
     return call(
-        edges_kernel,
-        (sds(G, 40, 128), sds(48, 256), sds(48, 256), sds(64, FINE), sds(64, FINE)),
+        pack_kernel,
+        (vds(G, 40, 128), hds(64, FINE), hds(64, FINE)),
         [SM, HB, HB],
-        [VM, VM, VM, HB, HB],
+        [VM, HB, HB],
         scratch_shapes=[
             pltpu.VMEM((256, 128), F32),
             pltpu.VMEM((256, 128), F32),
-            pltpu.VMEM((8, 8, FINE), F32),
-            pltpu.VMEM((8, 8, FINE), F32),
             pltpu.VMEM((8, 64, 128), F32),
             pltpu.VMEM((8, 64, 128), F32),
-            pltpu.SemaphoreType.DMA((8,)),
+            pltpu.SemaphoreType.DMA((6,)),
         ],
-        name="edges",
+        name="pack",
     )(me, modes, salinity)
 
 
@@ -255,11 +295,7 @@
     return out
 
 
-def inverse_kernel(recv, twc_hbm, tws_hbm, high_hbm, low_hbm, send, left_high, left_low, mid, twc, tws, inv_high, inv_low, sems):
-    copies = fetch(((twc_hbm, twc), (tws_hbm, tws), (high_hbm, inv_high), (low_hbm, inv_low)), sems)
-    for copy in copies[:2]:
-        copy.wait()
-
+def inverse_kernel(recv, twc, tws, inv_high, inv_low, send, left_high, left_low, mid):
     row_id = iota((8, 128), 0)
     lane_id = iota((8, 128), 1)
 
@@ -284,8 +320,6 @@
             put(r, 1, part, jnp.where(row_id == 0, value, 0.0))
             put(r, 1, part + 1, jnp.where(row_id == 0, roll(value, -1, 0), 0.0))
 
-    for copy in copies[2:]:
-        copy.wait()
     mid[...] = (
         mm(left_high[...], inv_high[...]) + mm(left_low[...], inv_high[...]) + mm(left_high[...], inv_low[...])
     )
@@ -332,37 +366,102 @@
             send[16 * g + d] = tile
 
 
-def inverse(recv):
-    t = tables()
-    twc, tws = map(jnp.asarray, t["tw"])
-    high, low = map(jnp.asarray, t["inv"])
+def inverse(recv, twc, tws, high, low):
     return call(
         inverse_kernel,
         sds(64, 8, 128),
-        [VM, HB, HB, HB, HB],
+        [VM] * 5,
         VM,
         scratch_shapes=[
             pltpu.VMEM((256, 512), BF16),
             pltpu.VMEM((256, 512), BF16),
             pltpu.VMEM((256, 256), F32),
-            pltpu.VMEM((G, 8, 128), F32),
-            pltpu.VMEM((G, 8, 128), F32),
-            pltpu.VMEM((512, 256), BF16),
-            pltpu.VMEM((512, 256), BF16),
-            pltpu.SemaphoreType.DMA((4,)),
         ],
         name="inverse",
     )(recv, twc, tws, high, low)
 
 
+def still_kernel(me, rate_hbm, sal_hbm, zlow_hbm, zhigh_hbm, edge_cols, from_south, from_north, parts_hbm, rate, salinity, zlow, zhigh, parts, sems, out_sems):
+    copies = fetch(((rate_hbm, rate), (sal_hbm, salinity), (zlow_hbm, zlow), (zhigh_hbm, zhigh)), sems)
+    west_t = edge_cols[(me[0] + G - 1) % G, 32:40, :].T
+    east_t = edge_cols[(me[0] + 1) % G, 32:40, :].T
+    last_row = iota((8, FINE), 0) == 7
+    first_row = iota((8, FINE), 0) == 0
+    last_lane = iota((8, 128), 1) == 127
+    first_lane = iota((8, 128), 1) == 0
+
+    def outer(rows, l):
+        line = jnp.concatenate([rows[16 + 8 * j + l : 17 + 8 * j + l, :] for j in range(4)], 1)
+        return jnp.broadcast_to(line, (8, FINE))
+
+    for copy in copies:
+        copy.wait()
+    stores = []
+    for yb in range(8):
+        ys = slice(8 * yb, 8 * yb + 8)
+        for l in range(8):
+            c = salinity[l, ys, :]
+            upper = salinity[l + 1, ys, :] if l < 7 else zhigh[ys, :]
+            lower = salinity[l - 1, ys, :] if l > 0 else zlow[ys, :]
+            if yb < 7:
+                north = salinity[l, 8 * yb + 1 : 8 * yb + 9, :]
+            else:
+                north = jnp.where(last_row, outer(from_north, l), roll(c, -1, 0))
+            if yb > 0:
+                south = salinity[l, 8 * yb - 1 : 8 * yb + 7, :]
+            else:
+                south = jnp.where(first_row, outer(from_south, l), roll(c, 1, 0))
+            at = (l % 2) * 64 + 8 * yb
+            ecol = jnp.broadcast_to(east_t[at : at + 8, 4 + l // 2 : 5 + l // 2], (8, 128))
+            wcol = jnp.broadcast_to(west_t[at : at + 8, 4 + l // 2 : 5 + l // 2], (8, 128))
+            e = roll(c, -1, 1)
+            w = roll(c, 1, 1)
+            e = jnp.concatenate([e[:, :-128], jnp.where(last_lane, ecol, e[:, -128:])], 1)
+            w = jnp.concatenate([jnp.where(first_lane, wcol, w[:, :128]), w[:, 128:]], 1)
+            k = rate[l] * 0.1
+            parts[0, l, ys, :] = c + k * (((e + w) + (north + south)) + (upper + lower) - 6.0 * c)
+            parts[1, l, ys, :] = (e - w) * 0.05
+            parts[2, l, ys, :] = (north - south) * 0.05
+            parts[3, l, ys, :] = (upper - lower) * 0.05
+        stores.append(pltpu.make_async_copy(parts.at[:, :, ys, :], parts_hbm.at[:, :, ys, :], out_sems.at[yb]))
+        stores[-1].start()
+    for store in stores:
+        store.wait()
+
+
+def still(me, rate, salinity, zlow, zhigh, recv1, from_south, from_north):
+    return call(
+        still_kernel,
+        hds(4, 8, 64, FINE),
+        [SM, HB, HB, HB, HB, VM, VM, VM],
+        HB,
+        scratch_shapes=[
+            pltpu.SMEM((8,), F32),
+            pltpu.VMEM((8, 64, FINE), F32),
+            pltpu.VMEM((64, FINE), F32),
+            pltpu.VMEM((64, FINE), F32),
+            pltpu.VMEM((4, 8, 64, FINE), F32),
+            pltpu.SemaphoreType.DMA((4,)),
+            pltpu.SemaphoreType.DMA((8,)),
+        ],
+        limit=24,
+        name="still",
+    )(me, rate, salinity, zlow, zhigh, recv1, from_south, from_north)
+
+
 CONSTS = ("ym", "edge", "yt", "filt", "fedge", "ref", "cm", "rm")
 
 
-def fine_kernel(me, grp_ref, rate_hbm, recv, edge_cols, salinity, zlow, zhigh, from_south, from_north, *rest):
+def fine_kernel(grp_ref, parts_hbm, recv, *rest):
     hbm, (out, spread), rest = rest[:8], rest[8:10], rest[10:]
-    (y_high, y_low, side, vel, total, warm, new_sal), consts, (rate, sems, out_sems) = rest[:7], rest[7:15], rest[15:]
-    *copies, rates = fetch(tuple(zip(hbm, consts)) + ((rate_hbm, rate),), sems)
-    copies = dict(zip(CONSTS, copies))
+    (y_high, y_low, side, vel, total, warm, new_sal, parts), consts, (sems, in_sems, out_sems) = (
+        rest[:8],
+        rest[8:16],
+        rest[16:],
+    )
+    copies = dict(zip(CONSTS, fetch(tuple(zip(hbm, consts)), sems)))
+    rows = [slice(8 * yb, 8 * yb + 8) for yb in range(8)]
+    loads = fetch([(parts_hbm.at[:, :, ys, :], parts.at[:, :, ys, :]) for ys in rows], in_sems)
     ym, edge, yt, filt, fedge, ref, cm, rm = consts
     grp = grp_ref[0]
     copies["ym"].wait()
@@ -390,7 +489,7 @@
     for f in range(3):
         for q in range(2):
             at = slice(64 * (2 * f + q), 64 * (2 * f + q) + 64)
-            high, low = halves(along_y(ym, f, q) * 0.05)
+            high, low = halves(along_y(ym, f, q))
             y_high[at, :] = high[:, :256]
             y_low[at, :] = low[:, :256]
             side[at, :] = mm(high[:, 256:], edge[q]) + mm(low[:, 256:], edge[q])
@@ -409,49 +508,15 @@
     vel[:, :128] += side[:, :128]
     vel[:, FINE - 128 :] += side[:, 128:]
 
-    west_t = edge_cols[(me[0] + G - 1) % G, 32:40, :].T
-    east_t = edge_cols[(me[0] + 1) % G, 32:40, :].T
-    last_row = iota((8, FINE), 0) == 7
-    first_row = iota((8, FINE), 0) == 0
-    last_lane = lane_id == 127
-    first_lane = lane_id == 0
-
-    def outer(rows, l):
-        line = jnp.concatenate([rows[16 + 8 * j + l : 17 + 8 * j + l, :] for j in range(4)], 1)
-        return jnp.broadcast_to(line, (8, FINE))
-
-    rates.wait()
     stores = []
     for yb in range(8):
-        ys = slice(8 * yb, 8 * yb + 8)
+        ys = rows[yb]
+        loads[yb].wait()
         for q in range(2):
             vx, vy, vz = (vel[64 * (2 * f + q) + 8 * yb : 64 * (2 * f + q) + 8 * yb + 8, :] for f in range(3))
             acc = None
             for l in range(4 * q, 4 * q + 4):
-                c = salinity[l, ys, :]
-                upper = salinity[l + 1, ys, :] if l < 7 else zhigh[ys, :]
-                lower = salinity[l - 1, ys, :] if l > 0 else zlow[ys, :]
-                if yb < 7:
-                    north = salinity[l, 8 * yb + 1 : 8 * yb + 9, :]
-                else:
-                    north = jnp.where(last_row, outer(from_north, l), roll(c, -1, 0))
-                if yb > 0:
-                    south = salinity[l, 8 * yb - 1 : 8 * yb + 7, :]
-                else:
-                    south = jnp.where(first_row, outer(from_south, l), roll(c, 1, 0))
-                at = (l % 2) * 64 + 8 * yb
-                ecol = jnp.broadcast_to(east_t[at : at + 8, 4 + l // 2 : 5 + l // 2], (8, 128))
-                wcol = jnp.broadcast_to(west_t[at : at + 8, 4 + l // 2 : 5 + l // 2], (8, 128))
-                e = roll(c, -1, 1)
-                w = roll(c, 1, 1)
-                e = jnp.concatenate([e[:, :-128], jnp.where(last_lane, ecol, e[:, -128:])], 1)
-                w = jnp.concatenate([jnp.where(first_lane, wcol, w[:, :128]), w[:, 128:]], 1)
-                k = rate[l] * 0.1
-                new = (
-                    c
-                    + k * (((e + w) + (north + south)) + (upper + lower) - 6.0 * c)
-                    - (vx * (e - w) + vy * (north - south) + vz * (upper - lower))
-                )
+                new = parts[0, l, ys, :] - (vx * parts[1, l, ys, :] + vy * parts[2, l, ys, :] + vz * parts[3, l, ys, :])
                 new_sal[l, ys, :] = new
                 acc = new if acc is None else acc + new
             total[64 * q + 8 * yb : 64 * q + 8 * yb + 8, :] = acc
@@ -460,7 +525,8 @@
     copies["cm"].wait()
     copies["rm"].wait()
     high, low = halves(total[...])
-    high, low = halves(mm(high, cm[...]) + mm(low, cm[...]))
+    means = [mm(high[:, at], cm[...]) + mm(low[:, at], cm[...]) for at in (slice(0, 512), slice(512, FINE))]
+    high, low = halves(jnp.concatenate(means, 1))
     mean = warm[...] - mm(rm[...], jnp.concatenate([high, low], 0))
     for a in range(G):
         spread[a] = mean
@@ -468,13 +534,12 @@
         store.wait()
 
 
-def fine(me, grp, recv1, recv2, salinity, zlow, zhigh, from_south, from_north, rate):
+def fine(grp, parts, recv2):
     consts = [jnp.asarray(tables()[name]) for name in CONSTS]
-    arrays = [recv2.reshape(512, 128), recv1, salinity, zlow, zhigh, from_south, from_north]
     return call(
         fine_kernel,
-        (sds(8, 64, FINE), sds(G, 32, 256)),
-        [SM, SM, HB] + [VM] * len(arrays) + [HB] * len(consts),
+        (sds(8, 64, FINE), vds(G, 32, 256)),
+        [SM, HB, VM] + [HB] * len(consts),
         [HB, VM],
         scratch_shapes=[
             pltpu.VMEM((384, 256), BF16),
@@ -484,38 +549,54 @@
             pltpu.VMEM((128, FINE), F32),
             pltpu.VMEM((32, 256), F32),
             pltpu.VMEM((8, 64, FINE), F32),
+            pltpu.VMEM((4, 8, 64, FINE), F32),
         ]
         + [pltpu.VMEM(x.shape, x.dtype) for x in consts]
-        + [pltpu.SMEM((8,), F32), pltpu.SemaphoreType.DMA((len(consts) + 1,)), pltpu.SemaphoreType.DMA((8,))],
-        limit=24,
+        + [pltpu.SemaphoreType.DMA((n,)) for n in (len(consts), 8, 8)],
+        limit=32,
         name="fine",
-    )(me, grp, rate, *arrays, *consts)
-
-
-def table_kernel(me, base, high, low):
+    )(grp, parts, recv2.reshape(512, 128), *consts)
+
+
+def stage_kernel(me, inner_hbm, outer_hbm, *rest):
+    count = (len(rest) - 5) // 2
+    hbm, dst, (high, low, inner, outer, sems) = rest[:count], rest[count : 2 * count], rest[2 * count :]
+    copies = fetch(((inner_hbm, inner), (outer_hbm, outer)) + tuple(zip(hbm, dst)), sems)
     turns = (iota((16, 128), 0) * me[0]) % G
     angle = turns.astype(F32) * (2.0 * math.pi / G)
     cos = jnp.concatenate([jnp.cos(angle)] * 2, 1)
     sin = -jnp.concatenate([jnp.sin(angle)] * 2, 1)
+    copies[0].wait()
+    copies[1].wait()
+    real, imag = cmul(inner[:, :256], inner[:, 256:], cos, sin)
     for t in range(G):
         rows = slice(16 * t, 16 * t + 16)
-        real, imag = base[rows, :256], base[rows, 256:]
-        for at, value in ((0, real * cos - imag * sin), (256, real * sin + imag * cos)):
-            high[rows, at : at + 256], low[rows, at : at + 256] = halves(value)
-
-
-def table(me):
-    return call(
-        table_kernel,
-        (sds(256, 512, dtype=BF16), sds(256, 512, dtype=BF16)),
-        [SM, VM],
-        [VM, VM],
-        name="table",
-    )(me, jnp.asarray(tables()["fwd"]))
-
-
-def forward_kernel(recv, table_high, table_low, cos_hbm, sin_hbm, out, left_high, left_low, mid, comb_cos, comb_sin, sems):
-    copies = fetch(((cos_hbm, comb_cos), (sin_hbm, comb_sin)), sems)
+        value = cmul(real, imag, outer[t : t + 1, :256], outer[t : t + 1, 256:])
+        for at in range(2):
+            high[rows, 256 * at : 256 * at + 256], low[rows, 256 * at : 256 * at + 256] = halves(value[at])
+    for copy in copies[2:]:
+        copy.wait()
+
+
+def stage(me):
+    t = tables()
+    consts = [jnp.asarray(x) for x in (*t["tw"], *t["inv"], *t["comb"])]
+    out = call(
+        stage_kernel,
+        [vds(*x.shape, dtype=x.dtype) for x in consts] + [vds(256, 512, dtype=BF16)] * 2,
+        [SM, HB, HB] + [HB] * len(consts),
+        [VM] * (len(consts) + 2),
+        scratch_shapes=[
+            pltpu.VMEM((G, 512), F32),
+            pltpu.VMEM((G, 512), F32),
+            pltpu.SemaphoreType.DMA((len(consts) + 2,)),
+        ],
+        name="stage",
+    )(me, *map(jnp.asarray, t["fwd"]), *consts)
+    return out[0:4], out[4:6], out[6:8]
+
+
+def forward_kernel(recv, table_high, table_low, comb_cos, comb_sin, out, left_high, left_low, mid):
     for a in range(G):
         high, low = halves(recv[a])
         left_high[32 * a : 32 * a + 32, :] = high
@@ -523,8 +604,6 @@
     mid[...] = (
         mm(left_high[...], table_high[...]) + mm(left_low[...], table_high[...]) + mm(left_high[...], table_low[...])
     )
-    for copy in copies:
-        copy.wait()
     real = imag = jnp.zeros((32, 256), F32)
     for a in range(G):
         c, s = comb_cos[a : a + 1, :], comb_sin[a : a + 1, :]
@@ -536,20 +615,16 @@
         out[g, 32:64, :] = imag
 
 
-def forward(recv, high, low):
-    cos, sin = map(jnp.asarray, tables()["comb"])
+def forward(recv, high, low, cos, sin):
     return call(
         forward_kernel,
         sds(4, 64, 256),
-        [VM, VM, VM, HB, HB],
+        [VM] * 5,
         VM,
         scratch_shapes=[
             pltpu.VMEM((512, 256), BF16),
             pltpu.VMEM((512, 256), BF16),
             pltpu.VMEM((512, 512), F32),
-            pltpu.VMEM((G, 256), F32),
-            pltpu.VMEM((G, 256), F32),
-            pltpu.SemaphoreType.DMA((2,)),
         ],
         name="forward",
     )(recv, high, low, cos, sin)
@@ -581,23 +656,22 @@
     me = lax.axis_index(GX).astype(jnp.int32).reshape(1)
     grp = lax.axis_index("grp").astype(jnp.int32).reshape(1)
     modes = coarse_modes.reshape(256, 256)
-    chunk, up, down, low_face, high_face = edges(me, modes, salinity)
+    up, down = outer_lines(modes, salinity)
+    from_south = shifted(up, "gy", 1)
+    from_north = shifted(down, "gy", -1)
+    chunk, low_face, high_face = pack(me, modes, salinity)
+    chunk = tails(chunk, from_south, from_north)
+    recv1 = lax.all_to_all(chunk, GX, 0, 0, tiled=True)
+    inv, comb, weights = stage(me)
     zlow = shifted(high_face, "grp", 1)
     zhigh = shifted(low_face, "grp", -1)
-    from_south = shifted(up, "gy", 1)
-    from_north = shifted(down, "gy", -1)
-    weights = table(me)
-    from_south, from_north, zlow, zhigh, weights = lax.optimization_barrier(
-        (from_south, from_north, zlow, zhigh, weights)
-    )
-    chunk = tails(chunk, from_south, from_north)
-    recv1 = lax.all_to_all(chunk, GX, 0, 0, tiled=True)
-    recv2 = lax.all_to_all(inverse(recv1), GRP_GX, 0, 0, tiled=True)
-    salinity_next, spread = fine(
-        me, grp, recv1, recv2, salinity, zlow, zhigh, from_south, from_north, diffusivity
-    )
+    recv1, zlow, zhigh = lax.optimization_barrier((recv1, zlow, zhigh))
+    send2 = inverse(recv1, *inv)
+    recv2 = lax.all_to_all(send2, GRP_GX, 0, 0, tiled=True)
+    parts = still(me, diffusivity, salinity, zlow, zhigh, recv1, from_south, from_north)
+    salinity_next, spread = fine(grp, parts, recv2)
     recv3 = lax.all_to_all(spread, GX, 0, 0, tiled=True)
-    recv4 = lax.all_to_all(forward(recv3, *weights), "grp", 0, 0, tiled=True)
+    recv4 = lax.all_to_all(forward(recv3, *weights, *comb), "grp", 0, 0, tiled=True)
     coarse_next = finish(me, viscosity, forcing_gain, recv4, modes)
     return (salinity_next, coarse_next.reshape(coarse_modes.shape))
 

time: 96.4 us -> 105 us (1.089)
  blocking collectives: 41.2 us -> 17.9 us
  Pallas kernels: 13.1 us -> 35.6 us
  starting transfers between devices: 15.7 us -> 29.4 us
  waiting for transfers between devices: 22.9 us -> 19.8 us
    all_to_all x1 -> x0, blocking collectives: 23 us -> none  [per_device(): recv1 = lax.all_to_all(chunk, GX, 0, 0, tiled=True)]
    pallas_call x7 -> x9, Pallas kernels: 13.1 us -> 35.6 us  [placed(): inner(*[x if spec is not HB else pltpu.with_memory_space_constraint(x, pl...]
    all_to_all x2 -> x3, starting transfers between devices: 10.7 us -> 24.4 us  [the longest x1 11.2 us: per_device(): recv1 = lax.all_to_all(chunk, GX, 0, 0, tiled=True)]
    all_to_all x2 -> x3, waiting for transfers between devices: 18.8 us -> 15.5 us  [the longest x1 6.38 us: per_device(): recv2 = lax.all_to_all(send2, GRP_GX, 0, 0, tiled=True)]
  transfers between devices with their start and end apart: 6 -> 7, of which waited for: 4 -> 4; matrix products, arithmetic and copies ran while one was open for 0% -> 0% of each run, Pallas kernels for 0% -> 24%
where the time goes in v3:
time: 105 us
  Pallas kernels  35.6 us (34%)
  starting transfers between devices  29.4 us (28%)
  waiting for transfers between devices  19.8 us (19%)
  blocking collectives  17.9 us (17%)
  between operations  2.04 us (2%)
    pallas_call x9, Pallas kernels, placed(): inner(*[x if spec is not HB else pltpu.with_memory_space_constraint(x, pl...  35.6 us
    all_to_all x1, blocking collectives, per_device(): recv3 = lax.all_to_all(spread, GX, 0, 0, tiled=True)  17.9 us
    all_to_all x1, starting transfers between devices, per_device(): recv1 = lax.all_to_all(chunk, GX, 0, 0, tiled=True)  11.2 us
    all_to_all x1, starting transfers between devices, per_device(): recv2 = lax.all_to_all(send2, GRP_GX, 0, 0, tiled=True)  8.83 us
    all_to_all x1, waiting for transfers between devices, per_device(): recv2 = lax.all_to_all(send2, GRP_GX, 0, 0, tiled=True)  6.38 us
    all_to_all x1, waiting for transfers between devices, per_device(): lax.all_to_all(forward(recv3, *weights, *comb), 'grp', 0, 0, tiled=True)  5.38 us
    ppermute x4, starting transfers between devices, shifted(): lax.ppermute(array, axis, [(i, (i + step) % count) for i in range(count)])  5.05 us
    all_to_all x1, starting transfers between devices, per_device(): lax.all_to_all(forward(recv3, *weights, *comb), 'grp', 0, 0, tiled=True)  4.31 us
  transfers between devices with their start and end apart: 7, of which 4 were waited for; matrix products, arithmetic and copies ran while one was open for 0% of the time, Pallas kernels for 24%

profile of v3, /device:TPU:32, one launch (start us, length us, event | category | flops | bytes accessed | tf_op | source)
XLA Modules:
  0.0 104.7 jit_solution(1970646761469914777)
XLA Ops:
  0.6 1.2 %outer_lines.1 = (f32[48,256]{1,0:T(8,128)S(1)}, f32[48,256]{1,0:T(8,128)S(1)}) custom-call(f32[16,16,256]{2,1,0:T(8,128)} %bitcast.6, f32[8,64,1024]{2,1,0:T(8,128)} %sal_hbm.1), custom_call_target="tpu_custom_call" | custom-call | tf_op jit(solution)/shard_map/outer_lines/pallas_call | solution.py:128
  1.9 0.1 collective-permute-start
  2.0 1.7 %collective-permute-start.1 = (f32[48,256]{1,0:T(8,128)S(1)}, f32[48,256]{1,0:T(8,128)S(1)}, u32[]{:S(2)}, u32[]{:S(2)}) collective-permute-start(f32[48,256]{1,0:T(8,128)S(1)} %get-tuple-element.22), channel_id=1, source_target_pairs={{0,3},{1,0},{2,1},{3,2},{4,7},{5,4},{6,5},{7,6},{8,11},{9,8},{10,9... | collective-permute-start | bytes 147464 | tf_op jit(solution)/shard_map/ppermute | solution.py:652
  3.7 17.0 %pack.1 = (f32[16,40,128]{2,1,0:T(8,128)S(1)}, f32[64,1024]{1,0:T(8,128)}, f32[64,1024]{1,0:T(8,128)}) custom-call(s32[1]{0:T(128)} %bitcast.1.me, f32[256,256]{1,0:T(8,128)} %bitcast.7, f32[8,64,1024]{2,1,0:T(8,128)} %sal_hbm.1), custom_call_target="tpu_custom_call" | custom-call | tf_op jit(solution)/shard_map/pack/pallas_call | solution.py:128
  20.7 0.0 collective-permute-done.from_south
  20.7 0.0 collective-permute-done.1.from_north
  20.8 0.8 tails.1
  21.5 11.2 %all-to-all-start = ((f32[16,40,128]{2,1,0:T(8,128)}), f32[16,40,128]{2,1,0:T(8,128)S(1)}, u32[]{:S(2)}, u32[]{:S(2)}) async-start(f32[16,40,128]{2,1,0:T(8,128)} %tails.1), calls=%async_computation | async-start | bytes 655360 | tf_op jit(solution)/shard_map/all_to_all | solution.py:664
  32.7 1.5 %collective-permute-start.2 = (f32[64,1024]{1,0:T(8,128)}, f32[64,1024]{1,0:T(8,128)S(1)}, u32[]{:S(2)}, u32[]{:S(2)}) collective-permute-start(f32[64,1024]{1,0:T(8,128)} %get-tuple-element.23), channel_id=1, source_target_pairs={{0,64},{64,128},{128,192},{192,0},{1,65},{65,129},{129,193},{193,1... | collective-permute-start | bytes 786440 | tf_op jit(solution)/shard_map/ppermute | solution.py:652
  34.2 1.7 %collective-permute-start.3 = (f32[64,1024]{1,0:T(8,128)}, f32[64,1024]{1,0:T(8,128)S(1)}, u32[]{:S(2)}, u32[]{:S(2)}) collective-permute-start(f32[64,1024]{1,0:T(8,128)} %get-tuple-element.24), channel_id=1, source_target_pairs={{0,192},{64,0},{128,64},{192,128},{1,193},{65,1},{129,65},{193,129... | collective-permute-start | bytes 786440 | tf_op jit(solution)/shard_map/ppermute | solution.py:652
  36.0 1.2 %stage.1 = (f32[16,8,128]{2,1,0:T(8,128)S(1)}, f32[16,8,128]{2,1,0:T(8,128)S(1)}, bf16[512,256]{1,0:T(8,128)(2,1)S(1)}, bf16[512,256]{1,0:T(8,128)(2,1)S(1)}, f3...) custom-call(s32[1]{0:T(128)} %bitcast.1.me, ...), custom_call_target="tpu_custom_call" | custom-call | tf_op jit(solution)/shard_map/stage/pallas_call | solution.py:128
  37.2 4.3 %collective-permute-done.2.zlow_hbm = f32[64,1024]{1,0:T(8,128)S(1)} collective-permute-done((f32[64,1024]{1,0:T(8,128)}, f32[64,1024]{1,0:T(8,128)S(1)}, u32[]{:S(2)}, u32[]{:S(2)}) %collective-permute-start.2) | collective-permute-done | bytes 262176 | tf_op jit(solution)/shard_map/ppermute | solution.py:652
  41.5 3.7 %all-to-all-done.edge_cols.recv = f32[16,40,128]{2,1,0:T(8,128)S(1)} async-done(((f32[16,40,128]{2,1,0:T(8,128)}), f32[16,40,128]{2,1,0:T(8,128)S(1)}, u32[]{:S(2)}, u32[]{:S(2)}) %all-to-all-start) | async-done | bytes 327712 | tf_op jit(solution)/shard_map/all_to_all | solution.py:664
  45.2 1.6 %inverse.1 = f32[64,8,128]{2,1,0:T(8,128)} custom-call(f32[16,40,128]{2,1,0:T(8,128)S(1)} %all-to-all-done.edge_cols.recv, f32[16,8,128]{2,1,0:T(8,128)S(1)} %get-tuple-element.28.twc, f32[16,8,128]{2,1,0:T(8,128)S(1)} %get-tuple-element.29.tws, bf16[512,256]{1,0:T(8,128)(2,1)S(1)} %get-tuple-element.30.inv_high, bf16[512,256]{1,0:T(8,128)(2,1)S(1)} %get-tuple-element.31.inv_low), custom_call_target="tpu_custom_call" | custom-call | tf_op jit(solution)/shard_map/inverse/pallas_call | solution.py:128
  46.8 8.8 %all-to-all-start.1 = ((f32[64,8,128]{2,1,0:T(8,128)}), f32[64,8,128]{2,1,0:T(8,128)S(1)}, u32[]{:S(2)}, u32[]{:S(2)}) async-start(f32[64,8,128]{2,1,0:T(8,128)} %inverse.1), calls=%async_computation.1 | async-start | bytes 524288 | tf_op jit(solution)/shard_map/all_to_all | solution.py:670
  55.6 6.8 %still.1.parts_hbm = f32[4,8,64,1024]{3,2,1,0:T(8,128)} custom-call(s32[1]{0:T(128)} %bitcast.1.me, f32[8]{0:T(128)} %rate_hbm.1, f32[8,64,1024]{2,1,0:T(8,128)} %sal_hbm.1, f32[64,1024]{1,0:T(8,128)} %copy-done.1, f32[64,1024]{1,0:T(8,128)} %copy-done.2, f32[16,40,128]{2,1,0:T(8,128)S(1)} %all-to-all-done.edge_cols.recv, ...), custom_call_target="tpu_custom_call" | custom-call | tf_op jit(solution)/shard_map/still/pallas_call | solution.py:128
  62.5 6.4 %all-to-all-done.1 = f32[64,8,128]{2,1,0:T(8,128)S(1)} async-done(((f32[64,8,128]{2,1,0:T(8,128)}), f32[64,8,128]{2,1,0:T(8,128)S(1)}, u32[]{:S(2)}, u32[]{:S(2)}) %all-to-all-start.1) | async-done | bytes 262176 | tf_op jit(solution)/shard_map/all_to_all | solution.py:670
  68.9 4.9 %fine.1 = (f32[8,64,1024]{2,1,0:T(8,128)}, f32[16,32,256]{2,1,0:T(8,128)S(1)}) custom-call(s32[1]{0:T(128)} %bitcast.grp_ref, f32[4,8,64,1024]{3,2,1,0:T(8,128)} %still.1.parts_hbm, f32[512,128]{1,0:T(8,128)S(1)} %bitcast.9, bf16[64,64]{1,0:T(8,128)(2,1)} %constant.59.clone.rest_0_, bf16[2,128,256]{2,1,0:T(8,128)(2,1)} %constant.60.clone.rest_1_, ...), custom_call_target="tpu_custom_call" | custom-call | tf_op jit(solution)/shard_map/fine/pallas_call | solution.py:128
  73.8 0.0 copy-start
  73.8 17.9 %all_to_all.20.recv = f32[16,32,256]{2,1,0:T(8,128)S(1)} all-to-all(f32[16,32,256]{2,1,0:T(8,128)S(1)} %get-tuple-element.33), channel_id=1, replica_groups=mesh['grp'=4,'gx_0'=2,'gx_1'=8,'gy'=4] {'gx_0','gx_1'}, dimensions={0} | all-to-all | bytes 1048576 | tf_op jit(solution)/shard_map/all_to_all | solution.py:673
  91.7 1.3 %forward.1 = f32[4,64,256]{2,1,0:T(8,128)} custom-call(f32[16,32,256]{2,1,0:T(8,128)S(1)} %all_to_all.20.recv, bf16[256,512]{1,0:T(8,128)(2,1)S(1)} %get-tuple-element.34.table_high, bf16[256,512]{1,0:T(8,128)(2,1)S(1)} %get-tuple-element.35.table_low, f32[16,256]{1,0:T(8,128)S(1)} %get-tuple-element.36.comb_cos, f32[16,256]{1,0:T(8,128)S(1)} %get-tuple-element.37.comb_sin), custom_call_target="tpu_custom_call" | custom-call | tf_op jit(solution)/shard_map/forward/pallas_call | solution.py:128
  93.0 4.3 %all-to-all-start.3 = ((f32[4,64,256]{2,1,0:T(8,128)}), f32[4,64,256]{2,1,0:T(8,128)S(1)}, u32[]{:S(2)}, u32[]{:S(2)}) async-start(f32[4,64,256]{2,1,0:T(8,128)} %forward.1), calls=%async_computation.3 | async-start | bytes 524288 | tf_op jit(solution)/shard_map/all_to_all | solution.py:674
  98.6 5.4 %all-to-all-done.3.recv = f32[4,64,256]{2,1,0:T(8,128)S(1)} async-done(((f32[4,64,256]{2,1,0:T(8,128)}), f32[4,64,256]{2,1,0:T(8,128)S(1)}, u32[]{:S(2)}, u32[]{:S(2)}) %all-to-all-start.3) | async-done | bytes 262176 | tf_op jit(solution)/shard_map/all_to_all | solution.py:674
  104.0 0.7 finish.1
  (6 shorter events, 0.0 us)
Async XLA Ops:
  1.9 18.9 %collective-permute-start = (f32[48,256]{1,0:T(8,128)S(1)}, f32[48,256]{1,0:T(8,128)S(1)}, u32[]{:S(2)}, u32[]{:S(2)}) collective-permute-start(f32[48,256]{1,0:T(8,128)S(1)} %get-tuple-element.21), channel_id=1, source_target_pairs={{0,1},{1,2},{2,3},{3,0},{4,5},{5,6},{6,7},{7,4},{8,9},{9,10},{10,1... | collective-permute-start | bytes 147464 | tf_op jit(solution)/shard_map/ppermute | solution.py:652
  2.0 18.8 %collective-permute-start.1 = (f32[48,256]{1,0:T(8,128)S(1)}, f32[48,256]{1,0:T(8,128)S(1)}, u32[]{:S(2)}, u32[]{:S(2)}) collective-permute-start(f32[48,256]{1,0:T(8,128)S(1)} %get-tuple-element.22), channel_id=1, source_target_pairs={{0,3},{1,0},{2,1},{3,2},{4,7},{5,4},{6,5},{7,6},{8,11},{9,8},{10,9... | collective-permute-start | bytes 147464 | tf_op jit(solution)/shard_map/ppermute | solution.py:652
  21.5 23.7 %all-to-all-start = ((f32[16,40,128]{2,1,0:T(8,128)}), f32[16,40,128]{2,1,0:T(8,128)S(1)}, u32[]{:S(2)}, u32[]{:S(2)}) async-start(f32[16,40,128]{2,1,0:T(8,128)} %tails.1), calls=%async_computation | async-start | bytes 655360 | tf_op jit(solution)/shard_map/all_to_all | solution.py:664
  32.7 8.7 %collective-permute-start.2 = (f32[64,1024]{1,0:T(8,128)}, f32[64,1024]{1,0:T(8,128)S(1)}, u32[]{:S(2)}, u32[]{:S(2)}) collective-permute-start(f32[64,1024]{1,0:T(8,128)} %get-tuple-element.23), channel_id=1, source_target_pairs={{0,64},{64,128},{128,192},{192,0},{1,65},{65,129},{129,193},{193,1... | collective-permute-start | bytes 786440 | tf_op jit(solution)/shard_map/ppermute | solution.py:652
  34.2 7.2 %collective-permute-start.3 = (f32[64,1024]{1,0:T(8,128)}, f32[64,1024]{1,0:T(8,128)S(1)}, u32[]{:S(2)}, u32[]{:S(2)}) collective-permute-start(f32[64,1024]{1,0:T(8,128)} %get-tuple-element.24), channel_id=1, source_target_pairs={{0,192},{64,0},{128,64},{192,128},{1,193},{65,1},{129,65},{193,129... | collective-permute-start | bytes 786440 | tf_op jit(solution)/shard_map/ppermute | solution.py:652
  41.5 14.2 %copy-start.1 = (f32[64,1024]{1,0:T(8,128)}, f32[64,1024]{1,0:T(8,128)S(1)}, u32[]{:S(2)}) copy-start(f32[64,1024]{1,0:T(8,128)S(1)} %collective-permute-done.2.zlow_hbm) | copy-start | bytes 786436
  41.5 14.2 %copy-start.2 = (f32[64,1024]{1,0:T(8,128)}, f32[64,1024]{1,0:T(8,128)S(1)}, u32[]{:S(2)}) copy-start(f32[64,1024]{1,0:T(8,128)S(1)} %collective-permute-done.3.zhigh_hbm) | copy-start | bytes 786436
  46.8 22.1 %all-to-all-start.1 = ((f32[64,8,128]{2,1,0:T(8,128)}), f32[64,8,128]{2,1,0:T(8,128)S(1)}, u32[]{:S(2)}, u32[]{:S(2)}) async-start(f32[64,8,128]{2,1,0:T(8,128)} %inverse.1), calls=%async_computation.1 | async-start | bytes 524288 | tf_op jit(solution)/shard_map/all_to_all | solution.py:670
  73.8 30.2 %copy-start = (f32[1,2,8,16,256]{4,3,2,1,0:T(8,128)S(1)}, f32[1,2,8,16,256]{4,3,2,1,0:T(8,128)}, u32[]{:S(2)}) copy-start(f32[1,2,8,16,256]{4,3,2,1,0:T(8,128)} %param.21) | copy-start | bytes 786436
  93.0 11.0 %all-to-all-start.3 = ((f32[4,64,256]{2,1,0:T(8,128)}), f32[4,64,256]{2,1,0:T(8,128)S(1)}, u32[]{:S(2)}, u32[]{:S(2)}) async-start(f32[4,64,256]{2,1,0:T(8,128)} %forward.1), calls=%async_computation.3 | async-start | bytes 524288 | tf_op jit(solution)/shard_map/all_to_all | solution.py:674

commit v4 on v3

--- a/solution.py
+++ b/solution.py
@@ -194,15 +194,15 @@
     )(modes.reshape(16, 16, 256), salinity)
 
 
-def pack_kernel(me, modes, sal, chunk, low_face, high_face, modes_a, modes_b, west, east, sems):
+def pack_kernel(me, modes, sal, chunk, tail, low_face, high_face, modes_a, modes_b, west, east, faces, lines, sems, out_sems):
     copies = fetch(
         (
             (modes.at[:, 0:128], modes_a),
             (modes.at[:, 128:256], modes_b),
+            (sal.at[0], faces.at[0]),
+            (sal.at[7], faces.at[1]),
             (sal.at[:, :, 0:128], west),
             (sal.at[:, :, FINE - 128 :], east),
-            (sal.at[0], low_face),
-            (sal.at[7], high_face),
         ),
         sems,
     )
@@ -210,9 +210,15 @@
         copy.wait()
     zero = jnp.zeros((8, 128), F32)
     for r in range(G):
-        chunk[r, 0:16, :] = modes_a[pl.ds(r, 16, stride=16), :]
-        chunk[r, 16:32, :] = modes_b[pl.ds(r, 16, stride=16), :]
-        chunk[r, 32:40, :] = zero
+        lines[r, 0:16, :] = modes_a[pl.ds(r, 16, stride=16), :]
+        lines[r, 16:32, :] = modes_b[pl.ds(r, 16, stride=16), :]
+        tail[r] = zero
+    stores = [pltpu.make_async_copy(lines, chunk.at[:, 0:32, :], out_sems.at[0])]
+    stores[0].start()
+    for i, face in enumerate((low_face, high_face)):
+        copies[2 + i].wait()
+        stores.append(pltpu.make_async_copy(faces.at[i], face, out_sems.at[1 + i]))
+        stores[-1].start()
     row_id = iota((8, 128), 0)
 
     def column(block, lane):
@@ -223,46 +229,59 @@
             tile = jnp.where(row_id == 4 + i, line, tile)
         return tile
 
-    for copy in copies[2:4]:
-        copy.wait()
-    chunk[(me[0] + 1) % G, 32:40, :] = column(east, 127)
-    chunk[(me[0] + G - 1) % G, 32:40, :] = column(west, 0)
     for copy in copies[4:]:
         copy.wait()
+    tail[(me[0] + 1) % G] = column(east, 127)
+    tail[(me[0] + G - 1) % G] = column(west, 0)
+    for store in stores:
+        store.wait()
 
 
 def pack(me, modes, salinity):
     return call(
         pack_kernel,
-        (vds(G, 40, 128), hds(64, FINE), hds(64, FINE)),
+        (hds(G, 40, 128), vds(G, 8, 128), hds(64, FINE), hds(64, FINE)),
         [SM, HB, HB],
-        [VM, HB, HB],
+        [HB, VM, HB, HB],
         scratch_shapes=[
             pltpu.VMEM((256, 128), F32),
             pltpu.VMEM((256, 128), F32),
             pltpu.VMEM((8, 64, 128), F32),
             pltpu.VMEM((8, 64, 128), F32),
+            pltpu.VMEM((2, 64, FINE), F32),
+            pltpu.VMEM((G, 32, 128), F32),
             pltpu.SemaphoreType.DMA((6,)),
+            pltpu.SemaphoreType.DMA((3,)),
         ],
         name="pack",
     )(me, modes, salinity)
 
 
-def tails_kernel(chunk, from_south, from_north, out):
+def tails_kernel(chunk, tail, from_south, from_north, out, tiles, sem):
     row_id = iota((8, 128), 0)
     for r in range(G):
         rows = from_south if r < 8 else from_north
         p = r % 8
-        tile = chunk[r, 32:40, :]
+        tile = tail[r]
         parts = (rows[p : p + 1, :128], rows[p : p + 1, 128:], rows[8 + p : 9 + p, :128], rows[8 + p : 9 + p, 128:])
         for i, part in enumerate(parts):
             tile = jnp.where(row_id == i, jnp.broadcast_to(part, (8, 128)), tile)
-        out[r, 0:32, :] = chunk[r, 0:32, :]
-        out[r, 32:40, :] = tile
-
-
-def tails(chunk, from_south, from_north):
-    return call(tails_kernel, sds(G, 40, 128), [VM] * 3, VM, name="tails")(chunk, from_south, from_north)
+        tiles[r] = tile
+    store = pltpu.make_async_copy(tiles, out.at[:, 32:40, :], sem)
+    store.start()
+    store.wait()
+
+
+def tails(chunk, tail, from_south, from_north):
+    return call(
+        tails_kernel,
+        hds(G, 40, 128),
+        [HB, VM, VM, VM],
+        HB,
+        input_output_aliases={0: 0},
+        scratch_shapes=[pltpu.VMEM((G, 8, 128), F32), pltpu.SemaphoreType.DMA],
+        name="tails",
+    )(chunk, tail, from_south, from_north)
 
 
 def cmul(a, b, c, s):
@@ -659,8 +678,8 @@
     up, down = outer_lines(modes, salinity)
     from_south = shifted(up, "gy", 1)
     from_north = shifted(down, "gy", -1)
-    chunk, low_face, high_face = pack(me, modes, salinity)
-    chunk = tails(chunk, from_south, from_north)
+    chunk, tail, low_face, high_face = pack(me, modes, salinity)
+    chunk = tails(chunk, tail, from_south, from_north)
     recv1 = lax.all_to_all(chunk, GX, 0, 0, tiled=True)
     inv, comb, weights = stage(me)
     zlow = shifted(high_face, "grp", 1)

time: 105 us -> 92.9 us (0.88)
  Pallas kernels: 35.6 us -> 20.5 us
  waiting for transfers between devices: 19.8 us -> 21.6 us
  blocking collectives: 17.9 us -> 19.2 us
    pallas_call x9, Pallas kernels: 35.6 us -> 20.5 us  [placed(): inner(*[x if spec is not HB else pltpu.with_memory_space_constraint(x, pl...]
    ppermute x4, waiting for transfers between devices: 4.28 us -> 5.76 us  [shifted(): lax.ppermute(array, axis, [(i, (i + step) % count) for i in range(count)])]
    all_to_all x1, blocking collectives: 17.9 us -> 19.2 us  [per_device(): recv3 = lax.all_to_all(spread, GX, 0, 0, tiled=True)]
  transfers between devices with their start and end apart: 7 -> 7, of which waited for: 4 -> 4; matrix products, arithmetic and copies ran while one was open for 0% -> 0% of each run, Pallas kernels for 24% -> 11%
where the time goes in v4:
time: 92.9 us; the launch traced here: 92.5 us
  starting transfers between devices  29.1 us (31%)
  waiting for transfers between devices  21.6 us (23%)
  Pallas kernels  20.5 us (22%)
  blocking collectives  19.2 us (21%)
  between operations  2.05 us (2%)
    pallas_call x9, Pallas kernels, placed(): inner(*[x if spec is not HB else pltpu.with_memory_space_constraint(x, pl...  20.5 us
    all_to_all x1, blocking collectives, per_device(): recv3 = lax.all_to_all(spread, GX, 0, 0, tiled=True)  19.2 us
    all_to_all x1, starting transfers between devices, per_device(): recv1 = lax.all_to_all(chunk, GX, 0, 0, tiled=True)  11.2 us
    all_to_all x1, starting transfers between devices, per_device(): recv2 = lax.all_to_all(send2, GRP_GX, 0, 0, tiled=True)  9.39 us
    all_to_all x1, waiting for transfers between devices, per_device(): recv2 = lax.all_to_all(send2, GRP_GX, 0, 0, tiled=True)  7.29 us
    ppermute x4, waiting for transfers between devices, shifted(): lax.ppermute(array, axis, [(i, (i + step) % count) for i in range(count)])  5.76 us
    all_to_all x1, waiting for transfers between devices, per_device(): lax.all_to_all(forward(recv3, *weights, *comb), 'grp', 0, 0, tiled=True)  5.35 us
    ppermute x4, starting transfers between devices, shifted(): lax.ppermute(array, axis, [(i, (i + step) % count) for i in range(count)])  5.05 us
  transfers between devices with their start and end apart: 7, of which 4 were waited for; matrix products, arithmetic and copies ran while one was open for 0% of the time, Pallas kernels for 11%

profile of v4, /device:TPU:32, one launch (start us, length us, event | category | flops | bytes accessed | tf_op | source)
XLA Modules:
  0.0 92.5 jit_solution(16802982481240932534)
XLA Ops:
  0.6 1.2 %outer_lines.1 = (f32[48,256]{1,0:T(8,128)S(1)}, f32[48,256]{1,0:T(8,128)S(1)}) custom-call(f32[16,16,256]{2,1,0:T(8,128)} %bitcast.6, f32[8,64,1024]{2,1,0:T(8,128)} %sal_hbm.1), custom_call_target="tpu_custom_call" | custom-call | tf_op jit(solution)/shard_map/outer_lines/pallas_call | solution.py:128
  1.9 0.1 collective-permute-start
  2.0 1.7 %collective-permute-start.1 = (f32[48,256]{1,0:T(8,128)S(1)}, f32[48,256]{1,0:T(8,128)S(1)}, u32[]{:S(2)}, u32[]{:S(2)}) collective-permute-start(f32[48,256]{1,0:T(8,128)S(1)} %get-tuple-element.24), channel_id=1, source_target_pairs={{0,3},{1,0},{2,1},{3,2},{4,7},{5,4},{6,5},{7,6},{8,11},{9,8},{10,9... | collective-permute-start | bytes 147464 | tf_op jit(solution)/shard_map/ppermute | solution.py:671
  3.7 2.0 %pack.1 = (f32[16,40,128]{2,1,0:T(8,128)}, f32[16,8,128]{2,1,0:T(8,128)S(1)}, f32[64,1024]{1,0:T(8,128)}, f32[64,1024]{1,0:T(8,128)}) custom-call(s32[1]{0:T(128)} %bitcast.1.me, f32[256,256]{1,0:T(8,128)} %bitcast.7, f32[8,64,1024]{2,1,0:T(8,128)} %sal_hbm.1), custom_call_target="tpu_custom_call" | custom-call | tf_op jit(solution)/shard_map/pack/pallas_call | solution.py:128
  5.7 0.0 collective-permute-done.from_south
  5.7 0.7 tails.1
  6.4 11.2 %all-to-all-start = ((f32[16,40,128]{2,1,0:T(8,128)}), f32[16,40,128]{2,1,0:T(8,128)S(1)}, u32[]{:S(2)}, u32[]{:S(2)}) async-start(f32[16,40,128]{2,1,0:T(8,128)} %tails.1), calls=%async_computation | async-start | bytes 655360 | tf_op jit(solution)/shard_map/all_to_all | solution.py:683
  17.6 1.5 %collective-permute-start.2 = (f32[64,1024]{1,0:T(8,128)}, f32[64,1024]{1,0:T(8,128)S(1)}, u32[]{:S(2)}, u32[]{:S(2)}) collective-permute-start(f32[64,1024]{1,0:T(8,128)} %get-tuple-element.25), channel_id=1, source_target_pairs={{0,64},{64,128},{128,192},{192,0},{1,65},{65,129},{129,193},{193,1... | collective-permute-start | bytes 786440 | tf_op jit(solution)/shard_map/ppermute | solution.py:671
  19.1 1.7 %collective-permute-start.3 = (f32[64,1024]{1,0:T(8,128)}, f32[64,1024]{1,0:T(8,128)S(1)}, u32[]{:S(2)}, u32[]{:S(2)}) collective-permute-start(f32[64,1024]{1,0:T(8,128)} %get-tuple-element.26), channel_id=1, source_target_pairs={{0,192},{64,0},{128,64},{192,128},{1,193},{65,1},{129,65},{193,129... | collective-permute-start | bytes 786440 | tf_op jit(solution)/shard_map/ppermute | solution.py:671
  20.8 1.2 %stage.1 = (f32[16,8,128]{2,1,0:T(8,128)S(1)}, f32[16,8,128]{2,1,0:T(8,128)S(1)}, bf16[512,256]{1,0:T(8,128)(2,1)S(1)}, bf16[512,256]{1,0:T(8,128)(2,1)S(1)}, f3...) custom-call(s32[1]{0:T(128)} %bitcast.1.me, ...), custom_call_target="tpu_custom_call" | custom-call | tf_op jit(solution)/shard_map/stage/pallas_call | solution.py:128
  22.1 5.8 %collective-permute-done.2.zlow_hbm = f32[64,1024]{1,0:T(8,128)S(1)} collective-permute-done((f32[64,1024]{1,0:T(8,128)}, f32[64,1024]{1,0:T(8,128)S(1)}, u32[]{:S(2)}, u32[]{:S(2)}) %collective-permute-start.2) | collective-permute-done | bytes 262176 | tf_op jit(solution)/shard_map/ppermute | solution.py:671
  27.8 0.0 collective-permute-done.3.zhigh_hbm
  27.8 3.2 %all-to-all-done.edge_cols.recv = f32[16,40,128]{2,1,0:T(8,128)S(1)} async-done(((f32[16,40,128]{2,1,0:T(8,128)}), f32[16,40,128]{2,1,0:T(8,128)S(1)}, u32[]{:S(2)}, u32[]{:S(2)}) %all-to-all-start) | async-done | bytes 327712 | tf_op jit(solution)/shard_map/all_to_all | solution.py:683
  31.0 1.6 %inverse.1 = f32[64,8,128]{2,1,0:T(8,128)} custom-call(f32[16,40,128]{2,1,0:T(8,128)S(1)} %all-to-all-done.edge_cols.recv, f32[16,8,128]{2,1,0:T(8,128)S(1)} %get-tuple-element.30.twc, f32[16,8,128]{2,1,0:T(8,128)S(1)} %get-tuple-element.31.tws, bf16[512,256]{1,0:T(8,128)(2,1)S(1)} %get-tuple-element.32.inv_high, bf16[512,256]{1,0:T(8,128)(2,1)S(1)} %get-tuple-element.33.inv_low), custom_call_target="tpu_custom_call" | custom-call | tf_op jit(solution)/shard_map/inverse/pallas_call | solution.py:128
  32.6 9.4 %all-to-all-start.1 = ((f32[64,8,128]{2,1,0:T(8,128)}), f32[64,8,128]{2,1,0:T(8,128)S(1)}, u32[]{:S(2)}, u32[]{:S(2)}) async-start(f32[64,8,128]{2,1,0:T(8,128)} %inverse.1), calls=%async_computation.1 | async-start | bytes 524288 | tf_op jit(solution)/shard_map/all_to_all | solution.py:689
  42.0 6.8 %still.1.parts_hbm = f32[4,8,64,1024]{3,2,1,0:T(8,128)} custom-call(s32[1]{0:T(128)} %bitcast.1.me, f32[8]{0:T(128)} %rate_hbm.1, f32[8,64,1024]{2,1,0:T(8,128)} %sal_hbm.1, f32[64,1024]{1,0:T(8,128)} %copy-done.1, f32[64,1024]{1,0:T(8,128)} %copy-done.2, f32[16,40,128]{2,1,0:T(8,128)S(1)} %all-to-all-done.edge_cols.recv, ...), custom_call_target="tpu_custom_call" | custom-call | tf_op jit(solution)/shard_map/still/pallas_call | solution.py:128
  48.9 7.3 %all-to-all-done.1 = f32[64,8,128]{2,1,0:T(8,128)S(1)} async-done(((f32[64,8,128]{2,1,0:T(8,128)}), f32[64,8,128]{2,1,0:T(8,128)S(1)}, u32[]{:S(2)}, u32[]{:S(2)}) %all-to-all-start.1) | async-done | bytes 262176 | tf_op jit(solution)/shard_map/all_to_all | solution.py:689
  56.2 4.9 %fine.1 = (f32[8,64,1024]{2,1,0:T(8,128)}, f32[16,32,256]{2,1,0:T(8,128)S(1)}) custom-call(s32[1]{0:T(128)} %bitcast.grp_ref, f32[4,8,64,1024]{3,2,1,0:T(8,128)} %still.1.parts_hbm, f32[512,128]{1,0:T(8,128)S(1)} %bitcast.9, bf16[64,64]{1,0:T(8,128)(2,1)} %constant.59.clone.rest_0_, bf16[2,128,256]{2,1,0:T(8,128)(2,1)} %constant.60.clone.rest_1_, ...), custom_call_target="tpu_custom_call" | custom-call | tf_op jit(solution)/shard_map/fine/pallas_call | solution.py:128
  61.1 0.0 copy-start
  61.1 19.2 %all_to_all.20.recv = f32[16,32,256]{2,1,0:T(8,128)S(1)} all-to-all(f32[16,32,256]{2,1,0:T(8,128)S(1)} %get-tuple-element.35), channel_id=1, replica_groups=mesh['grp'=4,'gx_0'=2,'gx_1'=8,'gy'=4] {'gx_0','gx_1'}, dimensions={0} | all-to-all | bytes 1048576 | tf_op jit(solution)/shard_map/all_to_all | solution.py:692
  80.4 1.3 %forward.1 = f32[4,64,256]{2,1,0:T(8,128)} custom-call(f32[16,32,256]{2,1,0:T(8,128)S(1)} %all_to_all.20.recv, bf16[256,512]{1,0:T(8,128)(2,1)S(1)} %get-tuple-element.36.table_high, bf16[256,512]{1,0:T(8,128)(2,1)S(1)} %get-tuple-element.37.table_low, f32[16,256]{1,0:T(8,128)S(1)} %get-tuple-element.38.comb_cos, f32[16,256]{1,0:T(8,128)S(1)} %get-tuple-element.39.comb_sin), custom_call_target="tpu_custom_call" | custom-call | tf_op jit(solution)/shard_map/forward/pallas_call | solution.py:128
  81.7 3.4 %all-to-all-start.3 = ((f32[4,64,256]{2,1,0:T(8,128)}), f32[4,64,256]{2,1,0:T(8,128)S(1)}, u32[]{:S(2)}, u32[]{:S(2)}) async-start(f32[4,64,256]{2,1,0:T(8,128)} %forward.1), calls=%async_computation.3 | async-start | bytes 524288 | tf_op jit(solution)/shard_map/all_to_all | solution.py:693
  86.4 5.3 %all-to-all-done.3.recv = f32[4,64,256]{2,1,0:T(8,128)S(1)} async-done(((f32[4,64,256]{2,1,0:T(8,128)}), f32[4,64,256]{2,1,0:T(8,128)S(1)}, u32[]{:S(2)}, u32[]{:S(2)}) %all-to-all-start.3) | async-done | bytes 262176 | tf_op jit(solution)/shard_map/all_to_all | solution.py:693
  91.7 0.7 finish.1
  (6 shorter events, 0.0 us)
Async XLA Ops:
  1.9 3.8 %collective-permute-start = (f32[48,256]{1,0:T(8,128)S(1)}, f32[48,256]{1,0:T(8,128)S(1)}, u32[]{:S(2)}, u32[]{:S(2)}) collective-permute-start(f32[48,256]{1,0:T(8,128)S(1)} %get-tuple-element.23), channel_id=1, source_target_pairs={{0,1},{1,2},{2,3},{3,0},{4,5},{5,6},{6,7},{7,4},{8,9},{9,10},{10,1... | collective-permute-start | bytes 147464 | tf_op jit(solution)/shard_map/ppermute | solution.py:671
  2.0 3.7 %collective-permute-start.1 = (f32[48,256]{1,0:T(8,128)S(1)}, f32[48,256]{1,0:T(8,128)S(1)}, u32[]{:S(2)}, u32[]{:S(2)}) collective-permute-start(f32[48,256]{1,0:T(8,128)S(1)} %get-tuple-element.24), channel_id=1, source_target_pairs={{0,3},{1,0},{2,1},{3,2},{4,7},{5,4},{6,5},{7,6},{8,11},{9,8},{10,9... | collective-permute-start | bytes 147464 | tf_op jit(solution)/shard_map/ppermute | solution.py:671
  6.4 24.6 %all-to-all-start = ((f32[16,40,128]{2,1,0:T(8,128)}), f32[16,40,128]{2,1,0:T(8,128)S(1)}, u32[]{:S(2)}, u32[]{:S(2)}) async-start(f32[16,40,128]{2,1,0:T(8,128)} %tails.1), calls=%async_computation | async-start | bytes 655360 | tf_op jit(solution)/shard_map/all_to_all | solution.py:683
  17.6 10.2 %collective-permute-start.2 = (f32[64,1024]{1,0:T(8,128)}, f32[64,1024]{1,0:T(8,128)S(1)}, u32[]{:S(2)}, u32[]{:S(2)}) collective-permute-start(f32[64,1024]{1,0:T(8,128)} %get-tuple-element.25), channel_id=1, source_target_pairs={{0,64},{64,128},{128,192},{192,0},{1,65},{65,129},{129,193},{193,1... | collective-permute-start | bytes 786440 | tf_op jit(solution)/shard_map/ppermute | solution.py:671
  19.1 8.7 %collective-permute-start.3 = (f32[64,1024]{1,0:T(8,128)}, f32[64,1024]{1,0:T(8,128)S(1)}, u32[]{:S(2)}, u32[]{:S(2)}) collective-permute-start(f32[64,1024]{1,0:T(8,128)} %get-tuple-element.26), channel_id=1, source_target_pairs={{0,192},{64,0},{128,64},{192,128},{1,193},{65,1},{129,65},{193,129... | collective-permute-start | bytes 786440 | tf_op jit(solution)/shard_map/ppermute | solution.py:671
  27.8 14.2 %copy-start.1 = (f32[64,1024]{1,0:T(8,128)}, f32[64,1024]{1,0:T(8,128)S(1)}, u32[]{:S(2)}) copy-start(f32[64,1024]{1,0:T(8,128)S(1)} %collective-permute-done.2.zlow_hbm) | copy-start | bytes 786436
  27.8 14.2 %copy-start.2 = (f32[64,1024]{1,0:T(8,128)}, f32[64,1024]{1,0:T(8,128)S(1)}, u32[]{:S(2)}) copy-start(f32[64,1024]{1,0:T(8,128)S(1)} %collective-permute-done.3.zhigh_hbm) | copy-start | bytes 786436
  32.6 23.6 %all-to-all-start.1 = ((f32[64,8,128]{2,1,0:T(8,128)}), f32[64,8,128]{2,1,0:T(8,128)S(1)}, u32[]{:S(2)}, u32[]{:S(2)}) async-start(f32[64,8,128]{2,1,0:T(8,128)} %inverse.1), calls=%async_computation.1 | async-start | bytes 524288 | tf_op jit(solution)/shard_map/all_to_all | solution.py:689
  61.1 30.6 %copy-start = (f32[1,2,8,16,256]{4,3,2,1,0:T(8,128)S(1)}, f32[1,2,8,16,256]{4,3,2,1,0:T(8,128)}, u32[]{:S(2)}) copy-start(f32[1,2,8,16,256]{4,3,2,1,0:T(8,128)} %param.21) | copy-start | bytes 786436
  81.7 10.1 %all-to-all-start.3 = ((f32[4,64,256]{2,1,0:T(8,128)}), f32[4,64,256]{2,1,0:T(8,128)S(1)}, u32[]{:S(2)}, u32[]{:S(2)}) async-start(f32[4,64,256]{2,1,0:T(8,128)} %forward.1), calls=%async_computation.3 | async-start | bytes 524288 | tf_op jit(solution)/shard_map/all_to_all | solution.py:693

commit v5 on v4

--- a/solution.py
+++ b/solution.py
@@ -400,8 +400,16 @@
     )(recv, twc, tws, high, low)
 
 
-def still_kernel(me, rate_hbm, sal_hbm, zlow_hbm, zhigh_hbm, edge_cols, from_south, from_north, parts_hbm, rate, salinity, zlow, zhigh, parts, sems, out_sems):
+EARLY = ("ym", "edge")
+LATE = ("ref", "yt", "filt", "fedge", "cm", "rm")
+
+
+def still_kernel(me, rate_hbm, sal_hbm, zlow_hbm, zhigh_hbm, edge_cols, from_south, from_north, *rest):
+    count = len(EARLY)
+    hbm, parts_hbm, kept, rest = rest[:count], rest[count], rest[count + 1 : 2 * count + 1], rest[2 * count + 1 :]
+    rate, salinity, zlow, zhigh, parts, sems, const_sems, out_sems = rest
     copies = fetch(((rate_hbm, rate), (sal_hbm, salinity), (zlow_hbm, zlow), (zhigh_hbm, zhigh)), sems)
+    stores = fetch(tuple(zip(hbm, kept)), const_sems)
     west_t = edge_cols[(me[0] + G - 1) % G, 32:40, :].T
     east_t = edge_cols[(me[0] + 1) % G, 32:40, :].T
     last_row = iota((8, FINE), 0) == 7
@@ -415,7 +423,6 @@
 
     for copy in copies:
         copy.wait()
-    stores = []
     for yb in range(8):
         ys = slice(8 * yb, 8 * yb + 8)
         for l in range(8):
@@ -449,11 +456,12 @@
 
 
 def still(me, rate, salinity, zlow, zhigh, recv1, from_south, from_north):
+    consts = [jnp.asarray(tables()[name]) for name in EARLY]
     return call(
         still_kernel,
-        hds(4, 8, 64, FINE),
-        [SM, HB, HB, HB, HB, VM, VM, VM],
-        HB,
+        [hds(4, 8, 64, FINE)] + [vds(*x.shape, dtype=x.dtype) for x in consts],
+        [SM, HB, HB, HB, HB, VM, VM, VM] + [HB] * len(consts),
+        [HB] + [VM] * len(consts),
         scratch_shapes=[
             pltpu.SMEM((8,), F32),
             pltpu.VMEM((8, 64, FINE), F32),
@@ -461,30 +469,23 @@
             pltpu.VMEM((64, FINE), F32),
             pltpu.VMEM((4, 8, 64, FINE), F32),
             pltpu.SemaphoreType.DMA((4,)),
+            pltpu.SemaphoreType.DMA((len(consts),)),
             pltpu.SemaphoreType.DMA((8,)),
         ],
         limit=24,
         name="still",
-    )(me, rate, salinity, zlow, zhigh, recv1, from_south, from_north)
-
-
-CONSTS = ("ym", "edge", "yt", "filt", "fedge", "ref", "cm", "rm")
-
-
-def fine_kernel(grp_ref, parts_hbm, recv, *rest):
-    hbm, (out, spread), rest = rest[:8], rest[8:10], rest[10:]
-    (y_high, y_low, side, vel, total, warm, new_sal, parts), consts, (sems, in_sems, out_sems) = (
-        rest[:8],
-        rest[8:16],
-        rest[16:],
-    )
-    copies = dict(zip(CONSTS, fetch(tuple(zip(hbm, consts)), sems)))
+    )(me, rate, salinity, zlow, zhigh, recv1, from_south, from_north, *consts)
+
+
+def fine_kernel(grp_ref, parts_hbm, recv, ym, edge, *rest):
+    count = len(LATE)
+    hbm, (out, spread), consts, rest = rest[:count], rest[count : count + 2], rest[count + 2 : 2 * count + 2], rest[2 * count + 2 :]
+    y_high, y_low, side, vel, total, warm, parts, in_sems, sems = rest
+    ref, yt, filt, fedge, cm, rm = consts
+    copies = dict(zip(LATE, fetch(tuple(zip(hbm, consts)), sems)))
     rows = [slice(8 * yb, 8 * yb + 8) for yb in range(8)]
     loads = fetch([(parts_hbm.at[:, :, ys, :], parts.at[:, :, ys, :]) for ys in rows], in_sems)
-    ym, edge, yt, filt, fedge, ref, cm, rm = consts
     grp = grp_ref[0]
-    copies["ym"].wait()
-    copies["edge"].wait()
     row_id = iota((8, 128), 0)
     lane_id = iota((8, 128), 1)
 
@@ -527,7 +528,6 @@
     vel[:, :128] += side[:, :128]
     vel[:, FINE - 128 :] += side[:, 128:]
 
-    stores = []
     for yb in range(8):
         ys = rows[yb]
         loads[yb].wait()
@@ -536,11 +536,9 @@
             acc = None
             for l in range(4 * q, 4 * q + 4):
                 new = parts[0, l, ys, :] - (vx * parts[1, l, ys, :] + vy * parts[2, l, ys, :] + vz * parts[3, l, ys, :])
-                new_sal[l, ys, :] = new
+                out[l, ys, :] = new
                 acc = new if acc is None else acc + new
             total[64 * q + 8 * yb : 64 * q + 8 * yb + 8, :] = acc
-        stores.append(pltpu.make_async_copy(new_sal.at[:, ys, :], out.at[:, ys, :], out_sems.at[yb]))
-        stores[-1].start()
     copies["cm"].wait()
     copies["rm"].wait()
     high, low = halves(total[...])
@@ -549,32 +547,30 @@
     mean = warm[...] - mm(rm[...], jnp.concatenate([high, low], 0))
     for a in range(G):
         spread[a] = mean
-    for store in stores:
-        store.wait()
-
-
-def fine(grp, parts, recv2):
-    consts = [jnp.asarray(tables()[name]) for name in CONSTS]
+
+
+def fine(grp, parts, recv2, early):
+    late = [jnp.asarray(tables()[name]) for name in LATE]
     return call(
         fine_kernel,
-        (sds(8, 64, FINE), vds(G, 32, 256)),
-        [SM, HB, VM] + [HB] * len(consts),
-        [HB, VM],
-        scratch_shapes=[
+        (vds(8, 64, FINE), vds(G, 32, 256)),
+        [SM, HB, VM] + [VM] * len(early) + [HB] * len(late),
+        [VM, VM],
+        scratch_shapes=[pltpu.VMEM(x.shape, x.dtype) for x in late]
+        + [
             pltpu.VMEM((384, 256), BF16),
             pltpu.VMEM((384, 256), BF16),
             pltpu.VMEM((384, 256), F32),
             pltpu.VMEM((384, FINE), F32),
             pltpu.VMEM((128, FINE), F32),
             pltpu.VMEM((32, 256), F32),
-            pltpu.VMEM((8, 64, FINE), F32),
             pltpu.VMEM((4, 8, 64, FINE), F32),
-        ]
-        + [pltpu.VMEM(x.shape, x.dtype) for x in consts]
-        + [pltpu.SemaphoreType.DMA((n,)) for n in (len(consts), 8, 8)],
-        limit=32,
+            pltpu.SemaphoreType.DMA((8,)),
+            pltpu.SemaphoreType.DMA((len(late),)),
+        ],
+        limit=24,
         name="fine",
-    )(grp, parts, recv2.reshape(512, 128), *consts)
+    )(grp, parts, recv2.reshape(512, 128), *early, *late)
 
 
 def stage_kernel(me, inner_hbm, outer_hbm, *rest):
@@ -687,8 +683,8 @@
     recv1, zlow, zhigh = lax.optimization_barrier((recv1, zlow, zhigh))
     send2 = inverse(recv1, *inv)
     recv2 = lax.all_to_all(send2, GRP_GX, 0, 0, tiled=True)
-    parts = still(me, diffusivity, salinity, zlow, zhigh, recv1, from_south, from_north)
-    salinity_next, spread = fine(grp, parts, recv2)
+    parts, *early = still(me, diffusivity, salinity, zlow, zhigh, recv1, from_south, from_north)
+    salinity_next, spread = fine(grp, parts, recv2, early)
     recv3 = lax.all_to_all(spread, GX, 0, 0, tiled=True)
     recv4 = lax.all_to_all(forward(recv3, *weights, *comb), "grp", 0, 0, tiled=True)
     coarse_next = finish(me, viscosity, forcing_gain, recv4, modes)

time: 92.9 us -> 92.6 us (level)
  local copies, waits for them, and re-layouts: 0.01 us -> 1.34 us
  waiting for transfers between devices: 21.6 us -> 20.3 us
    all_to_all x1, waiting for transfers between devices: 5.35 us -> 4.01 us  [per_device(): lax.all_to_all(forward(recv3, *weights, *comb), 'grp', 0, 0, tiled=True)]
    unnamed x6 -> x7, local copies, waits for them, and re-layouts: 0.01 us -> 1.34 us
  transfers between devices with their start and end apart: 7 -> 7, of which waited for: 4 -> 4; matrix products, arithmetic and copies ran while one was open for 0% -> 1% of each run, Pallas kernels for 11% -> 11%
where the time goes in v5:
time: 92.6 us; the launch traced here: 92.2 us
  starting transfers between devices  29.1 us (31%)
  waiting for transfers between devices  20.3 us (22%)
  Pallas kernels  20.2 us (22%)
  blocking collectives  19.1 us (21%)
  between operations  2.05 us (2%)
  local copies, waits for them, and re-layouts  1.34 us (1%)
    pallas_call x9, Pallas kernels, placed(): inner(*[x if spec is not HB else pltpu.with_memory_space_constraint(x, pl...  20.2 us
    all_to_all x1, blocking collectives, per_device(): recv3 = lax.all_to_all(spread, GX, 0, 0, tiled=True)  19.1 us
    all_to_all x1, starting transfers between devices, per_device(): recv1 = lax.all_to_all(chunk, GX, 0, 0, tiled=True)  11.2 us
    all_to_all x1, starting transfers between devices, per_device(): recv2 = lax.all_to_all(send2, GRP_GX, 0, 0, tiled=True)  9.39 us
    all_to_all x1, waiting for transfers between devices, per_device(): recv2 = lax.all_to_all(send2, GRP_GX, 0, 0, tiled=True)  7.38 us
    ppermute x4, waiting for transfers between devices, shifted(): lax.ppermute(array, axis, [(i, (i + step) % count) for i in range(count)])  5.77 us
    ppermute x4, starting transfers between devices, shifted(): lax.ppermute(array, axis, [(i, (i + step) % count) for i in range(count)])  5.05 us
    all_to_all x1, waiting for transfers between devices, per_device(): lax.all_to_all(forward(recv3, *weights, *comb), 'grp', 0, 0, tiled=True)  4.01 us
  transfers between devices with their start and end apart: 7, of which 4 were waited for; matrix products, arithmetic and copies ran while one was open for 1% of the time, Pallas kernels for 11%

profile of v5, /device:TPU:32, one launch (start us, length us, event | category | flops | bytes accessed | tf_op | source)
XLA Modules:
  0.0 92.2 jit_solution(6367285861607058641)
XLA Ops:
  0.6 1.2 %outer_lines.1 = (f32[48,256]{1,0:T(8,128)S(1)}, f32[48,256]{1,0:T(8,128)S(1)}) custom-call(f32[16,16,256]{2,1,0:T(8,128)} %bitcast.6, f32[8,64,1024]{2,1,0:T(8,128)} %sal_hbm.1), custom_call_target="tpu_custom_call" | custom-call | tf_op jit(solution)/shard_map/outer_lines/pallas_call | solution.py:128
  1.9 0.1 collective-permute-start
  2.0 1.7 %collective-permute-start.1 = (f32[48,256]{1,0:T(8,128)S(1)}, f32[48,256]{1,0:T(8,128)S(1)}, u32[]{:S(2)}, u32[]{:S(2)}) collective-permute-start(f32[48,256]{1,0:T(8,128)S(1)} %get-tuple-element.27), channel_id=1, source_target_pairs={{0,3},{1,0},{2,1},{3,2},{4,7},{5,4},{6,5},{7,6},{8,11},{9,8},{10,9... | collective-permute-start | bytes 147464 | tf_op jit(solution)/shard_map/ppermute | solution.py:667
  3.7 2.0 %pack.1 = (f32[16,40,128]{2,1,0:T(8,128)}, f32[16,8,128]{2,1,0:T(8,128)S(1)}, f32[64,1024]{1,0:T(8,128)}, f32[64,1024]{1,0:T(8,128)}) custom-call(s32[1]{0:T(128)} %bitcast.1.me, f32[256,256]{1,0:T(8,128)} %bitcast.7, f32[8,64,1024]{2,1,0:T(8,128)} %sal_hbm.1), custom_call_target="tpu_custom_call" | custom-call | tf_op jit(solution)/shard_map/pack/pallas_call | solution.py:128
  5.7 0.0 collective-permute-done.1.from_north
  5.7 0.7 tails.1
  6.4 11.2 %all-to-all-start = ((f32[16,40,128]{2,1,0:T(8,128)}), f32[16,40,128]{2,1,0:T(8,128)S(1)}, u32[]{:S(2)}, u32[]{:S(2)}) async-start(f32[16,40,128]{2,1,0:T(8,128)} %tails.1), calls=%async_computation | async-start | bytes 655360 | tf_op jit(solution)/shard_map/all_to_all | solution.py:679
  17.6 1.5 %collective-permute-start.2 = (f32[64,1024]{1,0:T(8,128)}, f32[64,1024]{1,0:T(8,128)S(1)}, u32[]{:S(2)}, u32[]{:S(2)}) collective-permute-start(f32[64,1024]{1,0:T(8,128)} %get-tuple-element.28), channel_id=1, source_target_pairs={{0,64},{64,128},{128,192},{192,0},{1,65},{65,129},{129,193},{193,1... | collective-permute-start | bytes 786440 | tf_op jit(solution)/shard_map/ppermute | solution.py:667
  19.1 1.7 %collective-permute-start.3 = (f32[64,1024]{1,0:T(8,128)}, f32[64,1024]{1,0:T(8,128)S(1)}, u32[]{:S(2)}, u32[]{:S(2)}) collective-permute-start(f32[64,1024]{1,0:T(8,128)} %get-tuple-element.29), channel_id=1, source_target_pairs={{0,192},{64,0},{128,64},{192,128},{1,193},{65,1},{129,65},{193,129... | collective-permute-start | bytes 786440 | tf_op jit(solution)/shard_map/ppermute | solution.py:667
  20.8 1.2 %stage.1 = (f32[16,8,128]{2,1,0:T(8,128)S(1)}, f32[16,8,128]{2,1,0:T(8,128)S(1)}, bf16[512,256]{1,0:T(8,128)(2,1)S(1)}, bf16[512,256]{1,0:T(8,128)(2,1)S(1)}, f3...) custom-call(s32[1]{0:T(128)} %bitcast.1.me, ...), custom_call_target="tpu_custom_call" | custom-call | tf_op jit(solution)/shard_map/stage/pallas_call | solution.py:128
  22.1 5.8 %collective-permute-done.2.zlow_hbm = f32[64,1024]{1,0:T(8,128)S(1)} collective-permute-done((f32[64,1024]{1,0:T(8,128)}, f32[64,1024]{1,0:T(8,128)S(1)}, u32[]{:S(2)}, u32[]{:S(2)}) %collective-permute-start.2) | collective-permute-done | bytes 262176 | tf_op jit(solution)/shard_map/ppermute | solution.py:667
  27.8 3.2 %all-to-all-done.edge_cols.recv = f32[16,40,128]{2,1,0:T(8,128)S(1)} async-done(((f32[16,40,128]{2,1,0:T(8,128)}), f32[16,40,128]{2,1,0:T(8,128)S(1)}, u32[]{:S(2)}, u32[]{:S(2)}) %all-to-all-start) | async-done | bytes 327712 | tf_op jit(solution)/shard_map/all_to_all | solution.py:679
  31.0 1.6 %inverse.1 = f32[64,8,128]{2,1,0:T(8,128)} custom-call(f32[16,40,128]{2,1,0:T(8,128)S(1)} %all-to-all-done.edge_cols.recv, f32[16,8,128]{2,1,0:T(8,128)S(1)} %get-tuple-element.34.twc, f32[16,8,128]{2,1,0:T(8,128)S(1)} %get-tuple-element.35.tws, bf16[512,256]{1,0:T(8,128)(2,1)S(1)} %get-tuple-element.36.inv_high, bf16[512,256]{1,0:T(8,128)(2,1)S(1)} %get-tuple-element.37.inv_low), custom_call_target="tpu_custom_call" | custom-call | tf_op jit(solution)/shard_map/inverse/pallas_call | solution.py:128
  32.6 9.4 %all-to-all-start.1 = ((f32[64,8,128]{2,1,0:T(8,128)}), f32[64,8,128]{2,1,0:T(8,128)S(1)}, u32[]{:S(2)}, u32[]{:S(2)}) async-start(f32[64,8,128]{2,1,0:T(8,128)} %inverse.1), calls=%async_computation.1 | async-start | bytes 524288 | tf_op jit(solution)/shard_map/all_to_all | solution.py:685
  42.0 6.8 %still.1 = (f32[4,8,64,1024]{3,2,1,0:T(8,128)}, bf16[64,64]{1,0:T(8,128)(2,1)S(1)}, bf16[2,128,256]{2,1,0:T(8,128)(2,1)S(1)}) custom-call(s32[1]{0:T(128)} %bitcast.1.me, f32[8]{0:T(128)} %rate_hbm.1, f32[8,64,1024]{2,1,0:T(8,128)} %sal_hbm.1, f32[64,1024]{1,0:T(8,128)} %copy-done.1, f32[64,1024]{1,0:T(8,128)} %copy-done.2, ...), custom_call_target="tpu_custom_call" | custom-call | tf_op jit(solution)/shard_map/still/pallas_call | solution.py:128
  48.8 7.4 %all-to-all-done.1 = f32[64,8,128]{2,1,0:T(8,128)S(1)} async-done(((f32[64,8,128]{2,1,0:T(8,128)}), f32[64,8,128]{2,1,0:T(8,128)S(1)}, u32[]{:S(2)}, u32[]{:S(2)}) %all-to-all-start.1) | async-done | bytes 262176 | tf_op jit(solution)/shard_map/all_to_all | solution.py:685
  56.2 4.8 %fine.1 = (f32[8,64,1024]{2,1,0:T(8,128)S(1)}, f32[16,32,256]{2,1,0:T(8,128)S(1)}) custom-call(s32[1]{0:T(128)} %bitcast.grp_ref, f32[4,8,64,1024]{3,2,1,0:T(8,128)} %get-tuple-element.33.parts_hbm, f32[512,128]{1,0:T(8,128)S(1)} %bitcast.9, bf16[64,64]{1,0:T(8,128)(2,1)S(1)} %get-tuple-element.38.ym, bf16[2,128,256]{2,1,0:T(8,128)(2,1)S(1)} %get-tuple-element.39.edge, ...), custom_call_target="tpu_custom_call" | custom-call | tf_op jit(solution)/shard_map/fine/pallas_call | solution.py:128
  60.9 19.1 %all_to_all.20.recv = f32[16,32,256]{2,1,0:T(8,128)S(1)} all-to-all(f32[16,32,256]{2,1,0:T(8,128)S(1)} %get-tuple-element.41), channel_id=1, replica_groups=mesh['grp'=4,'gx_0'=2,'gx_1'=8,'gy'=4] {'gx_0','gx_1'}, dimensions={0} | all-to-all | bytes 1048576 | tf_op jit(solution)/shard_map/all_to_all | solution.py:688
  80.0 1.3 %forward.1 = f32[4,64,256]{2,1,0:T(8,128)} custom-call(f32[16,32,256]{2,1,0:T(8,128)S(1)} %all_to_all.20.recv, bf16[256,512]{1,0:T(8,128)(2,1)S(1)} %get-tuple-element.42.table_high, bf16[256,512]{1,0:T(8,128)(2,1)S(1)} %get-tuple-element.43.table_low, f32[16,256]{1,0:T(8,128)S(1)} %get-tuple-element.44.comb_cos, f32[16,256]{1,0:T(8,128)S(1)} %get-tuple-element.45.comb_sin), custom_call_target="tpu_custom_call" | custom-call | tf_op jit(solution)/shard_map/forward/pallas_call | solution.py:128
  81.3 3.4 %all-to-all-start.3 = ((f32[4,64,256]{2,1,0:T(8,128)}), f32[4,64,256]{2,1,0:T(8,128)S(1)}, u32[]{:S(2)}, u32[]{:S(2)}) async-start(f32[4,64,256]{2,1,0:T(8,128)} %forward.1), calls=%async_computation.3 | async-start | bytes 524288 | tf_op jit(solution)/shard_map/all_to_all | solution.py:689
  86.1 0.0 copy-start
  86.1 1.3 %copy.25 = f32[8,64,1024]{2,1,0:T(8,128)} copy(f32[8,64,1024]{2,1,0:T(8,128)S(1)} %get-tuple-element.46) | data formatting | bytes 4194304
  87.4 4.0 %all-to-all-done.3.recv = f32[4,64,256]{2,1,0:T(8,128)S(1)} async-done(((f32[4,64,256]{2,1,0:T(8,128)}), f32[4,64,256]{2,1,0:T(8,128)S(1)}, u32[]{:S(2)}, u32[]{:S(2)}) %all-to-all-start.3) | async-done | bytes 262176 | tf_op jit(solution)/shard_map/all_to_all | solution.py:689
  91.4 0.7 finish.1
  (7 shorter events, 0.0 us)
Async XLA Ops:
  1.9 3.8 %collective-permute-start = (f32[48,256]{1,0:T(8,128)S(1)}, f32[48,256]{1,0:T(8,128)S(1)}, u32[]{:S(2)}, u32[]{:S(2)}) collective-permute-start(f32[48,256]{1,0:T(8,128)S(1)} %get-tuple-element.26), channel_id=1, source_target_pairs={{0,1},{1,2},{2,3},{3,0},{4,5},{5,6},{6,7},{7,4},{8,9},{9,10},{10,1... | collective-permute-start | bytes 147464 | tf_op jit(solution)/shard_map/ppermute | solution.py:667
  2.0 3.7 %collective-permute-start.1 = (f32[48,256]{1,0:T(8,128)S(1)}, f32[48,256]{1,0:T(8,128)S(1)}, u32[]{:S(2)}, u32[]{:S(2)}) collective-permute-start(f32[48,256]{1,0:T(8,128)S(1)} %get-tuple-element.27), channel_id=1, source_target_pairs={{0,3},{1,0},{2,1},{3,2},{4,7},{5,4},{6,5},{7,6},{8,11},{9,8},{10,9... | collective-permute-start | bytes 147464 | tf_op jit(solution)/shard_map/ppermute | solution.py:667
  6.4 24.6 %all-to-all-start = ((f32[16,40,128]{2,1,0:T(8,128)}), f32[16,40,128]{2,1,0:T(8,128)S(1)}, u32[]{:S(2)}, u32[]{:S(2)}) async-start(f32[16,40,128]{2,1,0:T(8,128)} %tails.1), calls=%async_computation | async-start | bytes 655360 | tf_op jit(solution)/shard_map/all_to_all | solution.py:679
  17.6 10.2 %collective-permute-start.2 = (f32[64,1024]{1,0:T(8,128)}, f32[64,1024]{1,0:T(8,128)S(1)}, u32[]{:S(2)}, u32[]{:S(2)}) collective-permute-start(f32[64,1024]{1,0:T(8,128)} %get-tuple-element.28), channel_id=1, source_target_pairs={{0,64},{64,128},{128,192},{192,0},{1,65},{65,129},{129,193},{193,1... | collective-permute-start | bytes 786440 | tf_op jit(solution)/shard_map/ppermute | solution.py:667
  19.1 8.7 %collective-permute-start.3 = (f32[64,1024]{1,0:T(8,128)}, f32[64,1024]{1,0:T(8,128)S(1)}, u32[]{:S(2)}, u32[]{:S(2)}) collective-permute-start(f32[64,1024]{1,0:T(8,128)} %get-tuple-element.29), channel_id=1, source_target_pairs={{0,192},{64,0},{128,64},{192,128},{1,193},{65,1},{129,65},{193,129... | collective-permute-start | bytes 786440 | tf_op jit(solution)/shard_map/ppermute | solution.py:667
  27.8 14.2 %copy-start.1 = (f32[64,1024]{1,0:T(8,128)}, f32[64,1024]{1,0:T(8,128)S(1)}, u32[]{:S(2)}) copy-start(f32[64,1024]{1,0:T(8,128)S(1)} %collective-permute-done.2.zlow_hbm) | copy-start | bytes 786436
  27.8 14.2 %copy-start.2 = (f32[64,1024]{1,0:T(8,128)}, f32[64,1024]{1,0:T(8,128)S(1)}, u32[]{:S(2)}) copy-start(f32[64,1024]{1,0:T(8,128)S(1)} %collective-permute-done.3.zhigh_hbm) | copy-start | bytes 786436
  32.6 23.6 %all-to-all-start.1 = ((f32[64,8,128]{2,1,0:T(8,128)}), f32[64,8,128]{2,1,0:T(8,128)S(1)}, u32[]{:S(2)}, u32[]{:S(2)}) async-start(f32[64,8,128]{2,1,0:T(8,128)} %inverse.1), calls=%async_computation.1 | async-start | bytes 524288 | tf_op jit(solution)/shard_map/all_to_all | solution.py:685
  81.3 10.1 %all-to-all-start.3 = ((f32[4,64,256]{2,1,0:T(8,128)}), f32[4,64,256]{2,1,0:T(8,128)S(1)}, u32[]{:S(2)}, u32[]{:S(2)}) async-start(f32[4,64,256]{2,1,0:T(8,128)} %forward.1), calls=%async_computation.3 | async-start | bytes 524288 | tf_op jit(solution)/shard_map/all_to_all | solution.py:689
  86.1 5.4 %copy-start = (f32[1,2,8,16,256]{4,3,2,1,0:T(8,128)S(1)}, f32[1,2,8,16,256]{4,3,2,1,0:T(8,128)}, u32[]{:S(2)}) copy-start(f32[1,2,8,16,256]{4,3,2,1,0:T(8,128)} %param.21) | copy-start | bytes 786436

commit v6 on v5

--- a/solution.py
+++ b/solution.py
@@ -51,19 +51,10 @@
         full[c + 1, n] += 1 - abs(o)
         full[c + 1 + (1 if o > 0 else -1), n] += abs(o)
     out["ref"] = full[1:-1][order].astype(jnp.bfloat16)
-    edge = np.zeros((2, 128, 256))
-    filt = np.zeros((W + 2, W))
-    for b in range(W):
-        filt[b : b + 3, b] = (0.125, 0.75, 0.125)
-    out["filt"] = filt[1:-1][order].astype(jnp.bfloat16)
-    fedge = np.zeros((2, 128, 256))
-    for q in range(2):
-        edge[q, 2 * q, :128] = full[0, :128]
-        edge[q, 2 * q + 1, 128:] = full[-1, -128:]
-        fedge[q, 2 * q] = filt[0]
-        fedge[q, 2 * q + 1] = filt[-1]
+    edge = np.zeros((128, 256))
+    edge[0, :128] = full[0, :128]
+    edge[1, 128:] = full[-1, -128:]
     out["edge"] = edge.astype(jnp.bfloat16)
-    out["fedge"] = fedge.astype(jnp.bfloat16)
     ym = np.zeros((64, 32))
     yt = np.zeros((16, 32))
     place = lambda c: 16 if c < 0 else 17 if c > 15 else c
@@ -314,7 +305,7 @@
     return out
 
 
-def inverse_kernel(recv, twc, tws, inv_high, inv_low, send, left_high, left_low, mid):
+def inverse_kernel(recv, twc, tws, inv_high, inv_low, send_hbm, left_high, left_low, mid, send, sems):
     row_id = iota((8, 128), 0)
     lane_id = iota((8, 128), 1)
 
@@ -370,6 +361,7 @@
     left = [roll(second[d], 1, 1) for d in range(G)]
     right = [roll(first[d], 1, 1) for d in range(G)]
     side = [roll(single[d], 5, 1) for d in range(G)]
+    stores = []
     for d in range(G):
         before, after = (d - 1) % G, (d + 1) % G
         own = jnp.where(lane_id == 0, left[before], jnp.where(lane_id == 1, right[after], 0.0))
@@ -382,31 +374,37 @@
             tile = jnp.where(row_id < 2, roll(first[d], -2 * g, 0), base)
             tile = jnp.where((row_id == 4) | (row_id == 5), roll(second[d], 4 - 2 * g, 0), tile)
             tile = jnp.where((row_id == 3) & (lane_id < 4), roll(rim, 3 - 2 * g, 0), tile)
-            send[16 * g + d] = tile
+            send[g, d] = tile
+        if d % 4 == 3:
+            ds = slice(d - 3, d + 1)
+            stores += fetch(((send.at[:, ds], send_hbm.at[:, ds]),), sems, d // 4)
+    for store in stores:
+        store.wait()
 
 
 def inverse(recv, twc, tws, high, low):
     return call(
         inverse_kernel,
-        sds(64, 8, 128),
+        hds(4, G, 8, 128),
         [VM] * 5,
-        VM,
+        HB,
         scratch_shapes=[
             pltpu.VMEM((256, 512), BF16),
             pltpu.VMEM((256, 512), BF16),
             pltpu.VMEM((256, 256), F32),
+            pltpu.VMEM((4, G, 8, 128), F32),
+            pltpu.SemaphoreType.DMA((4,)),
         ],
         name="inverse",
-    )(recv, twc, tws, high, low)
-
-
-EARLY = ("ym", "edge")
-LATE = ("ref", "yt", "filt", "fedge", "cm", "rm")
+    )(recv, twc, tws, high, low).reshape(64, 8, 128)
+
+
+EARLY = ("ym", "yt", "edge", "ref", "rm", "cm")
 
 
 def still_kernel(me, rate_hbm, sal_hbm, zlow_hbm, zhigh_hbm, edge_cols, from_south, from_north, *rest):
     count = len(EARLY)
-    hbm, parts_hbm, kept, rest = rest[:count], rest[count], rest[count + 1 : 2 * count + 1], rest[2 * count + 1 :]
+    hbm, (base, parts_hbm), kept, rest = rest[:count], rest[count : count + 2], rest[count + 2 : 2 * count + 2], rest[2 * count + 2 :]
     rate, salinity, zlow, zhigh, parts, sems, const_sems, out_sems = rest
     copies = fetch(((rate_hbm, rate), (sal_hbm, salinity), (zlow_hbm, zlow), (zhigh_hbm, zhigh)), sems)
     stores = fetch(tuple(zip(hbm, kept)), const_sems)
@@ -445,10 +443,10 @@
             e = jnp.concatenate([e[:, :-128], jnp.where(last_lane, ecol, e[:, -128:])], 1)
             w = jnp.concatenate([jnp.where(first_lane, wcol, w[:, :128]), w[:, 128:]], 1)
             k = rate[l] * 0.1
-            parts[0, l, ys, :] = c + k * (((e + w) + (north + south)) + (upper + lower) - 6.0 * c)
-            parts[1, l, ys, :] = (e - w) * 0.05
-            parts[2, l, ys, :] = (north - south) * 0.05
-            parts[3, l, ys, :] = (upper - lower) * 0.05
+            base[l, ys, :] = c + k * (((e + w) + (north + south)) + (upper + lower) - 6.0 * c)
+            parts[0, l, ys, :] = (e - w) * 0.05
+            parts[1, l, ys, :] = (north - south) * 0.05
+            parts[2, l, ys, :] = (upper - lower) * 0.05
         stores.append(pltpu.make_async_copy(parts.at[:, :, ys, :], parts_hbm.at[:, :, ys, :], out_sems.at[yb]))
         stores[-1].start()
     for store in stores:
@@ -459,15 +457,15 @@
     consts = [jnp.asarray(tables()[name]) for name in EARLY]
     return call(
         still_kernel,
-        [hds(4, 8, 64, FINE)] + [vds(*x.shape, dtype=x.dtype) for x in consts],
+        [vds(8, 64, FINE), hds(3, 8, 64, FINE)] + [vds(*x.shape, dtype=x.dtype) for x in consts],
         [SM, HB, HB, HB, HB, VM, VM, VM] + [HB] * len(consts),
-        [HB] + [VM] * len(consts),
+        [VM, HB] + [VM] * len(consts),
         scratch_shapes=[
             pltpu.SMEM((8,), F32),
             pltpu.VMEM((8, 64, FINE), F32),
             pltpu.VMEM((64, FINE), F32),
             pltpu.VMEM((64, FINE), F32),
-            pltpu.VMEM((4, 8, 64, FINE), F32),
+            pltpu.VMEM((3, 8, 64, FINE), F32),
             pltpu.SemaphoreType.DMA((4,)),
             pltpu.SemaphoreType.DMA((len(consts),)),
             pltpu.SemaphoreType.DMA((8,)),
@@ -477,12 +475,28 @@
     )(me, rate, salinity, zlow, zhigh, recv1, from_south, from_north, *consts)
 
 
-def fine_kernel(grp_ref, parts_hbm, recv, ym, edge, *rest):
-    count = len(LATE)
-    hbm, (out, spread), consts, rest = rest[:count], rest[count : count + 2], rest[count + 2 : 2 * count + 2], rest[2 * count + 2 :]
-    y_high, y_low, side, vel, total, warm, parts, in_sems, sems = rest
-    ref, yt, filt, fedge, cm, rm = consts
-    copies = dict(zip(LATE, fetch(tuple(zip(hbm, consts)), sems)))
+def fine_kernel(
+    grp_ref,
+    base,
+    parts_hbm,
+    recv,
+    ym,
+    yt,
+    edge,
+    ref,
+    rm,
+    cm,
+    out,
+    spread,
+    y_high,
+    y_low,
+    side_high,
+    side_low,
+    vel,
+    total,
+    parts,
+    in_sems,
+):
     rows = [slice(8 * yb, 8 * yb + 8) for yb in range(8)]
     loads = fetch([(parts_hbm.at[:, :, ys, :], parts.at[:, :, ys, :]) for ys in rows], in_sems)
     grp = grp_ref[0]
@@ -497,7 +511,7 @@
         for x, row in zip(main, (2, 6, 3)):
             s, n = roll(south, -row, 0), roll(north, 1 - row, 0)
             if row == 3:
-                s, n = roll(s, 2 * q - 4, 1), roll(n, 2 * q - 4, 1)
+                x, s, n = roll(x, -2 * q, 1), roll(s, -4, 1), roll(n, -4, 1)
             tile = jnp.where(row_id == 0, s, jnp.where(row_id == 1, n, 0.0))
             parts.append(jnp.concatenate([x, tile, jnp.zeros((8, 128), F32)], 0))
         return jnp.concatenate(parts, 1)
@@ -506,25 +520,14 @@
         high, low = halves(lines(f, q))
         return mm(table[...], jnp.concatenate([high, low], 0))
 
-    for f in range(3):
+    for f in range(4):
         for q in range(2):
-            at = slice(64 * (2 * f + q), 64 * (2 * f + q) + 64)
-            high, low = halves(along_y(ym, f, q))
-            y_high[at, :] = high[:, :256]
-            y_low[at, :] = low[:, :256]
-            side[at, :] = mm(high[:, 256:], edge[q]) + mm(low[:, 256:], edge[q])
-    for name in ("yt", "filt", "fedge"):
-        copies[name].wait()
-    for q in range(2):
-        high, low = halves(along_y(yt, 3, q))
-        warm[16 * q : 16 * q + 16, :] = (
-            mm(high[:, :256], filt[...])
-            + mm(low[:, :256], filt[...])
-            + mm(high[:, 256:], fedge[q])
-            + mm(low[:, 256:], fedge[q])
-        )
-    copies["ref"].wait()
+            at = slice(64 * (2 * f + q), 64 * (2 * f + q) + 64) if f < 3 else slice(384 + 16 * q, 400 + 16 * q)
+            high, low = halves(along_y(ym if f < 3 else yt, f, q))
+            y_high[at, :], side_high[at, :] = high[:, :256], high[:, 256:]
+            y_low[at, :], side_low[at, :] = low[:, :256], low[:, 256:]
     vel[...] = mm(y_high[...], ref[...]) + mm(y_low[...], ref[...])
+    side = mm(side_high[...], edge[...]) + mm(side_low[...], edge[...])
     vel[:, :128] += side[:, :128]
     vel[:, FINE - 128 :] += side[:, 128:]
 
@@ -535,47 +538,44 @@
             vx, vy, vz = (vel[64 * (2 * f + q) + 8 * yb : 64 * (2 * f + q) + 8 * yb + 8, :] for f in range(3))
             acc = None
             for l in range(4 * q, 4 * q + 4):
-                new = parts[0, l, ys, :] - (vx * parts[1, l, ys, :] + vy * parts[2, l, ys, :] + vz * parts[3, l, ys, :])
+                new = base[l, ys, :] - (vx * parts[0, l, ys, :] + vy * parts[1, l, ys, :] + vz * parts[2, l, ys, :])
                 out[l, ys, :] = new
                 acc = new if acc is None else acc + new
             total[64 * q + 8 * yb : 64 * q + 8 * yb + 8, :] = acc
-    copies["cm"].wait()
-    copies["rm"].wait()
     high, low = halves(total[...])
+    high, low = halves(vel[384:416, :] - mm(rm[...], jnp.concatenate([high, low], 0)))
     means = [mm(high[:, at], cm[...]) + mm(low[:, at], cm[...]) for at in (slice(0, 512), slice(512, FINE))]
-    high, low = halves(jnp.concatenate(means, 1))
-    mean = warm[...] - mm(rm[...], jnp.concatenate([high, low], 0))
+    mean = jnp.concatenate(means, 1)
     for a in range(G):
         spread[a] = mean
 
 
-def fine(grp, parts, recv2, early):
-    late = [jnp.asarray(tables()[name]) for name in LATE]
+def fine(grp, base, parts, recv2, consts):
     return call(
         fine_kernel,
         (vds(8, 64, FINE), vds(G, 32, 256)),
-        [SM, HB, VM] + [VM] * len(early) + [HB] * len(late),
+        [SM, VM, HB, VM] + [VM] * len(consts),
         [VM, VM],
-        scratch_shapes=[pltpu.VMEM(x.shape, x.dtype) for x in late]
-        + [
-            pltpu.VMEM((384, 256), BF16),
-            pltpu.VMEM((384, 256), BF16),
-            pltpu.VMEM((384, 256), F32),
-            pltpu.VMEM((384, FINE), F32),
+        input_output_aliases={1: 0},
+        scratch_shapes=[
+            pltpu.VMEM((416, 256), BF16),
+            pltpu.VMEM((416, 256), BF16),
+            pltpu.VMEM((416, 128), BF16),
+            pltpu.VMEM((416, 128), BF16),
+            pltpu.VMEM((416, FINE), F32),
             pltpu.VMEM((128, FINE), F32),
-            pltpu.VMEM((32, 256), F32),
-            pltpu.VMEM((4, 8, 64, FINE), F32),
+            pltpu.VMEM((3, 8, 64, FINE), F32),
             pltpu.SemaphoreType.DMA((8,)),
-            pltpu.SemaphoreType.DMA((len(late),)),
         ],
-        limit=24,
+        limit=20,
         name="fine",
-    )(grp, parts, recv2.reshape(512, 128), *early, *late)
+    )(grp, base, parts, recv2.reshape(512, 128), *consts)
 
 
 def stage_kernel(me, inner_hbm, outer_hbm, *rest):
-    count = (len(rest) - 5) // 2
-    hbm, dst, (high, low, inner, outer, sems) = rest[:count], rest[count : 2 * count], rest[2 * count :]
+    count = (len(rest) - 8) // 2
+    hbm, dst, rest = rest[:count], rest[count : 2 * count], rest[2 * count :]
+    high_hbm, low_hbm, high, low, inner, outer, sems, out_sems = rest
     copies = fetch(((inner_hbm, inner), (outer_hbm, outer)) + tuple(zip(hbm, dst)), sems)
     turns = (iota((16, 128), 0) * me[0]) % G
     angle = turns.astype(F32) * (2.0 * math.pi / G)
@@ -589,29 +589,33 @@
         value = cmul(real, imag, outer[t : t + 1, :256], outer[t : t + 1, 256:])
         for at in range(2):
             high[rows, 256 * at : 256 * at + 256], low[rows, 256 * at : 256 * at + 256] = halves(value[at])
-    for copy in copies[2:]:
+    for copy in copies[2:] + fetch(((high, high_hbm), (low, low_hbm)), out_sems):
         copy.wait()
 
 
 def stage(me):
     t = tables()
-    consts = [jnp.asarray(x) for x in (*t["tw"], *t["inv"], *t["comb"])]
+    consts = [jnp.asarray(x) for x in (*t["tw"], *t["inv"])]
     out = call(
         stage_kernel,
-        [vds(*x.shape, dtype=x.dtype) for x in consts] + [vds(256, 512, dtype=BF16)] * 2,
+        [vds(*x.shape, dtype=x.dtype) for x in consts] + [hds(256, 512, dtype=BF16)] * 2,
         [SM, HB, HB] + [HB] * len(consts),
-        [VM] * (len(consts) + 2),
+        [VM] * len(consts) + [HB] * 2,
         scratch_shapes=[
+            pltpu.VMEM((256, 512), BF16),
+            pltpu.VMEM((256, 512), BF16),
             pltpu.VMEM((G, 512), F32),
             pltpu.VMEM((G, 512), F32),
             pltpu.SemaphoreType.DMA((len(consts) + 2,)),
+            pltpu.SemaphoreType.DMA((2,)),
         ],
         name="stage",
     )(me, *map(jnp.asarray, t["fwd"]), *consts)
-    return out[0:4], out[4:6], out[6:8]
-
-
-def forward_kernel(recv, table_high, table_low, comb_cos, comb_sin, out, left_high, left_low, mid):
+    return out[0:4], out[4:6]
+
+
+def forward_kernel(recv, table_high, table_low, cos_hbm, sin_hbm, out, left_high, left_low, mid, comb_cos, comb_sin, sems):
+    copies = fetch(((cos_hbm, comb_cos), (sin_hbm, comb_sin)), sems)
     for a in range(G):
         high, low = halves(recv[a])
         left_high[32 * a : 32 * a + 32, :] = high
@@ -619,6 +623,8 @@
     mid[...] = (
         mm(left_high[...], table_high[...]) + mm(left_low[...], table_high[...]) + mm(left_high[...], table_low[...])
     )
+    for copy in copies:
+        copy.wait()
     real = imag = jnp.zeros((32, 256), F32)
     for a in range(G):
         c, s = comb_cos[a : a + 1, :], comb_sin[a : a + 1, :]
@@ -630,19 +636,22 @@
         out[g, 32:64, :] = imag
 
 
-def forward(recv, high, low, cos, sin):
+def forward(recv, high, low):
     return call(
         forward_kernel,
         sds(4, 64, 256),
-        [VM] * 5,
+        [VM, VM, VM, HB, HB],
         VM,
         scratch_shapes=[
             pltpu.VMEM((512, 256), BF16),
             pltpu.VMEM((512, 256), BF16),
             pltpu.VMEM((512, 512), F32),
+            pltpu.VMEM((G, 256), F32),
+            pltpu.VMEM((G, 256), F32),
+            pltpu.SemaphoreType.DMA((2,)),
         ],
         name="forward",
-    )(recv, high, low, cos, sin)
+    )(recv, high, low, *map(jnp.asarray, tables()["comb"]))
 
 
 def finish_kernel(me, viscosity, gain, recv, modes, out):
@@ -677,16 +686,16 @@
     chunk, tail, low_face, high_face = pack(me, modes, salinity)
     chunk = tails(chunk, tail, from_south, from_north)
     recv1 = lax.all_to_all(chunk, GX, 0, 0, tiled=True)
-    inv, comb, weights = stage(me)
+    inv, weights = stage(me)
     zlow = shifted(high_face, "grp", 1)
     zhigh = shifted(low_face, "grp", -1)
     recv1, zlow, zhigh = lax.optimization_barrier((recv1, zlow, zhigh))
     send2 = inverse(recv1, *inv)
     recv2 = lax.all_to_all(send2, GRP_GX, 0, 0, tiled=True)
-    parts, *early = still(me, diffusivity, salinity, zlow, zhigh, recv1, from_south, from_north)
-    salinity_next, spread = fine(grp, parts, recv2, early)
+    base, parts, *consts = still(me, diffusivity, salinity, zlow, zhigh, recv1, from_south, from_north)
+    salinity_next, spread = fine(grp, base, parts, recv2, consts)
     recv3 = lax.all_to_all(spread, GX, 0, 0, tiled=True)
-    recv4 = lax.all_to_all(forward(recv3, *weights, *comb), "grp", 0, 0, tiled=True)
+    recv4 = lax.all_to_all(forward(recv3, *weights), "grp", 0, 0, tiled=True)
     coarse_next = finish(me, viscosity, forcing_gain, recv4, modes)
     return (salinity_next, coarse_next.reshape(coarse_modes.shape))
 

time: 92.6 us -> 92.5 us (level)
  no operation moved by 1% of the time
where the time goes in v6:
time: 92.5 us; the launch traced here: 92 us
  starting transfers between devices  29.1 us (31%)
  waiting for transfers between devices  20.2 us (22%)
  Pallas kernels  20.1 us (22%)
  blocking collectives  19.1 us (21%)
  between operations  2.06 us (2%)
  local copies, waits for them, and re-layouts  1.34 us (1%)
    pallas_call x9, Pallas kernels, placed(): inner(*[x if spec is not HB else pltpu.with_memory_space_constraint(x, pl...  20.1 us
    all_to_all x1, blocking collectives, per_device(): recv3 = lax.all_to_all(spread, GX, 0, 0, tiled=True)  19.1 us
    all_to_all x1, starting transfers between devices, per_device(): recv1 = lax.all_to_all(chunk, GX, 0, 0, tiled=True)  11.2 us
    all_to_all x1, starting transfers between devices, per_device(): recv2 = lax.all_to_all(send2, GRP_GX, 0, 0, tiled=True)  9.4 us
    all_to_all x1, waiting for transfers between devices, per_device(): recv2 = lax.all_to_all(send2, GRP_GX, 0, 0, tiled=True)  7.74 us
    ppermute x4, waiting for transfers between devices, shifted(): lax.ppermute(array, axis, [(i, (i + step) % count) for i in range(count)])  5.27 us
    ppermute x4, starting transfers between devices, shifted(): lax.ppermute(array, axis, [(i, (i + step) % count) for i in range(count)])  5.05 us
    all_to_all x1, waiting for transfers between devices, per_device(): recv4 = lax.all_to_all(forward(recv3, *weights), 'grp', 0, 0, tiled=True)  4.01 us
  transfers between devices with their start and end apart: 7, of which 4 were waited for; matrix products, arithmetic and copies ran while one was open for 1% of the time, Pallas kernels for 11%

profile of v6, /device:TPU:32, one launch (start us, length us, event | category | flops | bytes accessed | tf_op | source)
XLA Modules:
  0.0 92.0 jit_solution(15026291129520638160)
XLA Ops:
  0.6 1.2 %outer_lines.1 = (f32[48,256]{1,0:T(8,128)S(1)}, f32[48,256]{1,0:T(8,128)S(1)}) custom-call(f32[16,16,256]{2,1,0:T(8,128)} %bitcast.7, f32[8,64,1024]{2,1,0:T(8,128)} %sal_hbm.1), custom_call_target="tpu_custom_call" | custom-call | tf_op jit(solution)/shard_map/outer_lines/pallas_call | solution.py:119
  1.9 0.1 collective-permute-start
  2.0 1.7 %collective-permute-start.1 = (f32[48,256]{1,0:T(8,128)S(1)}, f32[48,256]{1,0:T(8,128)S(1)}, u32[]{:S(2)}, u32[]{:S(2)}) collective-permute-start(f32[48,256]{1,0:T(8,128)S(1)} %get-tuple-element.30), channel_id=1, source_target_pairs={{0,3},{1,0},{2,1},{3,2},{4,7},{5,4},{6,5},{7,6},{8,11},{9,8},{10,9... | collective-permute-start | bytes 147464 | tf_op jit(solution)/shard_map/ppermute | solution.py:676
  3.7 2.0 %pack.1 = (f32[16,40,128]{2,1,0:T(8,128)}, f32[16,8,128]{2,1,0:T(8,128)S(1)}, f32[64,1024]{1,0:T(8,128)}, f32[64,1024]{1,0:T(8,128)}) custom-call(s32[1]{0:T(128)} %bitcast.1.me, f32[256,256]{1,0:T(8,128)} %bitcast.8, f32[8,64,1024]{2,1,0:T(8,128)} %sal_hbm.1), custom_call_target="tpu_custom_call" | custom-call | tf_op jit(solution)/shard_map/pack/pallas_call | solution.py:119
  5.7 0.0 collective-permute-done.from_south
  5.7 0.7 tails.1
  6.4 11.2 %all-to-all-start = ((f32[16,40,128]{2,1,0:T(8,128)}), f32[16,40,128]{2,1,0:T(8,128)S(1)}, u32[]{:S(2)}, u32[]{:S(2)}) async-start(f32[16,40,128]{2,1,0:T(8,128)} %tails.1), calls=%async_computation | async-start | bytes 655360 | tf_op jit(solution)/shard_map/all_to_all | solution.py:688
  17.6 1.5 %collective-permute-start.2 = (f32[64,1024]{1,0:T(8,128)}, f32[64,1024]{1,0:T(8,128)S(1)}, u32[]{:S(2)}, u32[]{:S(2)}) collective-permute-start(f32[64,1024]{1,0:T(8,128)} %get-tuple-element.31), channel_id=1, source_target_pairs={{0,64},{64,128},{128,192},{192,0},{1,65},{65,129},{129,193},{193,1... | collective-permute-start | bytes 786440 | tf_op jit(solution)/shard_map/ppermute | solution.py:676
  19.1 1.7 %collective-permute-start.3 = (f32[64,1024]{1,0:T(8,128)}, f32[64,1024]{1,0:T(8,128)S(1)}, u32[]{:S(2)}, u32[]{:S(2)}) collective-permute-start(f32[64,1024]{1,0:T(8,128)} %get-tuple-element.32), channel_id=1, source_target_pairs={{0,192},{64,0},{128,64},{192,128},{1,193},{65,1},{129,65},{193,129... | collective-permute-start | bytes 786440 | tf_op jit(solution)/shard_map/ppermute | solution.py:676
  20.8 1.7 %stage.1 = (f32[16,8,128]{2,1,0:T(8,128)S(1)}, f32[16,8,128]{2,1,0:T(8,128)S(1)}, bf16[512,256]{1,0:T(8,128)(2,1)S(1)}, bf16[512,256]{1,0:T(8,128)(2,1)S(1)}, bf...) custom-call(s32[1]{0:T(128)} %bitcast.1.me, f32[16,512]{1,0:T(8,128)} %constant.51.clone.inner_hbm, ...), custom_call_target="tpu_custom_call" | custom-call | tf_op jit(solution)/shard_map/stage/pallas_call | solution.py:119
  22.6 5.3 %collective-permute-done.2.zlow_hbm = f32[64,1024]{1,0:T(8,128)S(1)} collective-permute-done((f32[64,1024]{1,0:T(8,128)}, f32[64,1024]{1,0:T(8,128)S(1)}, u32[]{:S(2)}, u32[]{:S(2)}) %collective-permute-start.2) | collective-permute-done | bytes 262176 | tf_op jit(solution)/shard_map/ppermute | solution.py:676
  27.8 3.2 %all-to-all-done.edge_cols.recv = f32[16,40,128]{2,1,0:T(8,128)S(1)} async-done(((f32[16,40,128]{2,1,0:T(8,128)}), f32[16,40,128]{2,1,0:T(8,128)S(1)}, u32[]{:S(2)}, u32[]{:S(2)}) %all-to-all-start) | async-done | bytes 327712 | tf_op jit(solution)/shard_map/all_to_all | solution.py:688
  31.0 1.6 %inverse.1 = f32[4,16,8,128]{3,2,1,0:T(8,128)} custom-call(f32[16,40,128]{2,1,0:T(8,128)S(1)} %all-to-all-done.edge_cols.recv, f32[16,8,128]{2,1,0:T(8,128)S(1)} %get-tuple-element.38.twc, f32[16,8,128]{2,1,0:T(8,128)S(1)} %get-tuple-element.39.tws, bf16[512,256]{1,0:T(8,128)(2,1)S(1)} %get-tuple-element.40.inv_high, ...), custom_call_target="tpu_custom_call" | custom-call | tf_op jit(solution)/shard_map/inverse/pallas_call | solution.py:119
  32.6 9.4 %all-to-all-start.1 = ((f32[64,8,128]{2,1,0:T(8,128)}), f32[64,8,128]{2,1,0:T(8,128)S(1)}, u32[]{:S(2)}, u32[]{:S(2)}) async-start(f32[64,8,128]{2,1,0:T(8,128)} %bitcast.11), calls=%async_computation.1 | async-start | bytes 524288 | tf_op jit(solution)/shard_map/all_to_all | solution.py:694
  42.1 6.4 %still.1 = (f32[8,64,1024]{2,1,0:T(8,128)S(1)}, f32[3,8,64,1024]{3,2,1,0:T(8,128)}, bf16[64,64]{1,0:T(8,128)(2,1)S(1)}, bf16[16,64]{1,0:T(8,128)(2,1)S(1)}, bf16...) custom-call(s32[1]{0:T(128)} %bitcast.1.me, ...), custom_call_target="tpu_custom_call" | custom-call | tf_op jit(solution)/shard_map/still/pallas_call | solution.py:119
  48.5 7.7 %all-to-all-done.1 = f32[64,8,128]{2,1,0:T(8,128)S(1)} async-done(((f32[64,8,128]{2,1,0:T(8,128)}), f32[64,8,128]{2,1,0:T(8,128)S(1)}, u32[]{:S(2)}, u32[]{:S(2)}) %all-to-all-start.1) | async-done | bytes 262176 | tf_op jit(solution)/shard_map/all_to_all | solution.py:694
  56.2 4.0 %fine.1 = (f32[8,64,1024]{2,1,0:T(8,128)S(1)}, f32[16,32,256]{2,1,0:T(8,128)S(1)}) custom-call(s32[1]{0:T(128)} %bitcast.grp_ref, f32[8,64,1024]{2,1,0:T(8,128)S(1)} %get-tuple-element.36.base, f32[3,8,64,1024]{3,2,1,0:T(8,128)} %get-tuple-element.37.parts_hbm, f32[512,128]{1,0:T(8,128)S(1)} %bitcast.10, ...), custom_call_target="tpu_custom_call", output_to_operand_aliasing={{0}: (1, {})} | custom-call | tf_op jit(solution)/shard_map/fine/pallas_call | solution.py:119
  60.2 19.1 %all_to_all.20.recv = f32[16,32,256]{2,1,0:T(8,128)S(1)} all-to-all(f32[16,32,256]{2,1,0:T(8,128)S(1)} %get-tuple-element.49), channel_id=1, replica_groups=mesh['grp'=4,'gx_0'=2,'gx_1'=8,'gy'=4] {'gx_0','gx_1'}, dimensions={0} | all-to-all | bytes 1048576 | tf_op jit(solution)/shard_map/all_to_all | solution.py:697
  79.3 1.9 %forward.1 = f32[4,64,256]{2,1,0:T(8,128)} custom-call(f32[16,32,256]{2,1,0:T(8,128)S(1)} %all_to_all.20.recv, bf16[256,512]{1,0:T(8,128)(2,1)S(1)} %copy-done.1, bf16[256,512]{1,0:T(8,128)(2,1)S(1)} %copy-done.2, f32[16,256]{1,0:T(8,128)} %constant.59.clone.cos_hbm, f32[16,256]{1,0:T(8,128)} %constant.60.clone.sin_hbm), custom_call_target="tpu_custom_call" | custom-call | tf_op jit(solution)/shard_map/forward/pallas_call | solution.py:119
  81.2 3.4 %all-to-all-start.3 = ((f32[4,64,256]{2,1,0:T(8,128)}), f32[4,64,256]{2,1,0:T(8,128)S(1)}, u32[]{:S(2)}, u32[]{:S(2)}) async-start(f32[4,64,256]{2,1,0:T(8,128)} %forward.1), calls=%async_computation.3 | async-start | bytes 524288 | tf_op jit(solution)/shard_map/all_to_all | solution.py:698
  85.9 0.0 copy-start
  85.9 1.3 %copy.25 = f32[8,64,1024]{2,1,0:T(8,128)} copy(f32[8,64,1024]{2,1,0:T(8,128)S(1)} %get-tuple-element.52) | data formatting | bytes 4194304
  87.2 4.0 %all-to-all-done.3.recv = f32[4,64,256]{2,1,0:T(8,128)S(1)} async-done(((f32[4,64,256]{2,1,0:T(8,128)}), f32[4,64,256]{2,1,0:T(8,128)S(1)}, u32[]{:S(2)}, u32[]{:S(2)}) %all-to-all-start.3) | async-done | bytes 262176 | tf_op jit(solution)/shard_map/all_to_all | solution.py:698
  91.2 0.7 finish.1
  (11 shorter events, 0.0 us)
Async XLA Ops:
  1.9 3.8 %collective-permute-start = (f32[48,256]{1,0:T(8,128)S(1)}, f32[48,256]{1,0:T(8,128)S(1)}, u32[]{:S(2)}, u32[]{:S(2)}) collective-permute-start(f32[48,256]{1,0:T(8,128)S(1)} %get-tuple-element.29), channel_id=1, source_target_pairs={{0,1},{1,2},{2,3},{3,0},{4,5},{5,6},{6,7},{7,4},{8,9},{9,10},{10,1... | collective-permute-start | bytes 147464 | tf_op jit(solution)/shard_map/ppermute | solution.py:676
  2.0 3.7 %collective-permute-start.1 = (f32[48,256]{1,0:T(8,128)S(1)}, f32[48,256]{1,0:T(8,128)S(1)}, u32[]{:S(2)}, u32[]{:S(2)}) collective-permute-start(f32[48,256]{1,0:T(8,128)S(1)} %get-tuple-element.30), channel_id=1, source_target_pairs={{0,3},{1,0},{2,1},{3,2},{4,7},{5,4},{6,5},{7,6},{8,11},{9,8},{10,9... | collective-permute-start | bytes 147464 | tf_op jit(solution)/shard_map/ppermute | solution.py:676
  6.4 24.6 %all-to-all-start = ((f32[16,40,128]{2,1,0:T(8,128)}), f32[16,40,128]{2,1,0:T(8,128)S(1)}, u32[]{:S(2)}, u32[]{:S(2)}) async-start(f32[16,40,128]{2,1,0:T(8,128)} %tails.1), calls=%async_computation | async-start | bytes 655360 | tf_op jit(solution)/shard_map/all_to_all | solution.py:688
  17.6 10.2 %collective-permute-start.2 = (f32[64,1024]{1,0:T(8,128)}, f32[64,1024]{1,0:T(8,128)S(1)}, u32[]{:S(2)}, u32[]{:S(2)}) collective-permute-start(f32[64,1024]{1,0:T(8,128)} %get-tuple-element.31), channel_id=1, source_target_pairs={{0,64},{64,128},{128,192},{192,0},{1,65},{65,129},{129,193},{193,1... | collective-permute-start | bytes 786440 | tf_op jit(solution)/shard_map/ppermute | solution.py:676
  19.1 8.7 %collective-permute-start.3 = (f32[64,1024]{1,0:T(8,128)}, f32[64,1024]{1,0:T(8,128)S(1)}, u32[]{:S(2)}, u32[]{:S(2)}) collective-permute-start(f32[64,1024]{1,0:T(8,128)} %get-tuple-element.32), channel_id=1, source_target_pairs={{0,192},{64,0},{128,64},{192,128},{1,193},{65,1},{129,65},{193,129... | collective-permute-start | bytes 786440 | tf_op jit(solution)/shard_map/ppermute | solution.py:676
  27.8 14.2 %copy-start.3 = (f32[64,1024]{1,0:T(8,128)}, f32[64,1024]{1,0:T(8,128)S(1)}, u32[]{:S(2)}) copy-start(f32[64,1024]{1,0:T(8,128)S(1)} %collective-permute-done.2.zlow_hbm) | copy-start | bytes 786436
  27.8 14.2 %copy-start.4 = (f32[64,1024]{1,0:T(8,128)}, f32[64,1024]{1,0:T(8,128)S(1)}, u32[]{:S(2)}) copy-start(f32[64,1024]{1,0:T(8,128)S(1)} %collective-permute-done.3.zhigh_hbm) | copy-start | bytes 786436
  32.6 23.6 %all-to-all-start.1 = ((f32[64,8,128]{2,1,0:T(8,128)}), f32[64,8,128]{2,1,0:T(8,128)S(1)}, u32[]{:S(2)}, u32[]{:S(2)}) async-start(f32[64,8,128]{2,1,0:T(8,128)} %bitcast.11), calls=%async_computation.1 | async-start | bytes 524288 | tf_op jit(solution)/shard_map/all_to_all | solution.py:694
  56.2 23.1 %copy-start.1 = (bf16[256,512]{1,0:T(8,128)(2,1)S(1)}, bf16[256,512]{1,0:T(8,128)(2,1)}, u32[]{:S(2)}) copy-start(bf16[256,512]{1,0:T(8,128)(2,1)} %get-tuple-element.50.table_high) | copy-start | bytes 786436
  56.2 23.1 %copy-start.2 = (bf16[256,512]{1,0:T(8,128)(2,1)S(1)}, bf16[256,512]{1,0:T(8,128)(2,1)}, u32[]{:S(2)}) copy-start(bf16[256,512]{1,0:T(8,128)(2,1)} %get-tuple-element.51.table_low) | copy-start | bytes 786436
  81.2 10.1 %all-to-all-start.3 = ((f32[4,64,256]{2,1,0:T(8,128)}), f32[4,64,256]{2,1,0:T(8,128)S(1)}, u32[]{:S(2)}, u32[]{:S(2)}) async-start(f32[4,64,256]{2,1,0:T(8,128)} %forward.1), calls=%async_computation.3 | async-start | bytes 524288 | tf_op jit(solution)/shard_map/all_to_all | solution.py:698
  85.9 5.4 %copy-start = (f32[1,2,8,16,256]{4,3,2,1,0:T(8,128)S(1)}, f32[1,2,8,16,256]{4,3,2,1,0:T(8,128)}, u32[]{:S(2)}) copy-start(f32[1,2,8,16,256]{4,3,2,1,0:T(8,128)} %param.19) | copy-start | bytes 786436

commit v7 on v6

--- a/solution.py
+++ b/solution.py
@@ -85,8 +85,6 @@
             np.concatenate([np.cos(coarse_angle), -np.sin(coarse_angle)], 1),
         )
     )
-    angle = 2 * np.pi * (np.outer(g, k) % G) / G
-    out["comb"] = (np.cos(angle).astype(np.float32), np.sin(angle).astype(np.float32))
     return out
 
 
@@ -185,7 +183,7 @@
     )(modes.reshape(16, 16, 256), salinity)
 
 
-def pack_kernel(me, modes, sal, chunk, tail, low_face, high_face, modes_a, modes_b, west, east, faces, lines, sems, out_sems):
+def pack_kernel(me, modes, sal, chunk, low_face, high_face, modes_a, modes_b, west, east, faces, sems, out_sems):
     copies = fetch(
         (
             (modes.at[:, 0:128], modes_a),
@@ -201,14 +199,13 @@
         copy.wait()
     zero = jnp.zeros((8, 128), F32)
     for r in range(G):
-        lines[r, 0:16, :] = modes_a[pl.ds(r, 16, stride=16), :]
-        lines[r, 16:32, :] = modes_b[pl.ds(r, 16, stride=16), :]
-        tail[r] = zero
-    stores = [pltpu.make_async_copy(lines, chunk.at[:, 0:32, :], out_sems.at[0])]
-    stores[0].start()
+        chunk[r, 0:16, :] = modes_a[pl.ds(r, 16, stride=16), :]
+        chunk[r, 16:32, :] = modes_b[pl.ds(r, 16, stride=16), :]
+        chunk[r, 32:40, :] = zero
+    stores = []
     for i, face in enumerate((low_face, high_face)):
         copies[2 + i].wait()
-        stores.append(pltpu.make_async_copy(faces.at[i], face, out_sems.at[1 + i]))
+        stores.append(pltpu.make_async_copy(faces.at[i], face, out_sems.at[i]))
         stores[-1].start()
     row_id = iota((8, 128), 0)
 
@@ -222,8 +219,8 @@
 
     for copy in copies[4:]:
         copy.wait()
-    tail[(me[0] + 1) % G] = column(east, 127)
-    tail[(me[0] + G - 1) % G] = column(west, 0)
+    chunk[(me[0] + 1) % G, 32:40, :] = column(east, 127)
+    chunk[(me[0] + G - 1) % G, 32:40, :] = column(west, 0)
     for store in stores:
         store.wait()
 
@@ -231,48 +228,43 @@
 def pack(me, modes, salinity):
     return call(
         pack_kernel,
-        (hds(G, 40, 128), vds(G, 8, 128), hds(64, FINE), hds(64, FINE)),
+        (vds(G, 40, 128), hds(64, FINE), hds(64, FINE)),
         [SM, HB, HB],
-        [HB, VM, HB, HB],
+        [VM, HB, HB],
         scratch_shapes=[
             pltpu.VMEM((256, 128), F32),
             pltpu.VMEM((256, 128), F32),
             pltpu.VMEM((8, 64, 128), F32),
             pltpu.VMEM((8, 64, 128), F32),
             pltpu.VMEM((2, 64, FINE), F32),
-            pltpu.VMEM((G, 32, 128), F32),
             pltpu.SemaphoreType.DMA((6,)),
-            pltpu.SemaphoreType.DMA((3,)),
+            pltpu.SemaphoreType.DMA((2,)),
         ],
         name="pack",
     )(me, modes, salinity)
 
 
-def tails_kernel(chunk, tail, from_south, from_north, out, tiles, sem):
+def tails_kernel(chunk, from_south, from_north, out):
     row_id = iota((8, 128), 0)
     for r in range(G):
         rows = from_south if r < 8 else from_north
         p = r % 8
-        tile = tail[r]
+        tile = chunk[r, 32:40, :]
         parts = (rows[p : p + 1, :128], rows[p : p + 1, 128:], rows[8 + p : 9 + p, :128], rows[8 + p : 9 + p, 128:])
         for i, part in enumerate(parts):
             tile = jnp.where(row_id == i, jnp.broadcast_to(part, (8, 128)), tile)
-        tiles[r] = tile
-    store = pltpu.make_async_copy(tiles, out.at[:, 32:40, :], sem)
-    store.start()
-    store.wait()
-
-
-def tails(chunk, tail, from_south, from_north):
+        out[r, 32:40, :] = tile
+
+
+def tails(chunk, from_south, from_north):
     return call(
         tails_kernel,
-        hds(G, 40, 128),
-        [HB, VM, VM, VM],
-        HB,
+        vds(G, 40, 128),
+        [VM, VM, VM],
+        VM,
         input_output_aliases={0: 0},
-        scratch_shapes=[pltpu.VMEM((G, 8, 128), F32), pltpu.SemaphoreType.DMA],
         name="tails",
-    )(chunk, tail, from_south, from_north)
+    )(chunk, from_south, from_north)
 
 
 def cmul(a, b, c, s):
@@ -402,12 +394,9 @@
 EARLY = ("ym", "yt", "edge", "ref", "rm", "cm")
 
 
-def still_kernel(me, rate_hbm, sal_hbm, zlow_hbm, zhigh_hbm, edge_cols, from_south, from_north, *rest):
-    count = len(EARLY)
-    hbm, (base, parts_hbm), kept, rest = rest[:count], rest[count : count + 2], rest[count + 2 : 2 * count + 2], rest[2 * count + 2 :]
-    rate, salinity, zlow, zhigh, parts, sems, const_sems, out_sems = rest
-    copies = fetch(((rate_hbm, rate), (sal_hbm, salinity), (zlow_hbm, zlow), (zhigh_hbm, zhigh)), sems)
-    stores = fetch(tuple(zip(hbm, kept)), const_sems)
+def still_levels(
+    levels, runs, me, rate, salinity, zlow, zhigh, edge_cols, from_south, from_north, base, parts, parts_hbm, out_sems
+):
     west_t = edge_cols[(me[0] + G - 1) % G, 32:40, :].T
     east_t = edge_cols[(me[0] + 1) % G, 32:40, :].T
     last_row = iota((8, FINE), 0) == 7
@@ -419,11 +408,10 @@
         line = jnp.concatenate([rows[16 + 8 * j + l : 17 + 8 * j + l, :] for j in range(4)], 1)
         return jnp.broadcast_to(line, (8, FINE))
 
-    for copy in copies:
-        copy.wait()
+    stores = []
     for yb in range(8):
         ys = slice(8 * yb, 8 * yb + 8)
-        for l in range(8):
+        for l in levels:
             c = salinity[l, ys, :]
             upper = salinity[l + 1, ys, :] if l < 7 else zhigh[ys, :]
             lower = salinity[l - 1, ys, :] if l > 0 else zlow[ys, :]
@@ -447,32 +435,110 @@
             parts[0, l, ys, :] = (e - w) * 0.05
             parts[1, l, ys, :] = (north - south) * 0.05
             parts[2, l, ys, :] = (upper - lower) * 0.05
-        stores.append(pltpu.make_async_copy(parts.at[:, :, ys, :], parts_hbm.at[:, :, ys, :], out_sems.at[yb]))
-        stores[-1].start()
+        for at in runs:
+            stores.append(pltpu.make_async_copy(parts.at[:, at, ys, :], parts_hbm.at[:, at, ys, :], out_sems.at[len(stores)]))
+            stores[-1].start()
+    return stores
+
+
+def inner_kernel(me, rate_hbm, sal_hbm, edge_cols, from_south, from_north, inner_hbm, outer_hbm, *rest):
+    count = len(EARLY)
+    hbm, (base, parts_hbm, high_hbm, low_hbm), rest = rest[:count], rest[count : count + 4], rest[count + 4 :]
+    kept, rest = rest[:count], rest[count:]
+    rate, salinity, parts, high, low, inner, outer, sems, const_sems, out_sems, table_sems = rest
+    copies = fetch(
+        ((rate_hbm, rate), (sal_hbm, salinity), (inner_hbm, inner), (outer_hbm, outer)), sems
+    )
+    consts = fetch(tuple(zip(hbm, kept)), const_sems)
+    turns = (iota((16, 128), 0) * me[0]) % G
+    angle = turns.astype(F32) * (2.0 * math.pi / G)
+    cos = jnp.concatenate([jnp.cos(angle)] * 2, 1)
+    sin = -jnp.concatenate([jnp.sin(angle)] * 2, 1)
+    for copy in copies:
+        copy.wait()
+    stores = still_levels(
+        range(1, 7), (slice(1, 7),), me, rate, salinity, None, None, edge_cols, from_south, from_north, base, parts, parts_hbm, out_sems
+    )
+    real, imag = cmul(inner[:, :256], inner[:, 256:], cos, sin)
+    for t in range(G):
+        rows = slice(16 * t, 16 * t + 16)
+        value = cmul(real, imag, outer[t : t + 1, :256], outer[t : t + 1, 256:])
+        for at in range(2):
+            high[rows, 256 * at : 256 * at + 256], low[rows, 256 * at : 256 * at + 256] = halves(value[at])
+    for copy in stores + consts + fetch(((high, high_hbm), (low, low_hbm)), table_sems):
+        copy.wait()
+
+
+def inner_levels(me, rate, salinity, recv1, from_south, from_north):
+    consts = [jnp.asarray(tables()[name]) for name in EARLY]
+    out = call(
+        inner_kernel,
+        [vds(8, 64, FINE), hds(3, 8, 64, FINE)]
+        + [hds(256, 512, dtype=BF16)] * 2
+        + [vds(*x.shape, dtype=x.dtype) for x in consts],
+        [SM, HB, HB, VM, VM, VM, HB, HB] + [HB] * len(consts),
+        [VM, HB, HB, HB] + [VM] * len(consts),
+        scratch_shapes=[
+            pltpu.SMEM((8,), F32),
+            pltpu.VMEM((8, 64, FINE), F32),
+            pltpu.VMEM((3, 8, 64, FINE), F32),
+            pltpu.VMEM((256, 512), BF16),
+            pltpu.VMEM((256, 512), BF16),
+            pltpu.VMEM((G, 512), F32),
+            pltpu.VMEM((G, 512), F32),
+            pltpu.SemaphoreType.DMA((4,)),
+            pltpu.SemaphoreType.DMA((len(consts),)),
+            pltpu.SemaphoreType.DMA((8,)),
+            pltpu.SemaphoreType.DMA((2,)),
+        ],
+        limit=24,
+        name="inner_levels",
+    )(me, rate, salinity, recv1, from_south, from_north, *map(jnp.asarray, tables()["fwd"]), *consts)
+    return out[0], out[1], out[2:4], out[4:]
+
+
+def outer_kernel(
+    me, rate_hbm, sal_hbm, zlow_hbm, zhigh_hbm, edge_cols, from_south, from_north, base_in, parts_in, base, parts_hbm, *rest
+):
+    rate, salinity, zlow, zhigh, parts, sems, out_sems = rest
+    copies = fetch(
+        (
+            (rate_hbm, rate),
+            (sal_hbm.at[0:2], salinity.at[0:2]),
+            (sal_hbm.at[6:8], salinity.at[6:8]),
+            (zlow_hbm, zlow),
+            (zhigh_hbm, zhigh),
+        ),
+        sems,
+    )
+    for copy in copies:
+        copy.wait()
+    stores = still_levels(
+        (0, 7), (slice(0, 1), slice(7, 8)), me, rate, salinity, zlow, zhigh, edge_cols, from_south, from_north, base, parts, parts_hbm, out_sems
+    )
     for store in stores:
         store.wait()
 
 
-def still(me, rate, salinity, zlow, zhigh, recv1, from_south, from_north):
-    consts = [jnp.asarray(tables()[name]) for name in EARLY]
+def outer_levels(me, rate, salinity, zlow, zhigh, recv1, from_south, from_north, base, parts):
     return call(
-        still_kernel,
-        [vds(8, 64, FINE), hds(3, 8, 64, FINE)] + [vds(*x.shape, dtype=x.dtype) for x in consts],
-        [SM, HB, HB, HB, HB, VM, VM, VM] + [HB] * len(consts),
-        [VM, HB] + [VM] * len(consts),
+        outer_kernel,
+        [vds(8, 64, FINE), hds(3, 8, 64, FINE)],
+        [SM, HB, HB, HB, HB, VM, VM, VM, VM, HB],
+        [VM, HB],
+        input_output_aliases={8: 0, 9: 1},
         scratch_shapes=[
             pltpu.SMEM((8,), F32),
             pltpu.VMEM((8, 64, FINE), F32),
             pltpu.VMEM((64, FINE), F32),
             pltpu.VMEM((64, FINE), F32),
             pltpu.VMEM((3, 8, 64, FINE), F32),
-            pltpu.SemaphoreType.DMA((4,)),
-            pltpu.SemaphoreType.DMA((len(consts),)),
-            pltpu.SemaphoreType.DMA((8,)),
+            pltpu.SemaphoreType.DMA((5,)),
+            pltpu.SemaphoreType.DMA((16,)),
         ],
         limit=24,
-        name="still",
-    )(me, rate, salinity, zlow, zhigh, recv1, from_south, from_north, *consts)
+        name="outer_levels",
+    )(me, rate, salinity, zlow, zhigh, recv1, from_south, from_north, base, parts)
 
 
 def fine_kernel(
@@ -572,50 +638,11 @@
     )(grp, base, parts, recv2.reshape(512, 128), *consts)
 
 
-def stage_kernel(me, inner_hbm, outer_hbm, *rest):
-    count = (len(rest) - 8) // 2
-    hbm, dst, rest = rest[:count], rest[count : 2 * count], rest[2 * count :]
-    high_hbm, low_hbm, high, low, inner, outer, sems, out_sems = rest
-    copies = fetch(((inner_hbm, inner), (outer_hbm, outer)) + tuple(zip(hbm, dst)), sems)
-    turns = (iota((16, 128), 0) * me[0]) % G
+def forward_kernel(recv, table_high, table_low, out, left_high, left_low, mid):
+    turns = (iota((G, 128), 0) * iota((G, 128), 1)) % G
     angle = turns.astype(F32) * (2.0 * math.pi / G)
-    cos = jnp.concatenate([jnp.cos(angle)] * 2, 1)
-    sin = -jnp.concatenate([jnp.sin(angle)] * 2, 1)
-    copies[0].wait()
-    copies[1].wait()
-    real, imag = cmul(inner[:, :256], inner[:, 256:], cos, sin)
-    for t in range(G):
-        rows = slice(16 * t, 16 * t + 16)
-        value = cmul(real, imag, outer[t : t + 1, :256], outer[t : t + 1, 256:])
-        for at in range(2):
-            high[rows, 256 * at : 256 * at + 256], low[rows, 256 * at : 256 * at + 256] = halves(value[at])
-    for copy in copies[2:] + fetch(((high, high_hbm), (low, low_hbm)), out_sems):
-        copy.wait()
-
-
-def stage(me):
-    t = tables()
-    consts = [jnp.asarray(x) for x in (*t["tw"], *t["inv"])]
-    out = call(
-        stage_kernel,
-        [vds(*x.shape, dtype=x.dtype) for x in consts] + [hds(256, 512, dtype=BF16)] * 2,
-        [SM, HB, HB] + [HB] * len(consts),
-        [VM] * len(consts) + [HB] * 2,
-        scratch_shapes=[
-            pltpu.VMEM((256, 512), BF16),
-            pltpu.VMEM((256, 512), BF16),
-            pltpu.VMEM((G, 512), F32),
-            pltpu.VMEM((G, 512), F32),
-            pltpu.SemaphoreType.DMA((len(consts) + 2,)),
-            pltpu.SemaphoreType.DMA((2,)),
-        ],
-        name="stage",
-    )(me, *map(jnp.asarray, t["fwd"]), *consts)
-    return out[0:4], out[4:6]
-
-
-def forward_kernel(recv, table_high, table_low, cos_hbm, sin_hbm, out, left_high, left_low, mid, comb_cos, comb_sin, sems):
-    copies = fetch(((cos_hbm, comb_cos), (sin_hbm, comb_sin)), sems)
+    comb_cos = jnp.concatenate([jnp.cos(angle)] * 2, 1)
+    comb_sin = jnp.concatenate([jnp.sin(angle)] * 2, 1)
     for a in range(G):
         high, low = halves(recv[a])
         left_high[32 * a : 32 * a + 32, :] = high
@@ -623,8 +650,6 @@
     mid[...] = (
         mm(left_high[...], table_high[...]) + mm(left_low[...], table_high[...]) + mm(left_high[...], table_low[...])
     )
-    for copy in copies:
-        copy.wait()
     real = imag = jnp.zeros((32, 256), F32)
     for a in range(G):
         c, s = comb_cos[a : a + 1, :], comb_sin[a : a + 1, :]
@@ -640,18 +665,15 @@
     return call(
         forward_kernel,
         sds(4, 64, 256),
-        [VM, VM, VM, HB, HB],
+        [VM, VM, VM],
         VM,
         scratch_shapes=[
             pltpu.VMEM((512, 256), BF16),
             pltpu.VMEM((512, 256), BF16),
             pltpu.VMEM((512, 512), F32),
-            pltpu.VMEM((G, 256), F32),
-            pltpu.VMEM((G, 256), F32),
-            pltpu.SemaphoreType.DMA((2,)),
         ],
         name="forward",
-    )(recv, high, low, *map(jnp.asarray, tables()["comb"]))
+    )(recv, high, low)
 
 
 def finish_kernel(me, viscosity, gain, recv, modes, out):
@@ -683,16 +705,16 @@
     up, down = outer_lines(modes, salinity)
     from_south = shifted(up, "gy", 1)
     from_north = shifted(down, "gy", -1)
-    chunk, tail, low_face, high_face = pack(me, modes, salinity)
-    chunk = tails(chunk, tail, from_south, from_north)
+    chunk, low_face, high_face = pack(me, modes, salinity)
+    chunk = tails(chunk, from_south, from_north)
     recv1 = lax.all_to_all(chunk, GX, 0, 0, tiled=True)
-    inv, weights = stage(me)
+    send2 = inverse(recv1, *[jnp.asarray(x) for x in (*tables()["tw"], *tables()["inv"])])
+    send2, low_face, high_face, recv1 = lax.optimization_barrier((send2, low_face, high_face, recv1))
+    recv2 = lax.all_to_all(send2, GRP_GX, 0, 0, tiled=True)
     zlow = shifted(high_face, "grp", 1)
     zhigh = shifted(low_face, "grp", -1)
-    recv1, zlow, zhigh = lax.optimization_barrier((recv1, zlow, zhigh))
-    send2 = inverse(recv1, *inv)
-    recv2 = lax.all_to_all(send2, GRP_GX, 0, 0, tiled=True)
-    base, parts, *consts = still(me, diffusivity, salinity, zlow, zhigh, recv1, from_south, from_north)
+    base, parts, weights, consts = inner_levels(me, diffusivity, salinity, recv1, from_south, from_north)
+    base, parts = outer_levels(me, diffusivity, salinity, zlow, zhigh, recv1, from_south, from_north, base, parts)
     salinity_next, spread = fine(grp, base, parts, recv2, consts)
     recv3 = lax.all_to_all(spread, GX, 0, 0, tiled=True)
     recv4 = lax.all_to_all(forward(recv3, *weights), "grp", 0, 0, tiled=True)

time: 92.5 us -> 97.4 us (1.053)
  blocking collectives: 19.1 us -> 50 us
  waiting for transfers between devices: 20.2 us -> 7.71 us
  starting transfers between devices: 29.1 us -> 17 us
  Pallas kernels: 20.1 us -> 18.8 us
    all_to_all x0 -> x1, blocking collectives: none -> 24.4 us  [per_device(): recv1 = lax.all_to_all(chunk, GX, 0, 0, tiled=True)]
    all_to_all x1 -> x0, starting transfers between devices: 11.2 us -> none  [per_device(): recv1 = lax.all_to_all(chunk, GX, 0, 0, tiled=True)]
    all_to_all x1, waiting for transfers between devices: 7.74 us -> 0.01 us  [per_device(): recv2 = lax.all_to_all(send2, GRP_GX, 0, 0, tiled=True)]
    all_to_all x1, blocking collectives: 19.1 us -> 25.6 us  [per_device(): recv3 = lax.all_to_all(spread, GX, 0, 0, tiled=True)]
    all_to_all x1 -> x0, waiting for transfers between devices: 3.17 us -> none  [per_device(): recv1 = lax.all_to_all(chunk, GX, 0, 0, tiled=True)]
    ppermute x4, waiting for transfers between devices: 5.27 us -> 3.69 us  [shifted(): lax.ppermute(array, axis, [(i, (i + step) % count) for i in range(count)])]
    pallas_call x9, Pallas kernels: 20.1 us -> 18.8 us  [placed(): inner(*[x if spec is not HB else pltpu.with_memory_space_constraint(x, pl...]
  transfers between devices with their start and end apart: 7 -> 6, of which waited for: 4 -> 2; matrix products, arithmetic and copies ran while one was open for 1% -> 1% of each run, Pallas kernels for 11% -> 10%
where the time goes in v7:
time: 97.4 us; the launch traced here: 97 us
  blocking collectives  50 us (51%)
  Pallas kernels  18.8 us (19%)
  starting transfers between devices  17 us (17%)
  waiting for transfers between devices  7.71 us (8%)
  between operations  2.1 us (2%)
  local copies, waits for them, and re-layouts  1.36 us (1%)
    all_to_all x1, blocking collectives, per_device(): recv3 = lax.all_to_all(spread, GX, 0, 0, tiled=True)  25.6 us
    all_to_all x1, blocking collectives, per_device(): recv1 = lax.all_to_all(chunk, GX, 0, 0, tiled=True)  24.4 us
    pallas_call x9, Pallas kernels, placed(): inner(*[x if spec is not HB else pltpu.with_memory_space_constraint(x, pl...  18.8 us
    all_to_all x1, starting transfers between devices, per_device(): recv2 = lax.all_to_all(send2, GRP_GX, 0, 0, tiled=True)  8.51 us
    ppermute x4, starting transfers between devices, shifted(): lax.ppermute(array, axis, [(i, (i + step) % count) for i in range(count)])  5.13 us
    all_to_all x1, waiting for transfers between devices, per_device(): recv4 = lax.all_to_all(forward(recv3, *weights), 'grp', 0, 0, tiled=True)  4.01 us
    ppermute x4, waiting for transfers between devices, shifted(): lax.ppermute(array, axis, [(i, (i + step) % count) for i in range(count)])  3.69 us
    all_to_all x1, starting transfers between devices, per_device(): recv4 = lax.all_to_all(forward(recv3, *weights), 'grp', 0, 0, tiled=True)  3.41 us
  transfers between devices with their start and end apart: 6, of which 2 were waited for; matrix products, arithmetic and copies ran while one was open for 1% of the time, Pallas kernels for 10%

profile of v7, /device:TPU:32, one launch (start us, length us, event | category | flops | bytes accessed | tf_op | source)
XLA Modules:
  0.0 97.0 jit_solution(7785661366560211278)
XLA Ops:
  0.6 1.2 %outer_lines.1 = (f32[48,256]{1,0:T(8,128)S(1)}, f32[48,256]{1,0:T(8,128)S(1)}) custom-call(f32[16,16,256]{2,1,0:T(8,128)} %bitcast.7, f32[8,64,1024]{2,1,0:T(8,128)} %sal_hbm.3), custom_call_target="tpu_custom_call" | custom-call | tf_op jit(solution)/shard_map/outer_lines/pallas_call | solution.py:117
  1.9 0.0 copy-start.1
  1.9 0.0 copy-start.2
  1.9 0.0 copy-start.5
  1.9 0.0 copy-start.6
  1.9 0.1 collective-permute-start
  2.0 1.7 %collective-permute-start.1 = (f32[48,256]{1,0:T(8,128)S(1)}, f32[48,256]{1,0:T(8,128)S(1)}, u32[]{:S(2)}, u32[]{:S(2)}) collective-permute-start(f32[48,256]{1,0:T(8,128)S(1)} %get-tuple-element.27), channel_id=1, source_target_pairs={{0,3},{1,0},{2,1},{3,2},{4,7},{5,4},{6,5},{7,6},{8,11},{9,8},{10,9... | collective-permute-start | bytes 147464 | tf_op jit(solution)/shard_map/ppermute | solution.py:698
  3.7 1.9 %pack.1 = (f32[16,40,128]{2,1,0:T(8,128)S(1)}, f32[64,1024]{1,0:T(8,128)}, f32[64,1024]{1,0:T(8,128)}) custom-call(s32[1]{0:T(128)} %bitcast.1.me, f32[256,256]{1,0:T(8,128)} %bitcast.8, f32[8,64,1024]{2,1,0:T(8,128)} %sal_hbm.3), custom_call_target="tpu_custom_call" | custom-call | tf_op jit(solution)/shard_map/pack/pallas_call | solution.py:117
  5.7 24.4 %all_to_all.20.recv.edge_cols = f32[16,40,128]{2,1,0:T(8,128)S(1)} all-to-all(f32[16,40,128]{2,1,0:T(8,128)S(1)} %tails.1), channel_id=1, replica_groups=mesh['grp'=4,'gx_0'=2,'gx_1'=8,'gy'=4] {'gx_0','gx_1'}, dimensions={0} | all-to-all | bytes 655360 | tf_op jit(solution)/shard_map/all_to_all | solution.py:710
  30.2 1.6 %inverse.1 = f32[4,16,8,128]{3,2,1,0:T(8,128)} custom-call(f32[16,40,128]{2,1,0:T(8,128)S(1)} %all_to_all.20.recv.edge_cols, f32[16,8,128]{2,1,0:T(8,128)S(1)} %copy-done.5, f32[16,8,128]{2,1,0:T(8,128)S(1)} %copy-done.6, bf16[512,256]{1,0:T(8,128)(2,1)S(1)} %copy-done.1, bf16[512,256]{1,0:T(8,128)(2,1)S(1)} %copy-done.2), custom_call_target="tpu_custom_call" | custom-call | tf_op jit(solution)/shard_map/inverse/pallas_call | solution.py:117
  31.8 8.5 %all-to-all-start.1 = ((f32[64,8,128]{2,1,0:T(8,128)}), f32[64,8,128]{2,1,0:T(8,128)S(1)}, u32[]{:S(2)}, u32[]{:S(2)}) async-start(f32[64,8,128]{2,1,0:T(8,128)} %bitcast.11), calls=%async_computation.1 | async-start | bytes 524288 | tf_op jit(solution)/shard_map/all_to_all | solution.py:713
  40.3 1.5 %collective-permute-start.2 = (f32[64,1024]{1,0:T(8,128)}, f32[64,1024]{1,0:T(8,128)}, u32[]{:S(2)}, u32[]{:S(2)}) collective-permute-start(f32[64,1024]{1,0:T(8,128)} %get-tuple-element.30), channel_id=1, source_target_pairs={{0,64},{64,128},{128,192},{192,0},{1,65},{65,129},{129,193},{193,1... | collective-permute-start | bytes 786440 | tf_op jit(solution)/shard_map/ppermute | solution.py:698
  41.9 1.8 %collective-permute-start.3 = (f32[64,1024]{1,0:T(8,128)}, f32[64,1024]{1,0:T(8,128)}, u32[]{:S(2)}, u32[]{:S(2)}) collective-permute-start(f32[64,1024]{1,0:T(8,128)} %get-tuple-element.31), channel_id=1, source_target_pairs={{0,192},{64,0},{128,64},{192,128},{1,193},{65,1},{129,65},{193,129... | collective-permute-start | bytes 786440 | tf_op jit(solution)/shard_map/ppermute | solution.py:698
  43.6 4.9 %inner_levels.1 = (f32[8,64,1024]{2,1,0:T(8,128)S(1)}, f32[3,8,64,1024]{3,2,1,0:T(8,128)}, bf16[256,512]{1,0:T(8,128)(2,1)}, bf16[256,512]{1,0:T(8,128)(2,1)}, b...) custom-call(s32[1]{0:T(128)} %bitcast.1.me, ...), custom_call_target="tpu_custom_call" | custom-call | tf_op jit(solution)/shard_map/inner_levels/pallas_call | solution.py:117
  48.6 3.7 %collective-permute-done.2.zlow_hbm = f32[64,1024]{1,0:T(8,128)} collective-permute-done((f32[64,1024]{1,0:T(8,128)}, f32[64,1024]{1,0:T(8,128)}, u32[]{:S(2)}, u32[]{:S(2)}) %collective-permute-start.2) | collective-permute-done | bytes 262176 | tf_op jit(solution)/shard_map/ppermute | solution.py:698
  52.2 3.0 %outer_levels.1 = (f32[8,64,1024]{2,1,0:T(8,128)S(1)}, f32[3,8,64,1024]{3,2,1,0:T(8,128)}) custom-call(s32[1]{0:T(128)} %bitcast.1.me, f32[8]{0:T(128)} %rate_hbm.3, f32[8,64,1024]{2,1,0:T(8,128)} %sal_hbm.3, f32[64,1024]{1,0:T(8,128)} %collective-permute-done.2.zlow_hbm, ...), custom_call_target="tpu_custom_call", output_to_operand_aliasing={{0}: (8, {}), {1}: (9, {})} | custom-call | tf_op jit(solution)/shard_map/outer_levels/pallas_call | solution.py:117
  55.3 4.0 %fine.1 = (f32[8,64,1024]{2,1,0:T(8,128)S(1)}, f32[16,32,256]{2,1,0:T(8,128)S(1)}) custom-call(s32[1]{0:T(128)} %bitcast.grp_ref, f32[8,64,1024]{2,1,0:T(8,128)S(1)} %get-tuple-element.35.base, f32[3,8,64,1024]{3,2,1,0:T(8,128)} %get-tuple-element.36.parts_hbm, f32[512,128]{1,0:T(8,128)S(1)} %bitcast.10, ...), custom_call_target="tpu_custom_call", output_to_operand_aliasing={{0}: (1, {})} | custom-call | tf_op jit(solution)/shard_map/fine/pallas_call | solution.py:117
  59.3 25.6 %all_to_all.21.recv = f32[16,32,256]{2,1,0:T(8,128)S(1)} all-to-all(f32[16,32,256]{2,1,0:T(8,128)S(1)} %get-tuple-element.45), channel_id=1, replica_groups=mesh['grp'=4,'gx_0'=2,'gx_1'=8,'gy'=4] {'gx_0','gx_1'}, dimensions={0} | all-to-all | bytes 1048576 | tf_op jit(solution)/shard_map/all_to_all | solution.py:719
  84.9 1.3 %forward.1 = f32[4,64,256]{2,1,0:T(8,128)} custom-call(f32[16,32,256]{2,1,0:T(8,128)S(1)} %all_to_all.21.recv, bf16[256,512]{1,0:T(8,128)(2,1)S(1)} %copy-done.3, bf16[256,512]{1,0:T(8,128)(2,1)S(1)} %copy-done.4), custom_call_target="tpu_custom_call" | custom-call | tf_op jit(solution)/shard_map/forward/pallas_call | solution.py:117
  86.2 3.4 %all-to-all-start.3 = ((f32[4,64,256]{2,1,0:T(8,128)}), f32[4,64,256]{2,1,0:T(8,128)S(1)}, u32[]{:S(2)}, u32[]{:S(2)}) async-start(f32[4,64,256]{2,1,0:T(8,128)} %forward.1), calls=%async_computation.3 | async-start | bytes 524288 | tf_op jit(solution)/shard_map/all_to_all | solution.py:720
  90.9 0.0 copy-start
  90.9 1.3 %copy.27 = f32[8,64,1024]{2,1,0:T(8,128)} copy(f32[8,64,1024]{2,1,0:T(8,128)S(1)} %get-tuple-element.48) | data formatting | bytes 4194304
  92.2 4.0 %all-to-all-done.3.recv = f32[4,64,256]{2,1,0:T(8,128)S(1)} async-done(((f32[4,64,256]{2,1,0:T(8,128)}), f32[4,64,256]{2,1,0:T(8,128)S(1)}, u32[]{:S(2)}, u32[]{:S(2)}) %all-to-all-start.3) | async-done | bytes 262176 | tf_op jit(solution)/shard_map/all_to_all | solution.py:720
  96.2 0.7 finish.1
  (14 shorter events, 0.1 us)
Async XLA Ops:
  1.9 28.3 %copy-start.1 = (bf16[512,256]{1,0:T(8,128)(2,1)S(1)}, bf16[512,256]{1,0:T(8,128)(2,1)}, u32[]{:S(2)}) copy-start(bf16[512,256]{1,0:T(8,128)(2,1)} %constant.45.clone.inv_high) | copy-start | bytes 786436
  1.9 28.3 %copy-start.2 = (bf16[512,256]{1,0:T(8,128)(2,1)S(1)}, bf16[512,256]{1,0:T(8,128)(2,1)}, u32[]{:S(2)}) copy-start(bf16[512,256]{1,0:T(8,128)(2,1)} %constant.46.clone.inv_low) | copy-start | bytes 786436
  1.9 28.3 %copy-start.5 = (f32[16,8,128]{2,1,0:T(8,128)S(1)}, f32[16,8,128]{2,1,0:T(8,128)}, u32[]{:S(2)}) copy-start(f32[16,8,128]{2,1,0:T(8,128)} %constant.43.clone.twc) | copy-start | bytes 196612
  1.9 28.3 %copy-start.6 = (f32[16,8,128]{2,1,0:T(8,128)S(1)}, f32[16,8,128]{2,1,0:T(8,128)}, u32[]{:S(2)}) copy-start(f32[16,8,128]{2,1,0:T(8,128)} %constant.44.clone.tws) | copy-start | bytes 196612
  1.9 3.8 %collective-permute-start = (f32[48,256]{1,0:T(8,128)S(1)}, f32[48,256]{1,0:T(8,128)S(1)}, u32[]{:S(2)}, u32[]{:S(2)}) collective-permute-start(f32[48,256]{1,0:T(8,128)S(1)} %get-tuple-element.26), channel_id=1, source_target_pairs={{0,1},{1,2},{2,3},{3,0},{4,5},{5,6},{6,7},{7,4},{8,9},{9,10},{10,1... | collective-permute-start | bytes 147464 | tf_op jit(solution)/shard_map/ppermute | solution.py:698
  2.0 3.7 %collective-permute-start.1 = (f32[48,256]{1,0:T(8,128)S(1)}, f32[48,256]{1,0:T(8,128)S(1)}, u32[]{:S(2)}, u32[]{:S(2)}) collective-permute-start(f32[48,256]{1,0:T(8,128)S(1)} %get-tuple-element.27), channel_id=1, source_target_pairs={{0,3},{1,0},{2,1},{3,2},{4,7},{5,4},{6,5},{7,6},{8,11},{9,8},{10,9... | collective-permute-start | bytes 147464 | tf_op jit(solution)/shard_map/ppermute | solution.py:698
  31.8 23.5 %all-to-all-start.1 = ((f32[64,8,128]{2,1,0:T(8,128)}), f32[64,8,128]{2,1,0:T(8,128)S(1)}, u32[]{:S(2)}, u32[]{:S(2)}) async-start(f32[64,8,128]{2,1,0:T(8,128)} %bitcast.11), calls=%async_computation.1 | async-start | bytes 524288 | tf_op jit(solution)/shard_map/all_to_all | solution.py:713
  40.3 11.9 %collective-permute-start.2 = (f32[64,1024]{1,0:T(8,128)}, f32[64,1024]{1,0:T(8,128)}, u32[]{:S(2)}, u32[]{:S(2)}) collective-permute-start(f32[64,1024]{1,0:T(8,128)} %get-tuple-element.30), channel_id=1, source_target_pairs={{0,64},{64,128},{128,192},{192,0},{1,65},{65,129},{129,193},{193,1... | collective-permute-start | bytes 786440 | tf_op jit(solution)/shard_map/ppermute | solution.py:698
  41.9 10.4 %collective-permute-start.3 = (f32[64,1024]{1,0:T(8,128)}, f32[64,1024]{1,0:T(8,128)}, u32[]{:S(2)}, u32[]{:S(2)}) collective-permute-start(f32[64,1024]{1,0:T(8,128)} %get-tuple-element.31), channel_id=1, source_target_pairs={{0,192},{64,0},{128,64},{192,128},{1,193},{65,1},{129,65},{193,129... | collective-permute-start | bytes 786440 | tf_op jit(solution)/shard_map/ppermute | solution.py:698
  55.3 29.6 %copy-start.3 = (bf16[256,512]{1,0:T(8,128)(2,1)S(1)}, bf16[256,512]{1,0:T(8,128)(2,1)}, u32[]{:S(2)}) copy-start(bf16[256,512]{1,0:T(8,128)(2,1)} %get-tuple-element.46.table_high) | copy-start | bytes 786436
  55.3 29.6 %copy-start.4 = (bf16[256,512]{1,0:T(8,128)(2,1)S(1)}, bf16[256,512]{1,0:T(8,128)(2,1)}, u32[]{:S(2)}) copy-start(bf16[256,512]{1,0:T(8,128)(2,1)} %get-tuple-element.47.table_low) | copy-start | bytes 786436
  86.2 10.1 %all-to-all-start.3 = ((f32[4,64,256]{2,1,0:T(8,128)}), f32[4,64,256]{2,1,0:T(8,128)S(1)}, u32[]{:S(2)}, u32[]{:S(2)}) async-start(f32[4,64,256]{2,1,0:T(8,128)} %forward.1), calls=%async_computation.3 | async-start | bytes 524288 | tf_op jit(solution)/shard_map/all_to_all | solution.py:720
  90.9 5.4 %copy-start = (f32[1,2,8,16,256]{4,3,2,1,0:T(8,128)S(1)}, f32[1,2,8,16,256]{4,3,2,1,0:T(8,128)}, u32[]{:S(2)}) copy-start(f32[1,2,8,16,256]{4,3,2,1,0:T(8,128)} %param.17) | copy-start | bytes 786436

commit v8 on v6

--- a/solution.py
+++ b/solution.py
@@ -85,8 +85,6 @@
             np.concatenate([np.cos(coarse_angle), -np.sin(coarse_angle)], 1),
         )
     )
-    angle = 2 * np.pi * (np.outer(g, k) % G) / G
-    out["comb"] = (np.cos(angle).astype(np.float32), np.sin(angle).astype(np.float32))
     return out
 
 
@@ -614,8 +612,11 @@
     return out[0:4], out[4:6]
 
 
-def forward_kernel(recv, table_high, table_low, cos_hbm, sin_hbm, out, left_high, left_low, mid, comb_cos, comb_sin, sems):
-    copies = fetch(((cos_hbm, comb_cos), (sin_hbm, comb_sin)), sems)
+def forward_kernel(recv, table_high, table_low, out, left_high, left_low, mid):
+    turns = (iota((G, 128), 0) * iota((G, 128), 1)) % G
+    angle = turns.astype(F32) * (2.0 * math.pi / G)
+    comb_cos = jnp.concatenate([jnp.cos(angle)] * 2, 1)
+    comb_sin = jnp.concatenate([jnp.sin(angle)] * 2, 1)
     for a in range(G):
         high, low = halves(recv[a])
         left_high[32 * a : 32 * a + 32, :] = high
@@ -623,8 +624,6 @@
     mid[...] = (
         mm(left_high[...], table_high[...]) + mm(left_low[...], table_high[...]) + mm(left_high[...], table_low[...])
     )
-    for copy in copies:
-        copy.wait()
     real = imag = jnp.zeros((32, 256), F32)
     for a in range(G):
         c, s = comb_cos[a : a + 1, :], comb_sin[a : a + 1, :]
@@ -640,18 +639,15 @@
     return call(
         forward_kernel,
         sds(4, 64, 256),
-        [VM, VM, VM, HB, HB],
+        [VM, VM, VM],
         VM,
         scratch_shapes=[
             pltpu.VMEM((512, 256), BF16),
             pltpu.VMEM((512, 256), BF16),
             pltpu.VMEM((512, 512), F32),
-            pltpu.VMEM((G, 256), F32),
-            pltpu.VMEM((G, 256), F32),
-            pltpu.SemaphoreType.DMA((2,)),
         ],
         name="forward",
-    )(recv, high, low, *map(jnp.asarray, tables()["comb"]))
+    )(recv, high, low)
 
 
 def finish_kernel(me, viscosity, gain, recv, modes, out):

time: 92.5 us -> 91.9 us (level)
  no operation moved by 1% of the time
where the time goes in v8:
time: 91.9 us; the launch traced here: 91.4 us
  starting transfers between devices  29.1 us (32%)
  waiting for transfers between devices  20.2 us (22%)
  Pallas kernels  19.6 us (21%)
  blocking collectives  19.1 us (21%)
  between operations  2.06 us (2%)
  local copies, waits for them, and re-layouts  1.34 us (1%)
    pallas_call x9, Pallas kernels, placed(): inner(*[x if spec is not HB else pltpu.with_memory_space_constraint(x, pl...  19.6 us
    all_to_all x1, blocking collectives, per_device(): recv3 = lax.all_to_all(spread, GX, 0, 0, tiled=True)  19.1 us
    all_to_all x1, starting transfers between devices, per_device(): recv1 = lax.all_to_all(chunk, GX, 0, 0, tiled=True)  11.2 us
    all_to_all x1, starting transfers between devices, per_device(): recv2 = lax.all_to_all(send2, GRP_GX, 0, 0, tiled=True)  9.4 us
    all_to_all x1, waiting for transfers between devices, per_device(): recv2 = lax.all_to_all(send2, GRP_GX, 0, 0, tiled=True)  7.74 us
    ppermute x4, waiting for transfers between devices, shifted(): lax.ppermute(array, axis, [(i, (i + step) % count) for i in range(count)])  5.27 us
    ppermute x4, starting transfers between devices, shifted(): lax.ppermute(array, axis, [(i, (i + step) % count) for i in range(count)])  5.05 us
    all_to_all x1, waiting for transfers between devices, per_device(): recv4 = lax.all_to_all(forward(recv3, *weights), 'grp', 0, 0, tiled=True)  4.01 us
  transfers between devices with their start and end apart: 7, of which 4 were waited for; matrix products, arithmetic and copies ran while one was open for 1% of the time, Pallas kernels for 11%

profile of v8, /device:TPU:32, one launch (start us, length us, event | category | flops | bytes accessed | tf_op | source)
XLA Modules:
  0.0 91.4 jit_solution(1361868542880304424)
XLA Ops:
  0.6 1.2 %outer_lines.1 = (f32[48,256]{1,0:T(8,128)S(1)}, f32[48,256]{1,0:T(8,128)S(1)}) custom-call(f32[16,16,256]{2,1,0:T(8,128)} %bitcast.7, f32[8,64,1024]{2,1,0:T(8,128)} %sal_hbm.1), custom_call_target="tpu_custom_call" | custom-call | tf_op jit(solution)/shard_map/outer_lines/pallas_call | solution.py:117
  1.9 0.1 collective-permute-start
  2.0 1.7 %collective-permute-start.1 = (f32[48,256]{1,0:T(8,128)S(1)}, f32[48,256]{1,0:T(8,128)S(1)}, u32[]{:S(2)}, u32[]{:S(2)}) collective-permute-start(f32[48,256]{1,0:T(8,128)S(1)} %get-tuple-element.30), channel_id=1, source_target_pairs={{0,3},{1,0},{2,1},{3,2},{4,7},{5,4},{6,5},{7,6},{8,11},{9,8},{10,9... | collective-permute-start | bytes 147464 | tf_op jit(solution)/shard_map/ppermute | solution.py:672
  3.7 2.0 %pack.1 = (f32[16,40,128]{2,1,0:T(8,128)}, f32[16,8,128]{2,1,0:T(8,128)S(1)}, f32[64,1024]{1,0:T(8,128)}, f32[64,1024]{1,0:T(8,128)}) custom-call(s32[1]{0:T(128)} %bitcast.1.me, f32[256,256]{1,0:T(8,128)} %bitcast.8, f32[8,64,1024]{2,1,0:T(8,128)} %sal_hbm.1), custom_call_target="tpu_custom_call" | custom-call | tf_op jit(solution)/shard_map/pack/pallas_call | solution.py:117
  5.7 0.0 collective-permute-done.from_south
  5.7 0.7 tails.1
  6.4 11.2 %all-to-all-start = ((f32[16,40,128]{2,1,0:T(8,128)}), f32[16,40,128]{2,1,0:T(8,128)S(1)}, u32[]{:S(2)}, u32[]{:S(2)}) async-start(f32[16,40,128]{2,1,0:T(8,128)} %tails.1), calls=%async_computation | async-start | bytes 655360 | tf_op jit(solution)/shard_map/all_to_all | solution.py:684
  17.6 1.5 %collective-permute-start.2 = (f32[64,1024]{1,0:T(8,128)}, f32[64,1024]{1,0:T(8,128)S(1)}, u32[]{:S(2)}, u32[]{:S(2)}) collective-permute-start(f32[64,1024]{1,0:T(8,128)} %get-tuple-element.31), channel_id=1, source_target_pairs={{0,64},{64,128},{128,192},{192,0},{1,65},{65,129},{129,193},{193,1... | collective-permute-start | bytes 786440 | tf_op jit(solution)/shard_map/ppermute | solution.py:672
  19.1 1.7 %collective-permute-start.3 = (f32[64,1024]{1,0:T(8,128)}, f32[64,1024]{1,0:T(8,128)S(1)}, u32[]{:S(2)}, u32[]{:S(2)}) collective-permute-start(f32[64,1024]{1,0:T(8,128)} %get-tuple-element.32), channel_id=1, source_target_pairs={{0,192},{64,0},{128,64},{192,128},{1,193},{65,1},{129,65},{193,129... | collective-permute-start | bytes 786440 | tf_op jit(solution)/shard_map/ppermute | solution.py:672
  20.8 1.7 %stage.1 = (f32[16,8,128]{2,1,0:T(8,128)S(1)}, f32[16,8,128]{2,1,0:T(8,128)S(1)}, bf16[512,256]{1,0:T(8,128)(2,1)S(1)}, bf16[512,256]{1,0:T(8,128)(2,1)S(1)}, bf...) custom-call(s32[1]{0:T(128)} %bitcast.1.me, f32[16,512]{1,0:T(8,128)} %constant.47.clone.inner_hbm, ...), custom_call_target="tpu_custom_call" | custom-call | tf_op jit(solution)/shard_map/stage/pallas_call | solution.py:117
  22.6 5.3 %collective-permute-done.2.zlow_hbm = f32[64,1024]{1,0:T(8,128)S(1)} collective-permute-done((f32[64,1024]{1,0:T(8,128)}, f32[64,1024]{1,0:T(8,128)S(1)}, u32[]{:S(2)}, u32[]{:S(2)}) %collective-permute-start.2) | collective-permute-done | bytes 262176 | tf_op jit(solution)/shard_map/ppermute | solution.py:672
  27.8 3.2 %all-to-all-done.edge_cols.recv = f32[16,40,128]{2,1,0:T(8,128)S(1)} async-done(((f32[16,40,128]{2,1,0:T(8,128)}), f32[16,40,128]{2,1,0:T(8,128)S(1)}, u32[]{:S(2)}, u32[]{:S(2)}) %all-to-all-start) | async-done | bytes 327712 | tf_op jit(solution)/shard_map/all_to_all | solution.py:684
  31.0 1.6 %inverse.1 = f32[4,16,8,128]{3,2,1,0:T(8,128)} custom-call(f32[16,40,128]{2,1,0:T(8,128)S(1)} %all-to-all-done.edge_cols.recv, f32[16,8,128]{2,1,0:T(8,128)S(1)} %get-tuple-element.38.twc, f32[16,8,128]{2,1,0:T(8,128)S(1)} %get-tuple-element.39.tws, bf16[512,256]{1,0:T(8,128)(2,1)S(1)} %get-tuple-element.40.inv_high, ...), custom_call_target="tpu_custom_call" | custom-call | tf_op jit(solution)/shard_map/inverse/pallas_call | solution.py:117
  32.6 9.4 %all-to-all-start.1 = ((f32[64,8,128]{2,1,0:T(8,128)}), f32[64,8,128]{2,1,0:T(8,128)S(1)}, u32[]{:S(2)}, u32[]{:S(2)}) async-start(f32[64,8,128]{2,1,0:T(8,128)} %bitcast.11), calls=%async_computation.1 | async-start | bytes 524288 | tf_op jit(solution)/shard_map/all_to_all | solution.py:690
  42.1 6.4 %still.1 = (f32[8,64,1024]{2,1,0:T(8,128)S(1)}, f32[3,8,64,1024]{3,2,1,0:T(8,128)}, bf16[64,64]{1,0:T(8,128)(2,1)S(1)}, bf16[16,64]{1,0:T(8,128)(2,1)S(1)}, bf16...) custom-call(s32[1]{0:T(128)} %bitcast.1.me, ...), custom_call_target="tpu_custom_call" | custom-call | tf_op jit(solution)/shard_map/still/pallas_call | solution.py:117
  48.5 7.7 %all-to-all-done.1 = f32[64,8,128]{2,1,0:T(8,128)S(1)} async-done(((f32[64,8,128]{2,1,0:T(8,128)}), f32[64,8,128]{2,1,0:T(8,128)S(1)}, u32[]{:S(2)}, u32[]{:S(2)}) %all-to-all-start.1) | async-done | bytes 262176 | tf_op jit(solution)/shard_map/all_to_all | solution.py:690
  56.2 4.0 %fine.1 = (f32[8,64,1024]{2,1,0:T(8,128)S(1)}, f32[16,32,256]{2,1,0:T(8,128)S(1)}) custom-call(s32[1]{0:T(128)} %bitcast.grp_ref, f32[8,64,1024]{2,1,0:T(8,128)S(1)} %get-tuple-element.36.base, f32[3,8,64,1024]{3,2,1,0:T(8,128)} %get-tuple-element.37.parts_hbm, f32[512,128]{1,0:T(8,128)S(1)} %bitcast.10, ...), custom_call_target="tpu_custom_call", output_to_operand_aliasing={{0}: (1, {})} | custom-call | tf_op jit(solution)/shard_map/fine/pallas_call | solution.py:117
  60.2 19.1 %all_to_all.20.recv = f32[16,32,256]{2,1,0:T(8,128)S(1)} all-to-all(f32[16,32,256]{2,1,0:T(8,128)S(1)} %get-tuple-element.49), channel_id=1, replica_groups=mesh['grp'=4,'gx_0'=2,'gx_1'=8,'gy'=4] {'gx_0','gx_1'}, dimensions={0} | all-to-all | bytes 1048576 | tf_op jit(solution)/shard_map/all_to_all | solution.py:693
  79.3 1.3 %forward.1 = f32[4,64,256]{2,1,0:T(8,128)} custom-call(f32[16,32,256]{2,1,0:T(8,128)S(1)} %all_to_all.20.recv, bf16[256,512]{1,0:T(8,128)(2,1)S(1)} %copy-done.1, bf16[256,512]{1,0:T(8,128)(2,1)S(1)} %copy-done.2), custom_call_target="tpu_custom_call" | custom-call | tf_op jit(solution)/shard_map/forward/pallas_call | solution.py:117
  80.6 3.4 %all-to-all-start.3 = ((f32[4,64,256]{2,1,0:T(8,128)}), f32[4,64,256]{2,1,0:T(8,128)S(1)}, u32[]{:S(2)}, u32[]{:S(2)}) async-start(f32[4,64,256]{2,1,0:T(8,128)} %forward.1), calls=%async_computation.3 | async-start | bytes 524288 | tf_op jit(solution)/shard_map/all_to_all | solution.py:694
  85.3 0.0 copy-start
  85.3 1.3 %copy.23 = f32[8,64,1024]{2,1,0:T(8,128)} copy(f32[8,64,1024]{2,1,0:T(8,128)S(1)} %get-tuple-element.52) | data formatting | bytes 4194304
  86.6 4.0 %all-to-all-done.3.recv = f32[4,64,256]{2,1,0:T(8,128)S(1)} async-done(((f32[4,64,256]{2,1,0:T(8,128)}), f32[4,64,256]{2,1,0:T(8,128)S(1)}, u32[]{:S(2)}, u32[]{:S(2)}) %all-to-all-start.3) | async-done | bytes 262176 | tf_op jit(solution)/shard_map/all_to_all | solution.py:694
  90.7 0.7 finish.1
  (11 shorter events, 0.0 us)
Async XLA Ops:
  1.9 3.8 %collective-permute-start = (f32[48,256]{1,0:T(8,128)S(1)}, f32[48,256]{1,0:T(8,128)S(1)}, u32[]{:S(2)}, u32[]{:S(2)}) collective-permute-start(f32[48,256]{1,0:T(8,128)S(1)} %get-tuple-element.29), channel_id=1, source_target_pairs={{0,1},{1,2},{2,3},{3,0},{4,5},{5,6},{6,7},{7,4},{8,9},{9,10},{10,1... | collective-permute-start | bytes 147464 | tf_op jit(solution)/shard_map/ppermute | solution.py:672
  2.0 3.7 %collective-permute-start.1 = (f32[48,256]{1,0:T(8,128)S(1)}, f32[48,256]{1,0:T(8,128)S(1)}, u32[]{:S(2)}, u32[]{:S(2)}) collective-permute-start(f32[48,256]{1,0:T(8,128)S(1)} %get-tuple-element.30), channel_id=1, source_target_pairs={{0,3},{1,0},{2,1},{3,2},{4,7},{5,4},{6,5},{7,6},{8,11},{9,8},{10,9... | collective-permute-start | bytes 147464 | tf_op jit(solution)/shard_map/ppermute | solution.py:672
  6.4 24.6 %all-to-all-start = ((f32[16,40,128]{2,1,0:T(8,128)}), f32[16,40,128]{2,1,0:T(8,128)S(1)}, u32[]{:S(2)}, u32[]{:S(2)}) async-start(f32[16,40,128]{2,1,0:T(8,128)} %tails.1), calls=%async_computation | async-start | bytes 655360 | tf_op jit(solution)/shard_map/all_to_all | solution.py:684
  17.6 10.2 %collective-permute-start.2 = (f32[64,1024]{1,0:T(8,128)}, f32[64,1024]{1,0:T(8,128)S(1)}, u32[]{:S(2)}, u32[]{:S(2)}) collective-permute-start(f32[64,1024]{1,0:T(8,128)} %get-tuple-element.31), channel_id=1, source_target_pairs={{0,64},{64,128},{128,192},{192,0},{1,65},{65,129},{129,193},{193,1... | collective-permute-start | bytes 786440 | tf_op jit(solution)/shard_map/ppermute | solution.py:672
  19.1 8.7 %collective-permute-start.3 = (f32[64,1024]{1,0:T(8,128)}, f32[64,1024]{1,0:T(8,128)S(1)}, u32[]{:S(2)}, u32[]{:S(2)}) collective-permute-start(f32[64,1024]{1,0:T(8,128)} %get-tuple-element.32), channel_id=1, source_target_pairs={{0,192},{64,0},{128,64},{192,128},{1,193},{65,1},{129,65},{193,129... | collective-permute-start | bytes 786440 | tf_op jit(solution)/shard_map/ppermute | solution.py:672
  27.8 14.2 %copy-start.3 = (f32[64,1024]{1,0:T(8,128)}, f32[64,1024]{1,0:T(8,128)S(1)}, u32[]{:S(2)}) copy-start(f32[64,1024]{1,0:T(8,128)S(1)} %collective-permute-done.2.zlow_hbm) | copy-start | bytes 786436
  27.8 14.2 %copy-start.4 = (f32[64,1024]{1,0:T(8,128)}, f32[64,1024]{1,0:T(8,128)S(1)}, u32[]{:S(2)}) copy-start(f32[64,1024]{1,0:T(8,128)S(1)} %collective-permute-done.3.zhigh_hbm) | copy-start | bytes 786436
  32.6 23.6 %all-to-all-start.1 = ((f32[64,8,128]{2,1,0:T(8,128)}), f32[64,8,128]{2,1,0:T(8,128)S(1)}, u32[]{:S(2)}, u32[]{:S(2)}) async-start(f32[64,8,128]{2,1,0:T(8,128)} %bitcast.11), calls=%async_computation.1 | async-start | bytes 524288 | tf_op jit(solution)/shard_map/all_to_all | solution.py:690
  56.2 23.1 %copy-start.1 = (bf16[256,512]{1,0:T(8,128)(2,1)S(1)}, bf16[256,512]{1,0:T(8,128)(2,1)}, u32[]{:S(2)}) copy-start(bf16[256,512]{1,0:T(8,128)(2,1)} %get-tuple-element.50.table_high) | copy-start | bytes 786436
  56.2 23.1 %copy-start.2 = (bf16[256,512]{1,0:T(8,128)(2,1)S(1)}, bf16[256,512]{1,0:T(8,128)(2,1)}, u32[]{:S(2)}) copy-start(bf16[256,512]{1,0:T(8,128)(2,1)} %get-tuple-element.51.table_low) | copy-start | bytes 786436
  80.6 10.1 %all-to-all-start.3 = ((f32[4,64,256]{2,1,0:T(8,128)}), f32[4,64,256]{2,1,0:T(8,128)S(1)}, u32[]{:S(2)}, u32[]{:S(2)}) async-start(f32[4,64,256]{2,1,0:T(8,128)} %forward.1), calls=%async_computation.3 | async-start | bytes 524288 | tf_op jit(solution)/shard_map/all_to_all | solution.py:694
  85.3 5.4 %copy-start = (f32[1,2,8,16,256]{4,3,2,1,0:T(8,128)S(1)}, f32[1,2,8,16,256]{4,3,2,1,0:T(8,128)}, u32[]{:S(2)}) copy-start(f32[1,2,8,16,256]{4,3,2,1,0:T(8,128)} %param.17) | copy-start | bytes 786436

commit v9 on v8

--- a/solution.py
+++ b/solution.py
@@ -148,13 +148,15 @@
     return pltpu.roll(x, shift % x.shape[axis], axis)
 
 
-def lines_kernel(modes, sal, up, down, ends, south, north, sems):
+def lines_kernel(modes, sal, up, down, low_face, high_face, ends, south, north, sems):
     copies = fetch(
         (
             (modes.at[:, 0:8, :], ends.at[0]),
             (modes.at[:, 8:16, :], ends.at[1]),
             (sal.at[:, 0:8, :], south),
             (sal.at[:, 56:64, :], north),
+            (sal.at[0], low_face),
+            (sal.at[7], high_face),
         ),
         sems,
     )
@@ -170,26 +172,24 @@
 def outer_lines(modes, salinity):
     return call(
         lines_kernel,
-        (vds(48, 256), vds(48, 256)),
+        (vds(48, 256), vds(48, 256), vds(64, FINE), vds(64, FINE)),
         [HB, HB],
-        [VM, VM],
+        [VM] * 4,
         scratch_shapes=[
             pltpu.VMEM((2, 16, 8, 256), F32),
             pltpu.VMEM((8, 8, FINE), F32),
             pltpu.VMEM((8, 8, FINE), F32),
-            pltpu.SemaphoreType.DMA((4,)),
+            pltpu.SemaphoreType.DMA((6,)),
         ],
         name="outer_lines",
     )(modes.reshape(16, 16, 256), salinity)
 
 
-def pack_kernel(me, modes, sal, chunk, tail, low_face, high_face, modes_a, modes_b, west, east, faces, lines, sems, out_sems):
+def pack_kernel(me, modes, sal, chunk, modes_a, modes_b, west, east, sems):
     copies = fetch(
         (
             (modes.at[:, 0:128], modes_a),
             (modes.at[:, 128:256], modes_b),
-            (sal.at[0], faces.at[0]),
-            (sal.at[7], faces.at[1]),
             (sal.at[:, :, 0:128], west),
             (sal.at[:, :, FINE - 128 :], east),
         ),
@@ -199,15 +199,9 @@
         copy.wait()
     zero = jnp.zeros((8, 128), F32)
     for r in range(G):
-        lines[r, 0:16, :] = modes_a[pl.ds(r, 16, stride=16), :]
-        lines[r, 16:32, :] = modes_b[pl.ds(r, 16, stride=16), :]
-        tail[r] = zero
-    stores = [pltpu.make_async_copy(lines, chunk.at[:, 0:32, :], out_sems.at[0])]
-    stores[0].start()
-    for i, face in enumerate((low_face, high_face)):
-        copies[2 + i].wait()
-        stores.append(pltpu.make_async_copy(faces.at[i], face, out_sems.at[1 + i]))
-        stores[-1].start()
+        chunk[r, 0:16, :] = modes_a[pl.ds(r, 16, stride=16), :]
+        chunk[r, 16:32, :] = modes_b[pl.ds(r, 16, stride=16), :]
+        chunk[r, 32:40, :] = zero
     row_id = iota((8, 128), 0)
 
     def column(block, lane):
@@ -218,59 +212,50 @@
             tile = jnp.where(row_id == 4 + i, line, tile)
         return tile
 
-    for copy in copies[4:]:
+    for copy in copies[2:]:
         copy.wait()
-    tail[(me[0] + 1) % G] = column(east, 127)
-    tail[(me[0] + G - 1) % G] = column(west, 0)
-    for store in stores:
-        store.wait()
+    chunk[(me[0] + 1) % G, 32:40, :] = column(east, 127)
+    chunk[(me[0] + G - 1) % G, 32:40, :] = column(west, 0)
 
 
 def pack(me, modes, salinity):
     return call(
         pack_kernel,
-        (hds(G, 40, 128), vds(G, 8, 128), hds(64, FINE), hds(64, FINE)),
+        vds(G, 40, 128),
         [SM, HB, HB],
-        [HB, VM, HB, HB],
+        VM,
         scratch_shapes=[
             pltpu.VMEM((256, 128), F32),
             pltpu.VMEM((256, 128), F32),
             pltpu.VMEM((8, 64, 128), F32),
             pltpu.VMEM((8, 64, 128), F32),
-            pltpu.VMEM((2, 64, FINE), F32),
-            pltpu.VMEM((G, 32, 128), F32),
-            pltpu.SemaphoreType.DMA((6,)),
-            pltpu.SemaphoreType.DMA((3,)),
+            pltpu.SemaphoreType.DMA((4,)),
         ],
         name="pack",
     )(me, modes, salinity)
 
 
-def tails_kernel(chunk, tail, from_south, from_north, out, tiles, sem):
+def tails_kernel(chunk, from_south, from_north, out):
     row_id = iota((8, 128), 0)
     for r in range(G):
         rows = from_south if r < 8 else from_north
         p = r % 8
-        tile = tail[r]
+        tile = chunk[r, 32:40, :]
         parts = (rows[p : p + 1, :128], rows[p : p + 1, 128:], rows[8 + p : 9 + p, :128], rows[8 + p : 9 + p, 128:])
         for i, part in enumerate(parts):
             tile = jnp.where(row_id == i, jnp.broadcast_to(part, (8, 128)), tile)
-        tiles[r] = tile
-    store = pltpu.make_async_copy(tiles, out.at[:, 32:40, :], sem)
-    store.start()
-    store.wait()
-
-
-def tails(chunk, tail, from_south, from_north):
+        out[r, 32:40, :] = tile
+
+
+def tails(chunk, from_south, from_north):
     return call(
         tails_kernel,
-        hds(G, 40, 128),
-        [HB, VM, VM, VM],
-        HB,
+        vds(G, 40, 128),
+        [VM, VM, VM],
+        VM,
         input_output_aliases={0: 0},
-        scratch_shapes=[pltpu.VMEM((G, 8, 128), F32), pltpu.SemaphoreType.DMA],
         name="tails",
-    )(chunk, tail, from_south, from_north)
+    )(chunk, from_south, from_north)
 
 
 def cmul(a, b, c, s):
@@ -676,16 +661,17 @@
     me = lax.axis_index(GX).astype(jnp.int32).reshape(1)
     grp = lax.axis_index("grp").astype(jnp.int32).reshape(1)
     modes = coarse_modes.reshape(256, 256)
-    up, down = outer_lines(modes, salinity)
+    up, down, low_face, high_face = outer_lines(modes, salinity)
     from_south = shifted(up, "gy", 1)
     from_north = shifted(down, "gy", -1)
-    chunk, tail, low_face, high_face = pack(me, modes, salinity)
-    chunk = tails(chunk, tail, from_south, from_north)
-    recv1 = lax.all_to_all(chunk, GX, 0, 0, tiled=True)
-    inv, weights = stage(me)
     zlow = shifted(high_face, "grp", 1)
     zhigh = shifted(low_face, "grp", -1)
-    recv1, zlow, zhigh = lax.optimization_barrier((recv1, zlow, zhigh))
+    chunk, inv, weights = pack(me, modes, salinity), *stage(me)
+    chunk, from_south, from_north, zlow, zhigh, inv, weights = lax.optimization_barrier(
+        (chunk, from_south, from_north, zlow, zhigh, inv, weights)
+    )
+    chunk = tails(chunk, from_south, from_north)
+    recv1 = lax.all_to_all(chunk, GX, 0, 0, tiled=True)
     send2 = inverse(recv1, *inv)
     recv2 = lax.all_to_all(send2, GRP_GX, 0, 0, tiled=True)
     base, parts, *consts = still(me, diffusivity, salinity, zlow, zhigh, recv1, from_south, from_north)

time: 91.9 us -> 91.7 us (level)
  blocking collectives: 19.1 us -> 41.1 us
  starting transfers between devices: 29.1 us -> 16 us
  waiting for transfers between devices: 20.2 us -> 12.1 us
    all_to_all x0 -> x1, blocking collectives: none -> 23.1 us  [per_device(): recv1 = lax.all_to_all(chunk, GX, 0, 0, tiled=True)]
    all_to_all x1 -> x0, starting transfers between devices: 11.2 us -> none  [per_device(): recv1 = lax.all_to_all(chunk, GX, 0, 0, tiled=True)]
    ppermute x4, waiting for transfers between devices: 5.27 us -> 1.15 us  [shifted(): lax.ppermute(array, axis, [(i, (i + step) % count) for i in range(count)])]
    all_to_all x1 -> x0, waiting for transfers between devices: 3.17 us -> none  [per_device(): recv1 = lax.all_to_all(chunk, GX, 0, 0, tiled=True)]
    all_to_all x1, starting transfers between devices: 9.4 us -> 7.25 us  [per_device(): recv2 = lax.all_to_all(send2, GRP_GX, 0, 0, tiled=True)]
    all_to_all x1, blocking collectives: 19.1 us -> 18.1 us  [per_device(): recv3 = lax.all_to_all(spread, GX, 0, 0, tiled=True)]
  transfers between devices with their start and end apart: 7 -> 6, of which waited for: 4 -> 3; matrix products, arithmetic and copies ran while one was open for 1% -> 1% of each run, Pallas kernels for 11% -> 11%
where the time goes in v9:
time: 91.7 us; the launch traced here: 91.3 us
  blocking collectives  41.1 us (45%)
  Pallas kernels  18.7 us (20%)
  starting transfers between devices  16 us (17%)
  waiting for transfers between devices  12.1 us (13%)
  between operations  2.04 us (2%)
  local copies, waits for them, and re-layouts  1.34 us (1%)
    all_to_all x1, blocking collectives, per_device(): recv1 = lax.all_to_all(chunk, GX, 0, 0, tiled=True)  23.1 us
    pallas_call x9, Pallas kernels, placed(): inner(*[x if spec is not HB else pltpu.with_memory_space_constraint(x, pl...  18.7 us
    all_to_all x1, blocking collectives, per_device(): recv3 = lax.all_to_all(spread, GX, 0, 0, tiled=True)  18.1 us
    all_to_all x1, starting transfers between devices, per_device(): recv2 = lax.all_to_all(send2, GRP_GX, 0, 0, tiled=True)  7.25 us
    all_to_all x1, waiting for transfers between devices, per_device(): recv2 = lax.all_to_all(send2, GRP_GX, 0, 0, tiled=True)  6.94 us
    ppermute x4, starting transfers between devices, shifted(): lax.ppermute(array, axis, [(i, (i + step) % count) for i in range(count)])  5.06 us
    all_to_all x1, waiting for transfers between devices, per_device(): recv4 = lax.all_to_all(forward(recv3, *weights), 'grp', 0, 0, tiled=True)  4.05 us
    all_to_all x1, starting transfers between devices, per_device(): recv4 = lax.all_to_all(forward(recv3, *weights), 'grp', 0, 0, tiled=True)  3.64 us
  transfers between devices with their start and end apart: 6, of which 3 were waited for; matrix products, arithmetic and copies ran while one was open for 1% of the time, Pallas kernels for 11%

profile of v9, /device:TPU:32, one launch (start us, length us, event | category | flops | bytes accessed | tf_op | source)
XLA Modules:
  0.0 91.3 jit_solution(8171263894496611643)
XLA Ops:
  0.6 1.4 %outer_lines.1 = (f32[48,256]{1,0:T(8,128)S(1)}, f32[48,256]{1,0:T(8,128)S(1)}, f32[64,1024]{1,0:T(8,128)S(1)}, f32[64,1024]{1,0:T(8,128)S(1)}) custom-call(f32[16,16,256]{2,1,0:T(8,128)} %bitcast.7, f32[8,64,1024]{2,1,0:T(8,128)} %sal_hbm.1), custom_call_target="tpu_custom_call" | custom-call | tf_op jit(solution)/shard_map/outer_lines/pallas_call | solution.py:117
  2.0 1.6 %collective-permute-start.2 = (f32[64,1024]{1,0:T(8,128)S(1)}, f32[64,1024]{1,0:T(8,128)S(1)}, u32[]{:S(2)}, u32[]{:S(2)}) collective-permute-start(f32[64,1024]{1,0:T(8,128)S(1)} %get-tuple-element.35), channel_id=1, source_target_pairs={{0,64},{64,128},{128,192},{192,0},{1,65},{65,129},{129,193},{193,1... | collective-permute-start | bytes 786440 | tf_op jit(solution)/shard_map/ppermute | solution.py:657
  3.6 1.7 %collective-permute-start.3 = (f32[64,1024]{1,0:T(8,128)S(1)}, f32[64,1024]{1,0:T(8,128)S(1)}, u32[]{:S(2)}, u32[]{:S(2)}) collective-permute-start(f32[64,1024]{1,0:T(8,128)S(1)} %get-tuple-element.36), channel_id=1, source_target_pairs={{0,192},{64,0},{128,64},{192,128},{1,193},{65,1},{129,65},{193,129... | collective-permute-start | bytes 786440 | tf_op jit(solution)/shard_map/ppermute | solution.py:657
  5.4 0.0 collective-permute-start
  5.4 1.7 %collective-permute-start.1 = (f32[48,256]{1,0:T(8,128)S(1)}, f32[48,256]{1,0:T(8,128)S(1)}, u32[]{:S(2)}, u32[]{:S(2)}) collective-permute-start(f32[48,256]{1,0:T(8,128)S(1)} %get-tuple-element.34), channel_id=1, source_target_pairs={{0,3},{1,0},{2,1},{3,2},{4,7},{5,4},{6,5},{7,6},{8,11},{9,8},{10,9... | collective-permute-start | bytes 147464 | tf_op jit(solution)/shard_map/ppermute | solution.py:657
  7.1 1.4 %pack.1.chunk = f32[16,40,128]{2,1,0:T(8,128)S(1)} custom-call(s32[1]{0:T(128)} %bitcast.1.me, f32[256,256]{1,0:T(8,128)} %bitcast.8, f32[8,64,1024]{2,1,0:T(8,128)} %sal_hbm.1), custom_call_target="tpu_custom_call" | custom-call | tf_op jit(solution)/shard_map/pack/pallas_call | solution.py:117
  8.5 1.7 %stage.1 = (f32[16,8,128]{2,1,0:T(8,128)S(1)}, f32[16,8,128]{2,1,0:T(8,128)S(1)}, bf16[512,256]{1,0:T(8,128)(2,1)S(1)}, bf16[512,256]{1,0:T(8,128)(2,1)S(1)}, bf...) custom-call(s32[1]{0:T(128)} %bitcast.1.me, f32[16,512]{1,0:T(8,128)} %constant.47.clone.inner_hbm, ...), custom_call_target="tpu_custom_call" | custom-call | tf_op jit(solution)/shard_map/stage/pallas_call | solution.py:117
  10.2 0.0 collective-permute-done.from_south
  10.2 0.0 collective-permute-done.1.from_north
  10.2 1.1 %collective-permute-done.2.zlow_hbm = f32[64,1024]{1,0:T(8,128)S(1)} collective-permute-done((f32[64,1024]{1,0:T(8,128)S(1)}, f32[64,1024]{1,0:T(8,128)S(1)}, u32[]{:S(2)}, u32[]{:S(2)}) %collective-permute-start.2) | collective-permute-done | bytes 262176 | tf_op jit(solution)/shard_map/ppermute | solution.py:657
  11.4 0.0 collective-permute-done.3.zhigh_hbm
  11.4 23.1 %all_to_all.20.edge_cols.recv = f32[16,40,128]{2,1,0:T(8,128)S(1)} all-to-all(f32[16,40,128]{2,1,0:T(8,128)S(1)} %tails.1), channel_id=1, replica_groups=mesh['grp'=4,'gx_0'=2,'gx_1'=8,'gy'=4] {'gx_0','gx_1'}, dimensions={0} | all-to-all | bytes 655360 | tf_op jit(solution)/shard_map/all_to_all | solution.py:674
  34.5 1.6 %inverse.1 = f32[4,16,8,128]{3,2,1,0:T(8,128)} custom-call(f32[16,40,128]{2,1,0:T(8,128)S(1)} %all_to_all.20.edge_cols.recv, f32[16,8,128]{2,1,0:T(8,128)S(1)} %get-tuple-element.50.twc, f32[16,8,128]{2,1,0:T(8,128)S(1)} %get-tuple-element.51.tws, bf16[512,256]{1,0:T(8,128)(2,1)S(1)} %get-tuple-element.52.inv_high, ...), custom_call_target="tpu_custom_call" | custom-call | tf_op jit(solution)/shard_map/inverse/pallas_call | solution.py:117
  36.1 7.3 %all-to-all-start.1 = ((f32[64,8,128]{2,1,0:T(8,128)}), f32[64,8,128]{2,1,0:T(8,128)S(1)}, u32[]{:S(2)}, u32[]{:S(2)}) async-start(f32[64,8,128]{2,1,0:T(8,128)} %bitcast.11), calls=%async_computation.1 | async-start | bytes 524288 | tf_op jit(solution)/shard_map/all_to_all | solution.py:676
  43.4 6.5 %still.1 = (f32[8,64,1024]{2,1,0:T(8,128)S(1)}, f32[3,8,64,1024]{3,2,1,0:T(8,128)}, bf16[64,64]{1,0:T(8,128)(2,1)S(1)}, bf16[16,64]{1,0:T(8,128)(2,1)S(1)}, bf16...) custom-call(s32[1]{0:T(128)} %bitcast.1.me, ...), custom_call_target="tpu_custom_call" | custom-call | tf_op jit(solution)/shard_map/still/pallas_call | solution.py:117
  49.9 6.9 %all-to-all-done.1 = f32[64,8,128]{2,1,0:T(8,128)S(1)} async-done(((f32[64,8,128]{2,1,0:T(8,128)}), f32[64,8,128]{2,1,0:T(8,128)S(1)}, u32[]{:S(2)}, u32[]{:S(2)}) %all-to-all-start.1) | async-done | bytes 262176 | tf_op jit(solution)/shard_map/all_to_all | solution.py:676
  56.9 4.0 %fine.1 = (f32[8,64,1024]{2,1,0:T(8,128)S(1)}, f32[16,32,256]{2,1,0:T(8,128)S(1)}) custom-call(s32[1]{0:T(128)} %bitcast.grp_ref, f32[8,64,1024]{2,1,0:T(8,128)S(1)} %get-tuple-element.48.base, f32[3,8,64,1024]{3,2,1,0:T(8,128)} %get-tuple-element.49.parts_hbm, f32[512,128]{1,0:T(8,128)S(1)} %bitcast.10, ...), custom_call_target="tpu_custom_call", output_to_operand_aliasing={{0}: (1, {})} | custom-call | tf_op jit(solution)/shard_map/fine/pallas_call | solution.py:117
  60.8 18.1 %all_to_all.21.recv = f32[16,32,256]{2,1,0:T(8,128)S(1)} all-to-all(f32[16,32,256]{2,1,0:T(8,128)S(1)} %get-tuple-element.61), channel_id=1, replica_groups=mesh['grp'=4,'gx_0'=2,'gx_1'=8,'gy'=4] {'gx_0','gx_1'}, dimensions={0} | all-to-all | bytes 1048576 | tf_op jit(solution)/shard_map/all_to_all | solution.py:679
  78.9 1.3 %forward.1 = f32[4,64,256]{2,1,0:T(8,128)} custom-call(f32[16,32,256]{2,1,0:T(8,128)S(1)} %all_to_all.21.recv, bf16[256,512]{1,0:T(8,128)(2,1)S(1)} %copy-done.1, bf16[256,512]{1,0:T(8,128)(2,1)S(1)} %copy-done.2), custom_call_target="tpu_custom_call" | custom-call | tf_op jit(solution)/shard_map/forward/pallas_call | solution.py:117
  80.2 3.6 %all-to-all-start.3 = ((f32[4,64,256]{2,1,0:T(8,128)}), f32[4,64,256]{2,1,0:T(8,128)S(1)}, u32[]{:S(2)}, u32[]{:S(2)}) async-start(f32[4,64,256]{2,1,0:T(8,128)} %forward.1), calls=%async_computation.3 | async-start | bytes 524288 | tf_op jit(solution)/shard_map/all_to_all | solution.py:680
  85.1 0.0 copy-start
  85.2 1.3 %copy.23 = f32[8,64,1024]{2,1,0:T(8,128)} copy(f32[8,64,1024]{2,1,0:T(8,128)S(1)} %get-tuple-element.64) | data formatting | bytes 4194304
  86.5 4.0 %all-to-all-done.3.recv = f32[4,64,256]{2,1,0:T(8,128)S(1)} async-done(((f32[4,64,256]{2,1,0:T(8,128)}), f32[4,64,256]{2,1,0:T(8,128)S(1)}, u32[]{:S(2)}, u32[]{:S(2)}) %all-to-all-start.3) | async-done | bytes 262176 | tf_op jit(solution)/shard_map/all_to_all | solution.py:680
  90.5 0.7 finish.1
  (10 shorter events, 0.0 us)
Async XLA Ops:
  2.0 9.3 %collective-permute-start.2 = (f32[64,1024]{1,0:T(8,128)S(1)}, f32[64,1024]{1,0:T(8,128)S(1)}, u32[]{:S(2)}, u32[]{:S(2)}) collective-permute-start(f32[64,1024]{1,0:T(8,128)S(1)} %get-tuple-element.35), channel_id=1, source_target_pairs={{0,64},{64,128},{128,192},{192,0},{1,65},{65,129},{129,193},{193,1... | collective-permute-start | bytes 786440 | tf_op jit(solution)/shard_map/ppermute | solution.py:657
  3.6 7.8 %collective-permute-start.3 = (f32[64,1024]{1,0:T(8,128)S(1)}, f32[64,1024]{1,0:T(8,128)S(1)}, u32[]{:S(2)}, u32[]{:S(2)}) collective-permute-start(f32[64,1024]{1,0:T(8,128)S(1)} %get-tuple-element.36), channel_id=1, source_target_pairs={{0,192},{64,0},{128,64},{192,128},{1,193},{65,1},{129,65},{193,129... | collective-permute-start | bytes 786440 | tf_op jit(solution)/shard_map/ppermute | solution.py:657
  5.4 4.9 %collective-permute-start = (f32[48,256]{1,0:T(8,128)S(1)}, f32[48,256]{1,0:T(8,128)S(1)}, u32[]{:S(2)}, u32[]{:S(2)}) collective-permute-start(f32[48,256]{1,0:T(8,128)S(1)} %get-tuple-element.33), channel_id=1, source_target_pairs={{0,1},{1,2},{2,3},{3,0},{4,5},{5,6},{6,7},{7,4},{8,9},{9,10},{10,1... | collective-permute-start | bytes 147464 | tf_op jit(solution)/shard_map/ppermute | solution.py:657
  5.4 4.9 %collective-permute-start.1 = (f32[48,256]{1,0:T(8,128)S(1)}, f32[48,256]{1,0:T(8,128)S(1)}, u32[]{:S(2)}, u32[]{:S(2)}) collective-permute-start(f32[48,256]{1,0:T(8,128)S(1)} %get-tuple-element.34), channel_id=1, source_target_pairs={{0,3},{1,0},{2,1},{3,2},{4,7},{5,4},{6,5},{7,6},{8,11},{9,8},{10,9... | collective-permute-start | bytes 147464 | tf_op jit(solution)/shard_map/ppermute | solution.py:657
  11.4 32.0 %copy-start.3 = (f32[64,1024]{1,0:T(8,128)}, f32[64,1024]{1,0:T(8,128)S(1)}, u32[]{:S(2)}) copy-start(f32[64,1024]{1,0:T(8,128)S(1)} %collective-permute-done.2.zlow_hbm) | copy-start | bytes 786436
  11.4 32.0 %copy-start.4 = (f32[64,1024]{1,0:T(8,128)}, f32[64,1024]{1,0:T(8,128)S(1)}, u32[]{:S(2)}) copy-start(f32[64,1024]{1,0:T(8,128)S(1)} %collective-permute-done.3.zhigh_hbm) | copy-start | bytes 786436
  36.1 20.7 %all-to-all-start.1 = ((f32[64,8,128]{2,1,0:T(8,128)}), f32[64,8,128]{2,1,0:T(8,128)S(1)}, u32[]{:S(2)}, u32[]{:S(2)}) async-start(f32[64,8,128]{2,1,0:T(8,128)} %bitcast.11), calls=%async_computation.1 | async-start | bytes 524288 | tf_op jit(solution)/shard_map/all_to_all | solution.py:676
  56.9 22.0 %copy-start.1 = (bf16[256,512]{1,0:T(8,128)(2,1)S(1)}, bf16[256,512]{1,0:T(8,128)(2,1)}, u32[]{:S(2)}) copy-start(bf16[256,512]{1,0:T(8,128)(2,1)} %get-tuple-element.62.table_high) | copy-start | bytes 786436
  56.9 22.0 %copy-start.2 = (bf16[256,512]{1,0:T(8,128)(2,1)S(1)}, bf16[256,512]{1,0:T(8,128)(2,1)}, u32[]{:S(2)}) copy-start(bf16[256,512]{1,0:T(8,128)(2,1)} %get-tuple-element.63.table_low) | copy-start | bytes 786436
  80.2 10.3 %all-to-all-start.3 = ((f32[4,64,256]{2,1,0:T(8,128)}), f32[4,64,256]{2,1,0:T(8,128)S(1)}, u32[]{:S(2)}, u32[]{:S(2)}) async-start(f32[4,64,256]{2,1,0:T(8,128)} %forward.1), calls=%async_computation.3 | async-start | bytes 524288 | tf_op jit(solution)/shard_map/all_to_all | solution.py:680
  85.1 5.4 %copy-start = (f32[1,2,8,16,256]{4,3,2,1,0:T(8,128)S(1)}, f32[1,2,8,16,256]{4,3,2,1,0:T(8,128)}, u32[]{:S(2)}) copy-start(f32[1,2,8,16,256]{4,3,2,1,0:T(8,128)} %param.17) | copy-start | bytes 786436

commit v10 on v9

--- a/solution.py
+++ b/solution.py
@@ -160,13 +160,15 @@
         ),
         sems,
     )
-    for copy in copies:
+    for copy in copies[:4]:
         copy.wait()
     for dst, rows, end, row in ((up, north, 1, 7), (down, south, 0, 0)):
         dst[0:16, :] = ends[end, :, row, :]
         face = rows[:, row, :]
         for j in range(4):
             dst[16 + 8 * j : 24 + 8 * j, :] = face[:, 256 * j : 256 * j + 256]
+    for copy in copies[4:]:
+        copy.wait()
 
 
 def outer_lines(modes, salinity):
@@ -386,11 +388,27 @@
 
 
 def still_kernel(me, rate_hbm, sal_hbm, zlow_hbm, zhigh_hbm, edge_cols, from_south, from_north, *rest):
+    (inner_hbm, outer_hbm), rest = rest[:2], rest[2:]
     count = len(EARLY)
-    hbm, (base, parts_hbm), kept, rest = rest[:count], rest[count : count + 2], rest[count + 2 : 2 * count + 2], rest[2 * count + 2 :]
+    hbm, (base, parts_hbm, high_hbm, low_hbm), rest = rest[:count], rest[count : count + 4], rest[count + 4 :]
+    kept, (high, low, inner, outer, table_sems), rest = rest[:count], rest[count : count + 5], rest[count + 5 :]
     rate, salinity, zlow, zhigh, parts, sems, const_sems, out_sems = rest
     copies = fetch(((rate_hbm, rate), (sal_hbm, salinity), (zlow_hbm, zlow), (zhigh_hbm, zhigh)), sems)
     stores = fetch(tuple(zip(hbm, kept)), const_sems)
+    bases = fetch(((inner_hbm, inner), (outer_hbm, outer)), table_sems)
+    turns = (iota((16, 128), 0) * me[0]) % G
+    angle = turns.astype(F32) * (2.0 * math.pi / G)
+    cos = jnp.concatenate([jnp.cos(angle)] * 2, 1)
+    sin = -jnp.concatenate([jnp.sin(angle)] * 2, 1)
+    for copy in bases:
+        copy.wait()
+    real, imag = cmul(inner[:, :256], inner[:, 256:], cos, sin)
+    for t in range(G):
+        rows = slice(16 * t, 16 * t + 16)
+        value = cmul(real, imag, outer[t : t + 1, :256], outer[t : t + 1, 256:])
+        for at in range(2):
+            high[rows, 256 * at : 256 * at + 256], low[rows, 256 * at : 256 * at + 256] = halves(value[at])
+    stores += fetch(((high, high_hbm), (low, low_hbm)), table_sems, 2)
     west_t = edge_cols[(me[0] + G - 1) % G, 32:40, :].T
     east_t = edge_cols[(me[0] + 1) % G, 32:40, :].T
     last_row = iota((8, FINE), 0) == 7
@@ -440,10 +458,17 @@
     consts = [jnp.asarray(tables()[name]) for name in EARLY]
     return call(
         still_kernel,
-        [vds(8, 64, FINE), hds(3, 8, 64, FINE)] + [vds(*x.shape, dtype=x.dtype) for x in consts],
-        [SM, HB, HB, HB, HB, VM, VM, VM] + [HB] * len(consts),
-        [VM, HB] + [VM] * len(consts),
+        [vds(8, 64, FINE), hds(3, 8, 64, FINE)]
+        + [hds(256, 512, dtype=BF16)] * 2
+        + [vds(*x.shape, dtype=x.dtype) for x in consts],
+        [SM, HB, HB, HB, HB, VM, VM, VM] + [HB] * (2 + len(consts)),
+        [VM, HB, HB, HB] + [VM] * len(consts),
         scratch_shapes=[
+            pltpu.VMEM((256, 512), BF16),
+            pltpu.VMEM((256, 512), BF16),
+            pltpu.VMEM((G, 512), F32),
+            pltpu.VMEM((G, 512), F32),
+            pltpu.SemaphoreType.DMA((4,)),
             pltpu.SMEM((8,), F32),
             pltpu.VMEM((8, 64, FINE), F32),
             pltpu.VMEM((64, FINE), F32),
@@ -455,7 +480,7 @@
         ],
         limit=24,
         name="still",
-    )(me, rate, salinity, zlow, zhigh, recv1, from_south, from_north, *consts)
+    )(me, rate, salinity, zlow, zhigh, recv1, from_south, from_north, *map(jnp.asarray, tables()["fwd"]), *consts)
 
 
 def fine_kernel(
@@ -555,46 +580,24 @@
     )(grp, base, parts, recv2.reshape(512, 128), *consts)
 
 
-def stage_kernel(me, inner_hbm, outer_hbm, *rest):
-    count = (len(rest) - 8) // 2
-    hbm, dst, rest = rest[:count], rest[count : 2 * count], rest[2 * count :]
-    high_hbm, low_hbm, high, low, inner, outer, sems, out_sems = rest
-    copies = fetch(((inner_hbm, inner), (outer_hbm, outer)) + tuple(zip(hbm, dst)), sems)
-    turns = (iota((16, 128), 0) * me[0]) % G
-    angle = turns.astype(F32) * (2.0 * math.pi / G)
-    cos = jnp.concatenate([jnp.cos(angle)] * 2, 1)
-    sin = -jnp.concatenate([jnp.sin(angle)] * 2, 1)
-    copies[0].wait()
-    copies[1].wait()
-    real, imag = cmul(inner[:, :256], inner[:, 256:], cos, sin)
-    for t in range(G):
-        rows = slice(16 * t, 16 * t + 16)
-        value = cmul(real, imag, outer[t : t + 1, :256], outer[t : t + 1, 256:])
-        for at in range(2):
-            high[rows, 256 * at : 256 * at + 256], low[rows, 256 * at : 256 * at + 256] = halves(value[at])
-    for copy in copies[2:] + fetch(((high, high_hbm), (low, low_hbm)), out_sems):
+def stage_kernel(*refs):
+    sems = refs[-1]
+    count = len(refs) // 2
+    for copy in fetch(tuple(zip(refs[:count], refs[count:-1])), sems):
         copy.wait()
 
 
-def stage(me):
+def stage():
     t = tables()
     consts = [jnp.asarray(x) for x in (*t["tw"], *t["inv"])]
-    out = call(
+    return call(
         stage_kernel,
-        [vds(*x.shape, dtype=x.dtype) for x in consts] + [hds(256, 512, dtype=BF16)] * 2,
-        [SM, HB, HB] + [HB] * len(consts),
-        [VM] * len(consts) + [HB] * 2,
-        scratch_shapes=[
-            pltpu.VMEM((256, 512), BF16),
-            pltpu.VMEM((256, 512), BF16),
-            pltpu.VMEM((G, 512), F32),
-            pltpu.VMEM((G, 512), F32),
-            pltpu.SemaphoreType.DMA((len(consts) + 2,)),
-            pltpu.SemaphoreType.DMA((2,)),
-        ],
+        [vds(*x.shape, dtype=x.dtype) for x in consts],
+        [HB] * len(consts),
+        [VM] * len(consts),
+        scratch_shapes=[pltpu.SemaphoreType.DMA((len(consts),))],
         name="stage",
-    )(me, *map(jnp.asarray, t["fwd"]), *consts)
-    return out[0:4], out[4:6]
+    )(*consts)
 
 
 def forward_kernel(recv, table_high, table_low, out, left_high, left_low, mid):
@@ -635,21 +638,31 @@
     )(recv, high, low)
 
 
-def finish_kernel(me, viscosity, gain, recv, modes, out):
+def finish_kernel(me, viscosity, gain, recv, modes, out_hbm, out, sems):
     index = me[0] * W + iota((8, W), 1)
     number = jnp.where(index < NV // 2, index, index - NV).astype(F32)
     wave = (2.0 * math.pi / NV) * number
     damping = jnp.exp(-viscosity[0] * wave * wave)[0:1, :]
+    stores = []
     for c in range(2):
         for g in range(4):
             at = slice(128 * c + 32 * g, 128 * c + 32 * g + 32)
             out[at, :] = damping * modes[at, :] + gain[0] * recv[g, 32 * c : 32 * c + 32, :]
+        half = slice(128 * c, 128 * c + 128)
+        stores += fetch(((out.at[half], out_hbm.at[half]),), sems, c)
+    for store in stores:
+        store.wait()
 
 
 def finish(me, viscosity, gain, recv, modes):
-    return call(finish_kernel, sds(256, W), [SM, SM, SM, VM, VM], VM, name="finish")(
-        me, viscosity, gain, recv, modes
-    )
+    return call(
+        finish_kernel,
+        hds(256, W),
+        [SM, SM, SM, VM, VM],
+        HB,
+        scratch_shapes=[pltpu.VMEM((256, W), F32), pltpu.SemaphoreType.DMA((2,))],
+        name="finish",
+    )(me, viscosity, gain, recv, modes)
 
 
 def shifted(array, axis, step):
@@ -666,15 +679,16 @@
     from_north = shifted(down, "gy", -1)
     zlow = shifted(high_face, "grp", 1)
     zhigh = shifted(low_face, "grp", -1)
-    chunk, inv, weights = pack(me, modes, salinity), *stage(me)
-    chunk, from_south, from_north, zlow, zhigh, inv, weights = lax.optimization_barrier(
-        (chunk, from_south, from_north, zlow, zhigh, inv, weights)
+    chunk, inv = pack(me, modes, salinity), stage()
+    chunk, from_south, from_north, zlow, zhigh, inv = lax.optimization_barrier(
+        (chunk, from_south, from_north, zlow, zhigh, inv)
     )
     chunk = tails(chunk, from_south, from_north)
     recv1 = lax.all_to_all(chunk, GX, 0, 0, tiled=True)
     send2 = inverse(recv1, *inv)
     recv2 = lax.all_to_all(send2, GRP_GX, 0, 0, tiled=True)
-    base, parts, *consts = still(me, diffusivity, salinity, zlow, zhigh, recv1, from_south, from_north)
+    base, parts, *rest = still(me, diffusivity, salinity, zlow, zhigh, recv1, from_south, from_north)
+    weights, consts = rest[:2], rest[2:]
     salinity_next, spread = fine(grp, base, parts, recv2, consts)
     recv3 = lax.all_to_all(spread, GX, 0, 0, tiled=True)
     recv4 = lax.all_to_all(forward(recv3, *weights), "grp", 0, 0, tiled=True)

time: 91.7 us -> 91.9 us (level)
  transfers between devices with their start and end apart: 6 -> 6, of which waited for: 3 -> 3; matrix products, arithmetic and copies ran while one was open for 1% -> 1% of each run, Pallas kernels for 11% -> 10%
where the time goes in v10:
time: 91.9 us; the launch traced here: 91.5 us
  blocking collectives  41.1 us (45%)
  Pallas kernels  18.3 us (20%)
  starting transfers between devices  16.2 us (18%)
  waiting for transfers between devices  12.5 us (14%)
  between operations  2.04 us (2%)
  local copies, waits for them, and re-layouts  1.34 us (1%)
    all_to_all x1, blocking collectives, per_device(): recv1 = lax.all_to_all(chunk, GX, 0, 0, tiled=True)  23.1 us
    pallas_call x9, Pallas kernels, placed(): inner(*[x if spec is not HB else pltpu.with_memory_space_constraint(x, pl...  18.3 us
    all_to_all x1, blocking collectives, per_device(): recv3 = lax.all_to_all(spread, GX, 0, 0, tiled=True)  18.1 us
    all_to_all x1, starting transfers between devices, per_device(): recv2 = lax.all_to_all(send2, GRP_GX, 0, 0, tiled=True)  7.25 us
    all_to_all x1, waiting for transfers between devices, per_device(): recv2 = lax.all_to_all(send2, GRP_GX, 0, 0, tiled=True)  6.72 us
    ppermute x4, starting transfers between devices, shifted(): lax.ppermute(array, axis, [(i, (i + step) % count) for i in range(count)])  5.06 us
    all_to_all x1, waiting for transfers between devices, per_device(): recv4 = lax.all_to_all(forward(recv3, *weights), 'grp', 0, 0, tiled=True)  4.05 us
    all_to_all x1, starting transfers between devices, per_device(): recv4 = lax.all_to_all(forward(recv3, *weights), 'grp', 0, 0, tiled=True)  3.86 us
  transfers between devices with their start and end apart: 6, of which 3 were waited for; matrix products, arithmetic and copies ran while one was open for 1% of the time, Pallas kernels for 10%

profile of v10, /device:TPU:32, one launch (start us, length us, event | category | flops | bytes accessed | tf_op | source)
XLA Modules:
  0.0 91.5 jit_solution(11049809294199255380)
XLA Ops:
  0.6 1.4 %outer_lines.1 = (f32[48,256]{1,0:T(8,128)S(1)}, f32[48,256]{1,0:T(8,128)S(1)}, f32[64,1024]{1,0:T(8,128)S(1)}, f32[64,1024]{1,0:T(8,128)S(1)}) custom-call(f32[16,16,256]{2,1,0:T(8,128)} %bitcast.7, f32[8,64,1024]{2,1,0:T(8,128)} %sal_hbm.1), custom_call_target="tpu_custom_call" | custom-call | tf_op jit(solution)/shard_map/outer_lines/pallas_call | solution.py:117
  2.0 1.6 %collective-permute-start.2 = (f32[64,1024]{1,0:T(8,128)S(1)}, f32[64,1024]{1,0:T(8,128)S(1)}, u32[]{:S(2)}, u32[]{:S(2)}) collective-permute-start(f32[64,1024]{1,0:T(8,128)S(1)} %get-tuple-element.33), channel_id=1, source_target_pairs={{0,64},{64,128},{128,192},{192,0},{1,65},{65,129},{129,193},{193,1... | collective-permute-start | bytes 786440 | tf_op jit(solution)/shard_map/ppermute | solution.py:670
  3.6 1.7 %collective-permute-start.3 = (f32[64,1024]{1,0:T(8,128)S(1)}, f32[64,1024]{1,0:T(8,128)S(1)}, u32[]{:S(2)}, u32[]{:S(2)}) collective-permute-start(f32[64,1024]{1,0:T(8,128)S(1)} %get-tuple-element.34), channel_id=1, source_target_pairs={{0,192},{64,0},{128,64},{192,128},{1,193},{65,1},{129,65},{193,129... | collective-permute-start | bytes 786440 | tf_op jit(solution)/shard_map/ppermute | solution.py:670
  5.3 0.0 collective-permute-start
  5.3 1.7 %collective-permute-start.1 = (f32[48,256]{1,0:T(8,128)S(1)}, f32[48,256]{1,0:T(8,128)S(1)}, u32[]{:S(2)}, u32[]{:S(2)}) collective-permute-start(f32[48,256]{1,0:T(8,128)S(1)} %get-tuple-element.32), channel_id=1, source_target_pairs={{0,3},{1,0},{2,1},{3,2},{4,7},{5,4},{6,5},{7,6},{8,11},{9,8},{10,9... | collective-permute-start | bytes 147464 | tf_op jit(solution)/shard_map/ppermute | solution.py:670
  7.1 1.4 %pack.1.chunk = f32[16,40,128]{2,1,0:T(8,128)S(1)} custom-call(s32[1]{0:T(128)} %bitcast.1.me, f32[256,256]{1,0:T(8,128)} %bitcast.8, f32[8,64,1024]{2,1,0:T(8,128)} %sal_hbm.1), custom_call_target="tpu_custom_call" | custom-call | tf_op jit(solution)/shard_map/pack/pallas_call | solution.py:117
  8.5 1.1 %stage.1 = (f32[16,8,128]{2,1,0:T(8,128)S(1)}, f32[16,8,128]{2,1,0:T(8,128)S(1)}, bf16[512,256]{1,0:T(8,128)(2,1)S(1)}, bf16[512,256]{1,0:T(8,128)(2,1)S(1)}) custom-call(f32[16,8,128]{2,1,0:T(8,128)} %constant.43.clone.refs_0_, f32[16,8,128]{2,1,0:T(8,128)} %constant.44.clone.refs_1_, bf16[512,256]{1,0:T(8,128)(2,1)} %constant.45.clone.refs_2_, ...), custom_call_target="tpu_custom_call" | custom-call | tf_op jit(solution)/shard_map/stage/pallas_call | solution.py:117
  9.6 0.0 collective-permute-done.from_south
  9.6 0.0 collective-permute-done.1.from_north
  9.6 1.7 %collective-permute-done.2.zlow_hbm = f32[64,1024]{1,0:T(8,128)S(1)} collective-permute-done((f32[64,1024]{1,0:T(8,128)S(1)}, f32[64,1024]{1,0:T(8,128)S(1)}, u32[]{:S(2)}, u32[]{:S(2)}) %collective-permute-start.2) | collective-permute-done | bytes 262176 | tf_op jit(solution)/shard_map/ppermute | solution.py:670
  11.4 0.0 collective-permute-done.3.zhigh_hbm
  11.4 23.1 %all_to_all.20.edge_cols.recv = f32[16,40,128]{2,1,0:T(8,128)S(1)} all-to-all(f32[16,40,128]{2,1,0:T(8,128)S(1)} %tails.1), channel_id=1, replica_groups=mesh['grp'=4,'gx_0'=2,'gx_1'=8,'gy'=4] {'gx_0','gx_1'}, dimensions={0} | all-to-all | bytes 655360 | tf_op jit(solution)/shard_map/all_to_all | solution.py:687
  34.4 1.6 %inverse.1 = f32[4,16,8,128]{3,2,1,0:T(8,128)} custom-call(f32[16,40,128]{2,1,0:T(8,128)S(1)} %all_to_all.20.edge_cols.recv, f32[16,8,128]{2,1,0:T(8,128)S(1)} %get-tuple-element.46.twc, f32[16,8,128]{2,1,0:T(8,128)S(1)} %get-tuple-element.47.tws, bf16[512,256]{1,0:T(8,128)(2,1)S(1)} %get-tuple-element.48.inv_high, ...), custom_call_target="tpu_custom_call" | custom-call | tf_op jit(solution)/shard_map/inverse/pallas_call | solution.py:117
  36.1 7.3 %all-to-all-start.1 = ((f32[64,8,128]{2,1,0:T(8,128)}), f32[64,8,128]{2,1,0:T(8,128)S(1)}, u32[]{:S(2)}, u32[]{:S(2)}) async-start(f32[64,8,128]{2,1,0:T(8,128)} %bitcast.11), calls=%async_computation.1 | async-start | bytes 524288 | tf_op jit(solution)/shard_map/all_to_all | solution.py:689
  43.4 6.7 %still.1 = (f32[8,64,1024]{2,1,0:T(8,128)S(1)}, f32[3,8,64,1024]{3,2,1,0:T(8,128)}, bf16[256,512]{1,0:T(8,128)(2,1)}, bf16[256,512]{1,0:T(8,128)(2,1)}, bf16[64,...) custom-call(s32[1]{0:T(128)} %bitcast.1.me, ...), custom_call_target="tpu_custom_call" | custom-call | tf_op jit(solution)/shard_map/still/pallas_call | solution.py:117
  50.1 6.7 %all-to-all-done.1 = f32[64,8,128]{2,1,0:T(8,128)S(1)} async-done(((f32[64,8,128]{2,1,0:T(8,128)}), f32[64,8,128]{2,1,0:T(8,128)S(1)}, u32[]{:S(2)}, u32[]{:S(2)}) %all-to-all-start.1) | async-done | bytes 262176 | tf_op jit(solution)/shard_map/all_to_all | solution.py:689
  56.8 4.0 %fine.1 = (f32[8,64,1024]{2,1,0:T(8,128)S(1)}, f32[16,32,256]{2,1,0:T(8,128)S(1)}) custom-call(s32[1]{0:T(128)} %bitcast.grp_ref, f32[8,64,1024]{2,1,0:T(8,128)S(1)} %get-tuple-element.44.base, f32[3,8,64,1024]{3,2,1,0:T(8,128)} %get-tuple-element.45.parts_hbm, f32[512,128]{1,0:T(8,128)S(1)} %bitcast.10, ...), custom_call_target="tpu_custom_call", output_to_operand_aliasing={{0}: (1, {})} | custom-call | tf_op jit(solution)/shard_map/fine/pallas_call | solution.py:117
  60.8 18.1 %all_to_all.21.recv = f32[16,32,256]{2,1,0:T(8,128)S(1)} all-to-all(f32[16,32,256]{2,1,0:T(8,128)S(1)} %get-tuple-element.57), channel_id=1, replica_groups=mesh['grp'=4,'gx_0'=2,'gx_1'=8,'gy'=4] {'gx_0','gx_1'}, dimensions={0} | all-to-all | bytes 1048576 | tf_op jit(solution)/shard_map/all_to_all | solution.py:693
  78.9 1.3 %forward.1 = f32[4,64,256]{2,1,0:T(8,128)} custom-call(f32[16,32,256]{2,1,0:T(8,128)S(1)} %all_to_all.21.recv, bf16[256,512]{1,0:T(8,128)(2,1)S(1)} %copy-done.1, bf16[256,512]{1,0:T(8,128)(2,1)S(1)} %copy-done.2), custom_call_target="tpu_custom_call" | custom-call | tf_op jit(solution)/shard_map/forward/pallas_call | solution.py:117
  80.2 3.9 %all-to-all-start.3 = ((f32[4,64,256]{2,1,0:T(8,128)}), f32[4,64,256]{2,1,0:T(8,128)S(1)}, u32[]{:S(2)}, u32[]{:S(2)}) async-start(f32[4,64,256]{2,1,0:T(8,128)} %forward.1), calls=%async_computation.3 | async-start | bytes 524288 | tf_op jit(solution)/shard_map/all_to_all | solution.py:694
  85.3 0.0 copy-start
  85.3 1.3 %copy.23 = f32[8,64,1024]{2,1,0:T(8,128)} copy(f32[8,64,1024]{2,1,0:T(8,128)S(1)} %get-tuple-element.60) | data formatting | bytes 4194304
  86.7 4.0 %all-to-all-done.3.recv = f32[4,64,256]{2,1,0:T(8,128)S(1)} async-done(((f32[4,64,256]{2,1,0:T(8,128)}), f32[4,64,256]{2,1,0:T(8,128)S(1)}, u32[]{:S(2)}, u32[]{:S(2)}) %all-to-all-start.3) | async-done | bytes 262176 | tf_op jit(solution)/shard_map/all_to_all | solution.py:694
  90.7 0.7 finish.1
  (10 shorter events, 0.0 us)
Async XLA Ops:
  2.0 9.3 %collective-permute-start.2 = (f32[64,1024]{1,0:T(8,128)S(1)}, f32[64,1024]{1,0:T(8,128)S(1)}, u32[]{:S(2)}, u32[]{:S(2)}) collective-permute-start(f32[64,1024]{1,0:T(8,128)S(1)} %get-tuple-element.33), channel_id=1, source_target_pairs={{0,64},{64,128},{128,192},{192,0},{1,65},{65,129},{129,193},{193,1... | collective-permute-start | bytes 786440 | tf_op jit(solution)/shard_map/ppermute | solution.py:670
  3.6 7.8 %collective-permute-start.3 = (f32[64,1024]{1,0:T(8,128)S(1)}, f32[64,1024]{1,0:T(8,128)S(1)}, u32[]{:S(2)}, u32[]{:S(2)}) collective-permute-start(f32[64,1024]{1,0:T(8,128)S(1)} %get-tuple-element.34), channel_id=1, source_target_pairs={{0,192},{64,0},{128,64},{192,128},{1,193},{65,1},{129,65},{193,129... | collective-permute-start | bytes 786440 | tf_op jit(solution)/shard_map/ppermute | solution.py:670
  5.3 4.3 %collective-permute-start = (f32[48,256]{1,0:T(8,128)S(1)}, f32[48,256]{1,0:T(8,128)S(1)}, u32[]{:S(2)}, u32[]{:S(2)}) collective-permute-start(f32[48,256]{1,0:T(8,128)S(1)} %get-tuple-element.31), channel_id=1, source_target_pairs={{0,1},{1,2},{2,3},{3,0},{4,5},{5,6},{6,7},{7,4},{8,9},{9,10},{10,1... | collective-permute-start | bytes 147464 | tf_op jit(solution)/shard_map/ppermute | solution.py:670
  5.3 4.3 %collective-permute-start.1 = (f32[48,256]{1,0:T(8,128)S(1)}, f32[48,256]{1,0:T(8,128)S(1)}, u32[]{:S(2)}, u32[]{:S(2)}) collective-permute-start(f32[48,256]{1,0:T(8,128)S(1)} %get-tuple-element.32), channel_id=1, source_target_pairs={{0,3},{1,0},{2,1},{3,2},{4,7},{5,4},{6,5},{7,6},{8,11},{9,8},{10,9... | collective-permute-start | bytes 147464 | tf_op jit(solution)/shard_map/ppermute | solution.py:670
  11.3 32.0 %copy-start.3 = (f32[64,1024]{1,0:T(8,128)}, f32[64,1024]{1,0:T(8,128)S(1)}, u32[]{:S(2)}) copy-start(f32[64,1024]{1,0:T(8,128)S(1)} %collective-permute-done.2.zlow_hbm) | copy-start | bytes 786436
  11.4 32.0 %copy-start.4 = (f32[64,1024]{1,0:T(8,128)}, f32[64,1024]{1,0:T(8,128)S(1)}, u32[]{:S(2)}) copy-start(f32[64,1024]{1,0:T(8,128)S(1)} %collective-permute-done.3.zhigh_hbm) | copy-start | bytes 786436
  36.1 20.7 %all-to-all-start.1 = ((f32[64,8,128]{2,1,0:T(8,128)}), f32[64,8,128]{2,1,0:T(8,128)S(1)}, u32[]{:S(2)}, u32[]{:S(2)}) async-start(f32[64,8,128]{2,1,0:T(8,128)} %bitcast.11), calls=%async_computation.1 | async-start | bytes 524288 | tf_op jit(solution)/shard_map/all_to_all | solution.py:689
  56.8 22.0 %copy-start.1 = (bf16[256,512]{1,0:T(8,128)(2,1)S(1)}, bf16[256,512]{1,0:T(8,128)(2,1)}, u32[]{:S(2)}) copy-start(bf16[256,512]{1,0:T(8,128)(2,1)} %get-tuple-element.58.table_high) | copy-start | bytes 786436
  56.8 22.0 %copy-start.2 = (bf16[256,512]{1,0:T(8,128)(2,1)S(1)}, bf16[256,512]{1,0:T(8,128)(2,1)}, u32[]{:S(2)}) copy-start(bf16[256,512]{1,0:T(8,128)(2,1)} %get-tuple-element.59.table_low) | copy-start | bytes 786436
  80.2 10.5 %all-to-all-start.3 = ((f32[4,64,256]{2,1,0:T(8,128)}), f32[4,64,256]{2,1,0:T(8,128)S(1)}, u32[]{:S(2)}, u32[]{:S(2)}) async-start(f32[4,64,256]{2,1,0:T(8,128)} %forward.1), calls=%async_computation.3 | async-start | bytes 524288 | tf_op jit(solution)/shard_map/all_to_all | solution.py:694
  85.3 5.4 %copy-start = (f32[1,2,8,16,256]{4,3,2,1,0:T(8,128)S(1)}, f32[1,2,8,16,256]{4,3,2,1,0:T(8,128)}, u32[]{:S(2)}) copy-start(f32[1,2,8,16,256]{4,3,2,1,0:T(8,128)} %param.17) | copy-start | bytes 786436

commit v11 on v9

--- a/solution.py
+++ b/solution.py
@@ -292,26 +292,29 @@
     row_id = iota((8, 128), 0)
     lane_id = iota((8, 128), 1)
 
-    def put(r, top, part, value):
-        high, low = halves(value)
-        left_high[16 * r + 8 * top : 16 * r + 8 * top + 8, 128 * part : 128 * part + 128] = high
-        left_low[16 * r + 8 * top : 16 * r + 8 * top + 8, 128 * part : 128 * part + 128] = low
+    def put(row, part, upper, lower):
+        high, low = halves(jnp.concatenate([upper, lower], 0))
+        left_high[row : row + 16, 128 * part : 128 * part + 128] = high
+        left_low[row : row + 16, 128 * part : 128 * part + 128] = low
 
     for h in range(2):
         z = [(recv[g, 16 * h : 16 * h + 8, :], recv[g, 16 * h + 8 : 16 * h + 16, :]) for g in range(G)]
-        for r, (a, b) in enumerate(sixteen(z)):
-            a, b = cmul(a, b, twc[r, h : h + 1, :], tws[r, h : h + 1, :])
-            put(r, 0, h, a)
-            put(r, 0, 2 + h, b)
+        turned = [cmul(a, b, twc[r, h : h + 1, :], tws[r, h : h + 1, :]) for r, (a, b) in enumerate(sixteen(z))]
+        for r in range(0, G, 2):
+            for i in range(2):
+                put(8 * r, 2 * i + h, turned[r][i], turned[r + 1][i])
     z = []
     for g in range(G):
         tile = jnp.where(row_id < 4, recv[g, 32:40, :], 0.0)
         z.append((tile, roll(tile, -2, 0)))
-    for r, (a, b) in enumerate(sixteen(z)):
-        a, b = cmul(a, b, twc[r], tws[r])
-        for part, value in ((0, a), (2, b)):
-            put(r, 1, part, jnp.where(row_id == 0, value, 0.0))
-            put(r, 1, part + 1, jnp.where(row_id == 0, roll(value, -1, 0), 0.0))
+    rows = [[jnp.zeros((8, 128), F32)] * 2 for _ in range(4)]
+    for r, pair in enumerate(sixteen(z)):
+        pair = cmul(*pair, twc[r], tws[r])
+        for part in range(4):
+            value = roll(pair[part // 2], r % 8 - part % 2, 0)
+            rows[part][r // 8] = jnp.where(row_id == r % 8, value, rows[part][r // 8])
+    for part in range(4):
+        put(128, part, *rows[part])
 
     mid[...] = (
         mm(left_high[...], inv_high[...]) + mm(left_low[...], inv_high[...]) + mm(left_high[...], inv_low[...])
@@ -319,11 +322,11 @@
 
     first, second, single = [], [], []
     for r in range(G):
-        first.append(mid[16 * r : 16 * r + 8, 0:128])
-        second.append(mid[16 * r : 16 * r + 8, 128:256])
-        low = mid[16 * r + 8 : 16 * r + 16, 0:128]
-        high = mid[16 * r + 8 : 16 * r + 16, 128:256]
-        single.append(jnp.where(row_id == 0, low, roll(high, 1, 0)))
+        first.append(mid[8 * r : 8 * r + 8, 0:128])
+        second.append(mid[8 * r : 8 * r + 8, 128:256])
+        at = slice(128 + r // 8 * 8, 136 + r // 8 * 8)
+        low, high = roll(mid[at, 0:128], -(r % 8), 0), roll(mid[at, 128:256], 1 - r % 8, 0)
+        single.append(jnp.where(row_id == 0, low, high))
     for i in range(8):
         a, b = first[i], second[i]
         c, d = first[i + 8], second[i + 8]
@@ -372,9 +375,9 @@
         [VM] * 5,
         HB,
         scratch_shapes=[
-            pltpu.VMEM((256, 512), BF16),
-            pltpu.VMEM((256, 512), BF16),
-            pltpu.VMEM((256, 256), F32),
+            pltpu.VMEM((144, 512), BF16),
+            pltpu.VMEM((144, 512), BF16),
+            pltpu.VMEM((144, 256), F32),
             pltpu.VMEM((4, G, 8, 128), F32),
             pltpu.SemaphoreType.DMA((4,)),
         ],

time: 91.7 us -> 91.6 us (level)
  no operation moved by 1% of the time
where the time goes in v11:
time: 91.6 us; the launch traced here: 91.2 us
  blocking collectives  41.1 us (45%)
  Pallas kernels  18.6 us (20%)
  starting transfers between devices  16 us (17%)
  waiting for transfers between devices  12.1 us (13%)
  between operations  2.04 us (2%)
  local copies, waits for them, and re-layouts  1.34 us (1%)
    all_to_all x1, blocking collectives, per_device(): recv1 = lax.all_to_all(chunk, GX, 0, 0, tiled=True)  23.1 us
    pallas_call x9, Pallas kernels, placed(): inner(*[x if spec is not HB else pltpu.with_memory_space_constraint(x, pl...  18.6 us
    all_to_all x1, blocking collectives, per_device(): recv3 = lax.all_to_all(spread, GX, 0, 0, tiled=True)  18.1 us
    all_to_all x1, starting transfers between devices, per_device(): recv2 = lax.all_to_all(send2, GRP_GX, 0, 0, tiled=True)  7.25 us
    all_to_all x1, waiting for transfers between devices, per_device(): recv2 = lax.all_to_all(send2, GRP_GX, 0, 0, tiled=True)  6.94 us
    ppermute x4, starting transfers between devices, shifted(): lax.ppermute(array, axis, [(i, (i + step) % count) for i in range(count)])  5.06 us
    all_to_all x1, waiting for transfers between devices, per_device(): recv4 = lax.all_to_all(forward(recv3, *weights), 'grp', 0, 0, tiled=True)  4.05 us
    all_to_all x1, starting transfers between devices, per_device(): recv4 = lax.all_to_all(forward(recv3, *weights), 'grp', 0, 0, tiled=True)  3.64 us
  transfers between devices with their start and end apart: 6, of which 3 were waited for; matrix products, arithmetic and copies ran while one was open for 1% of the time, Pallas kernels for 11%

profile of v11, /device:TPU:32, one launch (start us, length us, event | category | flops | bytes accessed | tf_op | source)
XLA Modules:
  0.0 91.2 jit_solution(2015647894571096828)
XLA Ops:
  0.6 1.4 %outer_lines.1 = (f32[48,256]{1,0:T(8,128)S(1)}, f32[48,256]{1,0:T(8,128)S(1)}, f32[64,1024]{1,0:T(8,128)S(1)}, f32[64,1024]{1,0:T(8,128)S(1)}) custom-call(f32[16,16,256]{2,1,0:T(8,128)} %bitcast.7, f32[8,64,1024]{2,1,0:T(8,128)} %sal_hbm.1), custom_call_target="tpu_custom_call" | custom-call | tf_op jit(solution)/shard_map/outer_lines/pallas_call | solution.py:117
  2.0 1.6 %collective-permute-start.2 = (f32[64,1024]{1,0:T(8,128)S(1)}, f32[64,1024]{1,0:T(8,128)S(1)}, u32[]{:S(2)}, u32[]{:S(2)}) collective-permute-start(f32[64,1024]{1,0:T(8,128)S(1)} %get-tuple-element.35), channel_id=1, source_target_pairs={{0,64},{64,128},{128,192},{192,0},{1,65},{65,129},{129,193},{193,1... | collective-permute-start | bytes 786440 | tf_op jit(solution)/shard_map/ppermute | solution.py:660
  3.6 1.7 %collective-permute-start.3 = (f32[64,1024]{1,0:T(8,128)S(1)}, f32[64,1024]{1,0:T(8,128)S(1)}, u32[]{:S(2)}, u32[]{:S(2)}) collective-permute-start(f32[64,1024]{1,0:T(8,128)S(1)} %get-tuple-element.36), channel_id=1, source_target_pairs={{0,192},{64,0},{128,64},{192,128},{1,193},{65,1},{129,65},{193,129... | collective-permute-start | bytes 786440 | tf_op jit(solution)/shard_map/ppermute | solution.py:660
  5.4 0.0 collective-permute-start
  5.4 1.7 %collective-permute-start.1 = (f32[48,256]{1,0:T(8,128)S(1)}, f32[48,256]{1,0:T(8,128)S(1)}, u32[]{:S(2)}, u32[]{:S(2)}) collective-permute-start(f32[48,256]{1,0:T(8,128)S(1)} %get-tuple-element.34), channel_id=1, source_target_pairs={{0,3},{1,0},{2,1},{3,2},{4,7},{5,4},{6,5},{7,6},{8,11},{9,8},{10,9... | collective-permute-start | bytes 147464 | tf_op jit(solution)/shard_map/ppermute | solution.py:660
  7.1 1.4 %pack.1.chunk = f32[16,40,128]{2,1,0:T(8,128)S(1)} custom-call(s32[1]{0:T(128)} %bitcast.1.me, f32[256,256]{1,0:T(8,128)} %bitcast.8, f32[8,64,1024]{2,1,0:T(8,128)} %sal_hbm.1), custom_call_target="tpu_custom_call" | custom-call | tf_op jit(solution)/shard_map/pack/pallas_call | solution.py:117
  8.5 1.7 %stage.1 = (f32[16,8,128]{2,1,0:T(8,128)S(1)}, f32[16,8,128]{2,1,0:T(8,128)S(1)}, bf16[512,256]{1,0:T(8,128)(2,1)S(1)}, bf16[512,256]{1,0:T(8,128)(2,1)S(1)}, bf...) custom-call(s32[1]{0:T(128)} %bitcast.1.me, f32[16,512]{1,0:T(8,128)} %constant.47.clone.inner_hbm, ...), custom_call_target="tpu_custom_call" | custom-call | tf_op jit(solution)/shard_map/stage/pallas_call | solution.py:117
  10.2 0.0 collective-permute-done.from_south
  10.2 0.0 collective-permute-done.1.from_north
  10.2 1.1 %collective-permute-done.2.zlow_hbm = f32[64,1024]{1,0:T(8,128)S(1)} collective-permute-done((f32[64,1024]{1,0:T(8,128)S(1)}, f32[64,1024]{1,0:T(8,128)S(1)}, u32[]{:S(2)}, u32[]{:S(2)}) %collective-permute-start.2) | collective-permute-done | bytes 262176 | tf_op jit(solution)/shard_map/ppermute | solution.py:660
  11.4 0.0 collective-permute-done.3.zhigh_hbm
  11.4 23.1 %all_to_all.20.edge_cols.recv = f32[16,40,128]{2,1,0:T(8,128)S(1)} all-to-all(f32[16,40,128]{2,1,0:T(8,128)S(1)} %tails.1), channel_id=1, replica_groups=mesh['grp'=4,'gx_0'=2,'gx_1'=8,'gy'=4] {'gx_0','gx_1'}, dimensions={0} | all-to-all | bytes 655360 | tf_op jit(solution)/shard_map/all_to_all | solution.py:677
  34.5 1.6 %inverse.1 = f32[4,16,8,128]{3,2,1,0:T(8,128)} custom-call(f32[16,40,128]{2,1,0:T(8,128)S(1)} %all_to_all.20.edge_cols.recv, f32[16,8,128]{2,1,0:T(8,128)S(1)} %get-tuple-element.50.twc, f32[16,8,128]{2,1,0:T(8,128)S(1)} %get-tuple-element.51.tws, bf16[512,256]{1,0:T(8,128)(2,1)S(1)} %get-tuple-element.52.inv_high, ...), custom_call_target="tpu_custom_call" | custom-call | tf_op jit(solution)/shard_map/inverse/pallas_call | solution.py:117
  36.0 7.2 %all-to-all-start.1 = ((f32[64,8,128]{2,1,0:T(8,128)}), f32[64,8,128]{2,1,0:T(8,128)S(1)}, u32[]{:S(2)}, u32[]{:S(2)}) async-start(f32[64,8,128]{2,1,0:T(8,128)} %bitcast.11), calls=%async_computation.1 | async-start | bytes 524288 | tf_op jit(solution)/shard_map/all_to_all | solution.py:679
  43.3 6.5 %still.1 = (f32[8,64,1024]{2,1,0:T(8,128)S(1)}, f32[3,8,64,1024]{3,2,1,0:T(8,128)}, bf16[64,64]{1,0:T(8,128)(2,1)S(1)}, bf16[16,64]{1,0:T(8,128)(2,1)S(1)}, bf16...) custom-call(s32[1]{0:T(128)} %bitcast.1.me, ...), custom_call_target="tpu_custom_call" | custom-call | tf_op jit(solution)/shard_map/still/pallas_call | solution.py:117
  49.8 6.9 %all-to-all-done.1 = f32[64,8,128]{2,1,0:T(8,128)S(1)} async-done(((f32[64,8,128]{2,1,0:T(8,128)}), f32[64,8,128]{2,1,0:T(8,128)S(1)}, u32[]{:S(2)}, u32[]{:S(2)}) %all-to-all-start.1) | async-done | bytes 262176 | tf_op jit(solution)/shard_map/all_to_all | solution.py:679
  56.8 3.9 %fine.1 = (f32[8,64,1024]{2,1,0:T(8,128)S(1)}, f32[16,32,256]{2,1,0:T(8,128)S(1)}) custom-call(s32[1]{0:T(128)} %bitcast.grp_ref, f32[8,64,1024]{2,1,0:T(8,128)S(1)} %get-tuple-element.48.base, f32[3,8,64,1024]{3,2,1,0:T(8,128)} %get-tuple-element.49.parts_hbm, f32[512,128]{1,0:T(8,128)S(1)} %bitcast.10, ...), custom_call_target="tpu_custom_call", output_to_operand_aliasing={{0}: (1, {})} | custom-call | tf_op jit(solution)/shard_map/fine/pallas_call | solution.py:117
  60.7 18.1 %all_to_all.21.recv = f32[16,32,256]{2,1,0:T(8,128)S(1)} all-to-all(f32[16,32,256]{2,1,0:T(8,128)S(1)} %get-tuple-element.61), channel_id=1, replica_groups=mesh['grp'=4,'gx_0'=2,'gx_1'=8,'gy'=4] {'gx_0','gx_1'}, dimensions={0} | all-to-all | bytes 1048576 | tf_op jit(solution)/shard_map/all_to_all | solution.py:682
  78.8 1.3 %forward.1 = f32[4,64,256]{2,1,0:T(8,128)} custom-call(f32[16,32,256]{2,1,0:T(8,128)S(1)} %all_to_all.21.recv, bf16[256,512]{1,0:T(8,128)(2,1)S(1)} %copy-done.1, bf16[256,512]{1,0:T(8,128)(2,1)S(1)} %copy-done.2), custom_call_target="tpu_custom_call" | custom-call | tf_op jit(solution)/shard_map/forward/pallas_call | solution.py:117
  80.1 3.6 %all-to-all-start.3 = ((f32[4,64,256]{2,1,0:T(8,128)}), f32[4,64,256]{2,1,0:T(8,128)S(1)}, u32[]{:S(2)}, u32[]{:S(2)}) async-start(f32[4,64,256]{2,1,0:T(8,128)} %forward.1), calls=%async_computation.3 | async-start | bytes 524288 | tf_op jit(solution)/shard_map/all_to_all | solution.py:683
  85.1 0.0 copy-start
  85.1 1.3 %copy.23 = f32[8,64,1024]{2,1,0:T(8,128)} copy(f32[8,64,1024]{2,1,0:T(8,128)S(1)} %get-tuple-element.64) | data formatting | bytes 4194304
  86.4 4.0 %all-to-all-done.3.recv = f32[4,64,256]{2,1,0:T(8,128)S(1)} async-done(((f32[4,64,256]{2,1,0:T(8,128)}), f32[4,64,256]{2,1,0:T(8,128)S(1)}, u32[]{:S(2)}, u32[]{:S(2)}) %all-to-all-start.3) | async-done | bytes 262176 | tf_op jit(solution)/shard_map/all_to_all | solution.py:683
  90.4 0.7 finish.1
  (10 shorter events, 0.0 us)
Async XLA Ops:
  2.0 9.3 %collective-permute-start.2 = (f32[64,1024]{1,0:T(8,128)S(1)}, f32[64,1024]{1,0:T(8,128)S(1)}, u32[]{:S(2)}, u32[]{:S(2)}) collective-permute-start(f32[64,1024]{1,0:T(8,128)S(1)} %get-tuple-element.35), channel_id=1, source_target_pairs={{0,64},{64,128},{128,192},{192,0},{1,65},{65,129},{129,193},{193,1... | collective-permute-start | bytes 786440 | tf_op jit(solution)/shard_map/ppermute | solution.py:660
  3.6 7.8 %collective-permute-start.3 = (f32[64,1024]{1,0:T(8,128)S(1)}, f32[64,1024]{1,0:T(8,128)S(1)}, u32[]{:S(2)}, u32[]{:S(2)}) collective-permute-start(f32[64,1024]{1,0:T(8,128)S(1)} %get-tuple-element.36), channel_id=1, source_target_pairs={{0,192},{64,0},{128,64},{192,128},{1,193},{65,1},{129,65},{193,129... | collective-permute-start | bytes 786440 | tf_op jit(solution)/shard_map/ppermute | solution.py:660
  5.4 4.9 %collective-permute-start = (f32[48,256]{1,0:T(8,128)S(1)}, f32[48,256]{1,0:T(8,128)S(1)}, u32[]{:S(2)}, u32[]{:S(2)}) collective-permute-start(f32[48,256]{1,0:T(8,128)S(1)} %get-tuple-element.33), channel_id=1, source_target_pairs={{0,1},{1,2},{2,3},{3,0},{4,5},{5,6},{6,7},{7,4},{8,9},{9,10},{10,1... | collective-permute-start | bytes 147464 | tf_op jit(solution)/shard_map/ppermute | solution.py:660
  5.4 4.9 %collective-permute-start.1 = (f32[48,256]{1,0:T(8,128)S(1)}, f32[48,256]{1,0:T(8,128)S(1)}, u32[]{:S(2)}, u32[]{:S(2)}) collective-permute-start(f32[48,256]{1,0:T(8,128)S(1)} %get-tuple-element.34), channel_id=1, source_target_pairs={{0,3},{1,0},{2,1},{3,2},{4,7},{5,4},{6,5},{7,6},{8,11},{9,8},{10,9... | collective-permute-start | bytes 147464 | tf_op jit(solution)/shard_map/ppermute | solution.py:660
  11.4 31.9 %copy-start.3 = (f32[64,1024]{1,0:T(8,128)}, f32[64,1024]{1,0:T(8,128)S(1)}, u32[]{:S(2)}) copy-start(f32[64,1024]{1,0:T(8,128)S(1)} %collective-permute-done.2.zlow_hbm) | copy-start | bytes 786436
  11.4 31.9 %copy-start.4 = (f32[64,1024]{1,0:T(8,128)}, f32[64,1024]{1,0:T(8,128)S(1)}, u32[]{:S(2)}) copy-start(f32[64,1024]{1,0:T(8,128)S(1)} %collective-permute-done.3.zhigh_hbm) | copy-start | bytes 786436
  36.0 20.7 %all-to-all-start.1 = ((f32[64,8,128]{2,1,0:T(8,128)}), f32[64,8,128]{2,1,0:T(8,128)S(1)}, u32[]{:S(2)}, u32[]{:S(2)}) async-start(f32[64,8,128]{2,1,0:T(8,128)} %bitcast.11), calls=%async_computation.1 | async-start | bytes 524288 | tf_op jit(solution)/shard_map/all_to_all | solution.py:679
  56.8 22.0 %copy-start.1 = (bf16[256,512]{1,0:T(8,128)(2,1)S(1)}, bf16[256,512]{1,0:T(8,128)(2,1)}, u32[]{:S(2)}) copy-start(bf16[256,512]{1,0:T(8,128)(2,1)} %get-tuple-element.62.table_high) | copy-start | bytes 786436
  56.8 22.0 %copy-start.2 = (bf16[256,512]{1,0:T(8,128)(2,1)S(1)}, bf16[256,512]{1,0:T(8,128)(2,1)}, u32[]{:S(2)}) copy-start(bf16[256,512]{1,0:T(8,128)(2,1)} %get-tuple-element.63.table_low) | copy-start | bytes 786436
  80.1 10.3 %all-to-all-start.3 = ((f32[4,64,256]{2,1,0:T(8,128)}), f32[4,64,256]{2,1,0:T(8,128)S(1)}, u32[]{:S(2)}, u32[]{:S(2)}) async-start(f32[4,64,256]{2,1,0:T(8,128)} %forward.1), calls=%async_computation.3 | async-start | bytes 524288 | tf_op jit(solution)/shard_map/all_to_all | solution.py:683
  85.1 5.4 %copy-start = (f32[1,2,8,16,256]{4,3,2,1,0:T(8,128)S(1)}, f32[1,2,8,16,256]{4,3,2,1,0:T(8,128)}, u32[]{:S(2)}) copy-start(f32[1,2,8,16,256]{4,3,2,1,0:T(8,128)} %param.17) | copy-start | bytes 786436
